TPU v7x, 512 devices: a whole 4x4x16 slice. The times are simulated.
512 devices in a mesh: lat: 16 (over y, x_lo, core), lon: 32 (over z, x_hi).
Axes of the slice: x: 4 (x_hi: 2, x_lo: 2; x = x_hi * 2 + x_lo), y: 4, z: 16, core: 2. Of those that a mesh axis runs over, the one named last changes fastest.
Arguments:
- queries: bfloat16 [384, 768, 128], P('lat', 'lon'), may hold values from -8 to 8
- keys: bfloat16 [384, 768, 128], P('lat', 'lon'), may hold values from -8 to 8
- values: bfloat16 [384, 768, 128], P('lat', 'lon'), may hold values from -6 to 6
- out_grad: bfloat16 [384, 768, 128], P('lat', 'lon'), may hold values from -6 to 6
Outputs:
- attended: bfloat16 [384, 768, 128], P('lat', 'lon')
- grad_queries: bfloat16 [384, 768, 128], P('lat', 'lon')
- grad_keys: bfloat16 [384, 768, 128], P('lat', 'lon')
- grad_values: bfloat16 [384, 768, 128], P('lat', 'lon')
All inputs are finite; a program needn't handle non-finite values.
Results may differ from a plain program's by a relative error of at most 0.018.
Values may be sent and summed in bfloat16 or wider, within the bound.
No kernel may reach another device: no remote copies, remote signals or barrier semaphores. Data moves between devices by JAX's collectives and lax.ppermute only.
A program may use at most 128 MiB of HBM per device.

v0:
```python
import math

import jax
import jax.numpy as jnp
from jax import lax
from jax.sharding import PartitionSpec as P

HEADS = 2
HEAD_DIM = 64
RADIUS = 22
BLOCK_LAT = 8
BLOCK_LON = 24
WINDOW = 45


masked_value = -1e30


def from_behind(block, axis, distance):
    devices = range(lax.axis_size(axis))
    route = [(i - distance, i) for i in devices if i - distance in devices]
    return lax.ppermute(block, axis, route)


def from_behind_2(value, axis, by):
    peers = lax.axis_size(axis)
    return lax.ppermute(value, axis, [(i, (i + by) % peers) for i in range(peers)])


def extended_2(cells, sides, width, closed):
    for axis, dim in sides:
        count = lax.axis_size(axis)
        ends = count if closed else count - 1
        head = lax.slice_in_dim(cells, 0, width, axis=dim)
        tail = lax.slice_in_dim(cells, cells.shape[dim] - width, cells.shape[dim], axis=dim)
        cells = jnp.concatenate(
            [
                lax.ppermute(tail, axis, [(i, (i + 1) % count) for i in range(ends)]),
                cells,
                lax.ppermute(head, axis, [((i + 1) % count, i) for i in range(ends)]),
            ],
            axis=dim,
        )
    return cells


def window_mask(query_rows, key_rows, height):
    first_key = jnp.clip(query_rows - RADIUS, 0, height - WINDOW)
    lat_ok = (key_rows[None, :] >= first_key[:, None]) & (
        key_rows[None, :] < first_key[:, None] + WINDOW
    )
    offsets = (
        jnp.arange(BLOCK_LON + 2 * RADIUS, dtype=jnp.int32)[None, :]
        - jnp.arange(BLOCK_LON, dtype=jnp.int32)[:, None]
    )
    lon_ok = (offsets >= 0) & (offsets <= 2 * RADIUS)
    inside = lat_ok[:, None, :, None] & lon_ok[None, :, None, :]
    return inside.reshape(
        BLOCK_LAT * BLOCK_LON, (BLOCK_LAT + 2 * RADIUS) * (BLOCK_LON + 2 * RADIUS)
    )


def attend(query_block, grad_block, key_slab, inside):
    query_count = query_block.shape[0]
    key_count = key_slab.shape[0]
    channels = query_block.shape[1]
    scale = 1.0 / math.sqrt(HEAD_DIM)
    query_heads = query_block.reshape(query_count, HEADS, HEAD_DIM)
    grad_heads = grad_block.reshape(query_count, HEADS, HEAD_DIM)
    key_heads = key_slab[:, :channels].reshape(key_count, HEADS, HEAD_DIM)
    value_heads = key_slab[:, channels:].reshape(key_count, HEADS, HEAD_DIM)
    scores = (
        jnp.einsum("qhd,khd->hqk", query_heads, key_heads, preferred_element_type=jnp.float32)
        * scale
    )
    scores = jnp.where(inside[None], scores, masked_value)
    row_max = jnp.max(scores, axis=-1)
    log_total = row_max + jnp.log(jnp.sum(jnp.exp(scores - row_max[..., None]), axis=-1))
    weights = jnp.exp(scores - log_total[..., None]).astype(jnp.bfloat16)
    attended = jnp.einsum(
        "hqk,khd->qhd", weights, value_heads, preferred_element_type=jnp.float32
    ).astype(jnp.bfloat16)
    correction = jnp.sum(grad_heads.astype(jnp.float32) * attended.astype(jnp.float32), axis=-1).T
    grad_weights = jnp.einsum(
        "qhd,khd->hqk", grad_heads, value_heads, preferred_element_type=jnp.float32
    )
    grad_scores = (
        weights.astype(jnp.float32) * (grad_weights - correction[..., None]) * scale
    ).astype(jnp.bfloat16)
    grad_query = jnp.einsum(
        "hqk,khd->qhd", grad_scores, key_heads, preferred_element_type=jnp.float32
    ).astype(jnp.bfloat16)
    grad_key = jnp.einsum(
        "hqk,qhd->khd", grad_scores, query_heads, preferred_element_type=jnp.float32
    ).reshape(key_count, channels)
    grad_value = jnp.einsum(
        "hqk,qhd->khd", weights, grad_heads, preferred_element_type=jnp.float32
    ).reshape(key_count, channels)
    grad_pair = jnp.concatenate([grad_key, grad_value], axis=-1)
    return (
        attended.reshape(query_count, channels),
        grad_query.reshape(query_count, channels),
        grad_pair,
    )


def fold_rows(gradient, tile_rows):
    from_south = from_behind(gradient[:RADIUS], "lat", -1)
    from_north = from_behind(gradient[tile_rows + RADIUS :], "lat", 1)
    interior = gradient[RADIUS : tile_rows + RADIUS]
    interior = interior.at[tile_rows - RADIUS :].add(from_south)
    return interior.at[:RADIUS].add(from_north)


def fold_cols(gradient, tile_cols):
    from_east = from_behind_2(gradient[:, :RADIUS], "lon", -1)
    from_west = from_behind_2(gradient[:, tile_cols + RADIUS :], "lon", 1)
    interior = gradient[:, RADIUS : tile_cols + RADIUS]
    interior = interior.at[:, tile_cols - RADIUS :].add(from_east)
    return interior.at[:, :RADIUS].add(from_west)


def body(queries, keys, values, out_grad):
    tile_rows, tile_cols, channels = queries.shape
    key_value = jnp.concatenate([keys, values], axis=-1)
    taller = extended_2(key_value, (("lat", 0),), RADIUS, False)
    extended = extended_2(taller, (("lon", 1),), RADIUS, True)
    height = tile_rows * lax.axis_size("lat")
    first_row = lax.axis_index("lat") * tile_rows
    blocks_lat = tile_rows // BLOCK_LAT
    blocks_lon = tile_cols // BLOCK_LON
    slab_rows = BLOCK_LAT + 2 * RADIUS
    slab_cols = BLOCK_LON + 2 * RADIUS
    zero_index = jnp.zeros((), jnp.int32)

    def step(gradient, block_index):
        row_start = block_index // blocks_lon * BLOCK_LAT
        col_start = block_index % blocks_lon * BLOCK_LON
        first_key = jnp.clip(first_row + row_start - RADIUS, 0, height - WINDOW)
        slab_start = jnp.clip(first_key - first_row + RADIUS, 0, tile_rows - BLOCK_LAT)
        key_slab = lax.dynamic_slice(
            extended, (slab_start, col_start, zero_index), (slab_rows, slab_cols, 2 * channels)
        )
        key_slab = key_slab.reshape(slab_rows * slab_cols, 2 * channels)
        query_block = lax.dynamic_slice(
            queries, (row_start, col_start, zero_index), (BLOCK_LAT, BLOCK_LON, channels)
        ).reshape(-1, channels)
        grad_block = lax.dynamic_slice(
            out_grad, (row_start, col_start, zero_index), (BLOCK_LAT, BLOCK_LON, channels)
        ).reshape(-1, channels)
        query_rows = first_row + row_start + jnp.arange(BLOCK_LAT, dtype=jnp.int32)
        key_rows = first_row - RADIUS + slab_start + jnp.arange(slab_rows, dtype=jnp.int32)
        inside = window_mask(query_rows, key_rows, height)
        attended, grad_query, grad_pair = attend(query_block, grad_block, key_slab, inside)
        current = lax.dynamic_slice(
            gradient, (slab_start, col_start, zero_index), (slab_rows, slab_cols, 2 * channels)
        )
        gradient = lax.dynamic_update_slice(
            gradient,
            current + grad_pair.reshape(slab_rows, slab_cols, 2 * channels),
            (slab_start, col_start, zero_index),
        )
        return (gradient, (attended, grad_query))

    start_grad = jnp.zeros(
        (tile_rows + 2 * RADIUS, tile_cols + 2 * RADIUS, 2 * channels), jnp.float32
    )
    gradient, stacked = lax.scan(
        step, start_grad, jnp.arange(blocks_lat * blocks_lon, dtype=jnp.int32)
    )

    def assemble(pieces):
        depth = pieces.shape[-1]
        shaped = pieces.reshape(blocks_lat, blocks_lon, BLOCK_LAT, BLOCK_LON, depth)
        return shaped.transpose(0, 2, 1, 3, 4).reshape(tile_rows, tile_cols, depth)

    interior = fold_cols(fold_rows(gradient, tile_rows), tile_cols)
    grad_keys = interior[..., :channels].astype(jnp.bfloat16)
    grad_values = interior[..., channels:].astype(jnp.bfloat16)
    return (assemble(stacked[0]), assemble(stacked[1]), grad_keys, grad_values)


def solution(mesh):
    in_specs = (
        P("lat", "lon", None),
        P("lat", "lon", None),
        P("lat", "lon", None),
        P("lat", "lon", None),
    )
    out_specs = (
        P("lat", "lon", None),
        P("lat", "lon", None),
        P("lat", "lon", None),
        P("lat", "lon", None),
    )
    return jax.shard_map(body, mesh=mesh, in_specs=in_specs, out_specs=out_specs, check_vma=False)
```

profile of v0, /device:TPU:18, one launch (start us, length us, event | category | flops | bytes accessed | tf_op | source)
XLA Modules:
  0.0 340.6 jit_solution(7760367816558046622)
XLA Ops:
  14.0 4.3 %collective-permute-start.2 = (bf16[68,22,256]{2,0,1:T(8,128)(2,1)}, bf16[68,22,256]{2,0,1:T(8,128)(2,1)S(1)}, u32[]{:S(2)}, u32[]{:S(2)}) collective-permute-start(bf16[68,22,256]{2,0,1:T(8,128)(2,1)} %get-tuple-element.278), channel_id=1, source_target_pairs={{0,1},{1,2},{2,3},{3,4},{4,5},{5,6},{6,7},{7,8},{8,9},{9,10},{10,1... | collective-permute-start | bytes 2297864 | tf_op jit(solution)/shard_map/ppermute | solution.py:38
  18.3 10.9 %collective-permute-start.3 = (bf16[68,22,256]{2,0,1:T(8,128)(2,1)S(1)}, bf16[68,22,256]{2,0,1:T(8,128)(2,1)S(1)}, u32[]{:S(2)}, u32[]{:S(2)}) collective-permute-start(bf16[68,22,256]{2,0,1:T(8,128)(2,1)S(1)} %get-tuple-element.279), channel_id=1, source_target_pairs={{1,0},{2,1},{3,2},{4,3},{5,4},{6,5},{7,6},{8,7},{9,8},{10,9},{11,1... | collective-permute-start | bytes 2297864 | tf_op jit(solution)/shard_map/ppermute | solution.py:40
  29.2 24.0 %collective-permute-done.2 = bf16[68,22,256]{2,0,1:T(8,128)(2,1)S(1)} collective-permute-done((bf16[68,22,256]{2,0,1:T(8,128)(2,1)}, bf16[68,22,256]{2,0,1:T(8,128)(2,1)S(1)}, u32[]{:S(2)}, u32[]{:S(2)}) %collective-permute-start.2) | collective-permute-done | bytes 765984 | tf_op jit(solution)/shard_map/ppermute | solution.py:38
  53.1 5.9 %collective-permute-done.3 = bf16[68,22,256]{2,0,1:T(8,128)(2,1)S(1)} collective-permute-done((bf16[68,22,256]{2,0,1:T(8,128)(2,1)S(1)}, bf16[68,22,256]{2,0,1:T(8,128)(2,1)S(1)}, u32[]{:S(2)}, u32[]{:S(2)}) %collective-permute-start.3) | collective-permute-done | bytes 765984 | tf_op jit(solution)/shard_map/ppermute | solution.py:40
  64.2 195.1 %while.21 = (s32[]{:T(128)}, f32[68,68,256]{2,1,0:T(8,128)}, bf16[3,192,128]{2,1,0:T(8,128)(2,1)}, bf16[3,192,128]{2,1,0:T(8,128)(2,1)}, s32[3]{0:T(128)S(1)}, /...) while((s32[]{:T(128)}, f32[68,68,256]{2,1,0:T(8,128)}, ...), condition=%wide.region_4.5_spmd, body=%wide.region_0.4_spmd.sunk | while | flops 1061746688 | bytes 126691848 | solution.py:168
  81.9 7.1 %copy.88 = f32[52,68,256]{1,0,2:T(8,128)} copy(f32[52,68,256]{2,1,0:T(8,128)} %constant_dynamic-slice_fusion.8) | data formatting | bytes 7241728 | tf_op jit(solution)/shard_map/while/body/eval_jaxpr/dynamic_slice | solution.py:155
  101.4 4.2 %concatenate.35 = f32[52,68,128]{1,0,2:T(8,128)} reshape(f32[3536,2,64]{0,2,1:T(8,128)} %convolution_bitcast_fusion.5) | data formatting | bytes 3620864 | tf_op jit(solution)/shard_map/while/body/eval_jaxpr/concatenate | solution.py:99
  108.4 8.9 %maximum_add_fusion.2 = f32[52,68,256]{1,0,2:T(8,128)} fusion(f32[52,68,256]{1,0,2:T(8,128)} %copy.88, f32[52,68,128]{1,0,2:T(8,128)} %concatenate.34, f32[52,68,128]{1,0,2:T(8,128)} %concatenate.35), kind=kLoop, calls=%fused_computation.clone.1 | loop fusion | flops 1810432 | bytes 10862592 | tf_op jit(solution)/shard_map/while/body/eval_jaxpr/add | solution.py:160
  117.3 7.7 %copy.93 = f32[52,68,256]{2,1,0:T(8,128)} copy(f32[52,68,256]{1,0,2:T(8,128)} %maximum_add_fusion.2) | data formatting | bytes 7241728 | tf_op jit(solution)/shard_map/while/body/eval_jaxpr/dynamic_update_slice | solution.py:158
  124.9 4.3 %constant_dynamic-update-slice_fusion.5 = f32[68,68,256]{2,1,0:T(8,128)} fusion(f32[68,68,256]{2,1,0:T(8,128)} %get-tuple-element.380, f32[52,68,256]{2,1,0:T(8,128)} %copy.93, s32[]{:T(128)S(6)} %min.40), kind=kLoop, calls=%fused_computation.23.clone.1 | loop fusion | bytes 7667716 | tf_op jit(solution)/shard_map/while/body/eval_jaxpr/dynamic_update_slice | solution.py:158
  147.0 7.1 %copy.88 = f32[52,68,256]{1,0,2:T(8,128)} copy(f32[52,68,256]{2,1,0:T(8,128)} %constant_dynamic-slice_fusion.8) | data formatting | bytes 7241728 | tf_op jit(solution)/shard_map/while/body/eval_jaxpr/dynamic_slice | solution.py:155
  166.5 4.2 %concatenate.35 = f32[52,68,128]{1,0,2:T(8,128)} reshape(f32[3536,2,64]{0,2,1:T(8,128)} %convolution_bitcast_fusion.5) | data formatting | bytes 3620864 | tf_op jit(solution)/shard_map/while/body/eval_jaxpr/concatenate | solution.py:99
  173.5 8.9 %maximum_add_fusion.2 = f32[52,68,256]{1,0,2:T(8,128)} fusion(f32[52,68,256]{1,0,2:T(8,128)} %copy.88, f32[52,68,128]{1,0,2:T(8,128)} %concatenate.34, f32[52,68,128]{1,0,2:T(8,128)} %concatenate.35), kind=kLoop, calls=%fused_computation.clone.1 | loop fusion | flops 1810432 | bytes 10862592 | tf_op jit(solution)/shard_map/while/body/eval_jaxpr/add | solution.py:160
  182.4 7.7 %copy.93 = f32[52,68,256]{2,1,0:T(8,128)} copy(f32[52,68,256]{1,0,2:T(8,128)} %maximum_add_fusion.2) | data formatting | bytes 7241728 | tf_op jit(solution)/shard_map/while/body/eval_jaxpr/dynamic_update_slice | solution.py:158
  190.0 4.3 %constant_dynamic-update-slice_fusion.5 = f32[68,68,256]{2,1,0:T(8,128)} fusion(f32[68,68,256]{2,1,0:T(8,128)} %get-tuple-element.380, f32[52,68,256]{2,1,0:T(8,128)} %copy.93, s32[]{:T(128)S(6)} %min.40), kind=kLoop, calls=%fused_computation.23.clone.1 | loop fusion | bytes 7667716 | tf_op jit(solution)/shard_map/while/body/eval_jaxpr/dynamic_update_slice | solution.py:158
  212.0 7.1 %copy.88 = f32[52,68,256]{1,0,2:T(8,128)} copy(f32[52,68,256]{2,1,0:T(8,128)} %constant_dynamic-slice_fusion.8) | data formatting | bytes 7241728 | tf_op jit(solution)/shard_map/while/body/eval_jaxpr/dynamic_slice | solution.py:155
  231.5 4.2 %concatenate.35 = f32[52,68,128]{1,0,2:T(8,128)} reshape(f32[3536,2,64]{0,2,1:T(8,128)} %convolution_bitcast_fusion.5) | data formatting | bytes 3620864 | tf_op jit(solution)/shard_map/while/body/eval_jaxpr/concatenate | solution.py:99
  238.6 8.9 %maximum_add_fusion.2 = f32[52,68,256]{1,0,2:T(8,128)} fusion(f32[52,68,256]{1,0,2:T(8,128)} %copy.88, f32[52,68,128]{1,0,2:T(8,128)} %concatenate.34, f32[52,68,128]{1,0,2:T(8,128)} %concatenate.35), kind=kLoop, calls=%fused_computation.clone.1 | loop fusion | flops 1810432 | bytes 10862592 | tf_op jit(solution)/shard_map/while/body/eval_jaxpr/add | solution.py:160
  247.4 7.7 %copy.93 = f32[52,68,256]{2,1,0:T(8,128)} copy(f32[52,68,256]{1,0,2:T(8,128)} %maximum_add_fusion.2) | data formatting | bytes 7241728 | tf_op jit(solution)/shard_map/while/body/eval_jaxpr/dynamic_update_slice | solution.py:158
  255.1 4.2 %constant_dynamic-update-slice_fusion.5 = f32[68,68,256]{2,1,0:T(8,128)} fusion(f32[68,68,256]{2,1,0:T(8,128)} %get-tuple-element.380, f32[52,68,256]{2,1,0:T(8,128)} %copy.93, s32[]{:T(128)S(6)} %min.40), kind=kLoop, calls=%fused_computation.23.clone.1 | loop fusion | bytes 7667716 | tf_op jit(solution)/shard_map/while/body/eval_jaxpr/dynamic_update_slice | solution.py:158
  261.6 4.2 %collective-permute-start.4 = (f32[22,68,256]{2,1,0:T(8,128)S(1)}, f32[22,68,256]{2,1,0:T(8,128)S(1)}, u32[]{:S(2)}, u32[]{:S(2)}) collective-permute-start(f32[22,68,256]{2,1,0:T(8,128)S(1)} %get-tuple-element.275), channel_id=1, source_target_pairs={{32,0},{64,32},{96,64},{128,96},{160,128},{192,160},{224,192},{256... | collective-permute-start | bytes 4595720 | tf_op jit(solution)/shard_map/ppermute | solution.py:22
  267.9 31.2 %collective-permute-done.4 = f32[22,68,256]{2,1,0:T(8,128)S(1)} collective-permute-done((f32[22,68,256]{2,1,0:T(8,128)S(1)}, f32[22,68,256]{2,1,0:T(8,128)S(1)}, u32[]{:S(2)}, u32[]{:S(2)}) %collective-permute-start.4) | collective-permute-done | bytes 1531936 | tf_op jit(solution)/shard_map/ppermute | solution.py:22
  303.2 9.1 %collective-permute-start.6 = (f32[24,22,256]{2,0,1:T(8,128)S(1)}, f32[24,22,256]{2,0,1:T(8,128)S(1)}, u32[]{:S(2)}, u32[]{:S(2)}) collective-permute-start(f32[24,22,256]{2,0,1:T(8,128)S(1)} %copy.65), channel_id=1, source_target_pairs={{0,31},{1,0},{2,1},{3,2},{4,3},{5,4},{6,5},{7,6},{8,7},{9,8},{10,9... | collective-permute-start | bytes 1622024 | tf_op jit(solution)/shard_map/ppermute | solution.py:27
  314.5 17.0 %collective-permute-done.6 = f32[24,22,256]{2,0,1:T(8,128)S(1)} collective-permute-done((f32[24,22,256]{2,0,1:T(8,128)S(1)}, f32[24,22,256]{2,0,1:T(8,128)S(1)}, u32[]{:S(2)}, u32[]{:S(2)}) %collective-permute-start.6) | collective-permute-done | bytes 540704 | tf_op jit(solution)/shard_map/ppermute | solution.py:27
  (158 shorter events, 134.6 us)
Async XLA Ops:
  2.7 8.0 %collective-permute-start = (bf16[22,24,256]{2,0,1:T(8,128)(2,1)S(1)}, bf16[22,24,256]{2,0,1:T(8,128)(2,1)S(1)}, u32[]{:S(2)}, u32[]{:S(2)}) collective-permute-start(bf16[22,24,256]{2,0,1:T(8,128)(2,1)S(1)} %get-tuple-element.282), channel_id=1, source_target_pairs={{0,32},{32,64},{64,96},{96,128},{128,160},{160,192},{192,224},{224... | collective-permute-start | bytes 811016 | tf_op jit(solution)/shard_map/ppermute | solution.py:38
  4.6 8.0 %collective-permute-start.1 = (bf16[22,24,256]{2,0,1:T(8,128)(2,1)S(1)}, bf16[22,24,256]{2,0,1:T(8,128)(2,1)S(1)}, u32[]{:S(2)}, u32[]{:S(2)}) collective-permute-start(bf16[22,24,256]{2,0,1:T(8,128)(2,1)S(1)} %get-tuple-element.283), channel_id=1, source_target_pairs={{32,0},{64,32},{96,64},{128,96},{160,128},{192,160},{224,192},{256... | collective-permute-start | bytes 811016 | tf_op jit(solution)/shard_map/ppermute | solution.py:40
  14.0 39.2 %collective-permute-start.2 = (bf16[68,22,256]{2,0,1:T(8,128)(2,1)}, bf16[68,22,256]{2,0,1:T(8,128)(2,1)S(1)}, u32[]{:S(2)}, u32[]{:S(2)}) collective-permute-start(bf16[68,22,256]{2,0,1:T(8,128)(2,1)} %get-tuple-element.278), channel_id=1, source_target_pairs={{0,1},{1,2},{2,3},{3,4},{4,5},{5,6},{6,7},{7,8},{8,9},{9,10},{10,1... | collective-permute-start | bytes 2297864 | tf_op jit(solution)/shard_map/ppermute | solution.py:38
  18.3 40.7 %collective-permute-start.3 = (bf16[68,22,256]{2,0,1:T(8,128)(2,1)S(1)}, bf16[68,22,256]{2,0,1:T(8,128)(2,1)S(1)}, u32[]{:S(2)}, u32[]{:S(2)}) collective-permute-start(bf16[68,22,256]{2,0,1:T(8,128)(2,1)S(1)} %get-tuple-element.279), channel_id=1, source_target_pairs={{1,0},{2,1},{3,2},{4,3},{5,4},{6,5},{7,6},{8,7},{9,8},{10,9},{11,1... | collective-permute-start | bytes 2297864 | tf_op jit(solution)/shard_map/ppermute | solution.py:40
  75.9 13.0 %copy-start = (bf16[3536,128]{0,1:T(8,128)(2,1)}, bf16[3536,128]{0,1:T(8,128)(2,1)S(1)}, u32[]{:S(2)}) copy-start(bf16[3536,128]{0,1:T(8,128)(2,1)S(1)} %copy.91) | copy-start | bytes 2715652 | tf_op jit(solution)/shard_map/while
  91.2 1.3 copy-start.2
  95.8 1.9 copy-start.1
  101.4 4.2 %copy-start.4 = (f32[3536,2,64]{0,2,1:T(8,128)S(1)}, f32[3536,2,64]{0,2,1:T(8,128)}, u32[]{:S(2)}) copy-start(f32[3536,2,64]{0,2,1:T(8,128)} %convolution_bitcast_fusion.4) | copy-start | bytes 5431300 | tf_op jit(solution)/shard_map/while
  141.0 13.0 %copy-start = (bf16[3536,128]{0,1:T(8,128)(2,1)}, bf16[3536,128]{0,1:T(8,128)(2,1)S(1)}, u32[]{:S(2)}) copy-start(bf16[3536,128]{0,1:T(8,128)(2,1)S(1)} %copy.91) | copy-start | bytes 2715652 | tf_op jit(solution)/shard_map/while
  156.3 1.3 copy-start.2
  161.0 1.9 copy-start.1
  166.5 4.2 %copy-start.4 = (f32[3536,2,64]{0,2,1:T(8,128)S(1)}, f32[3536,2,64]{0,2,1:T(8,128)}, u32[]{:S(2)}) copy-start(f32[3536,2,64]{0,2,1:T(8,128)} %convolution_bitcast_fusion.4) | copy-start | bytes 5431300 | tf_op jit(solution)/shard_map/while
  206.1 13.0 %copy-start = (bf16[3536,128]{0,1:T(8,128)(2,1)}, bf16[3536,128]{0,1:T(8,128)(2,1)S(1)}, u32[]{:S(2)}) copy-start(bf16[3536,128]{0,1:T(8,128)(2,1)S(1)} %copy.91) | copy-start | bytes 2715652 | tf_op jit(solution)/shard_map/while
  221.4 1.3 copy-start.2
  226.0 1.9 copy-start.1
  231.5 4.2 %copy-start.4 = (f32[3536,2,64]{0,2,1:T(8,128)S(1)}, f32[3536,2,64]{0,2,1:T(8,128)}, u32[]{:S(2)}) copy-start(f32[3536,2,64]{0,2,1:T(8,128)} %convolution_bitcast_fusion.4) | copy-start | bytes 5431300 | tf_op jit(solution)/shard_map/while
  259.3 8.4 %copy-start.3 = (f32[68,68,256]{2,1,0:T(8,128)S(1)}, f32[68,68,256]{2,1,0:T(8,128)}, u32[]{:S(2)}) copy-start(f32[68,68,256]{2,1,0:T(8,128)} %get-tuple-element.211) | copy-start | bytes 14204932
  261.6 37.5 %collective-permute-start.4 = (f32[22,68,256]{2,1,0:T(8,128)S(1)}, f32[22,68,256]{2,1,0:T(8,128)S(1)}, u32[]{:S(2)}, u32[]{:S(2)}) collective-permute-start(f32[22,68,256]{2,1,0:T(8,128)S(1)} %get-tuple-element.275), channel_id=1, source_target_pairs={{32,0},{64,32},{96,64},{128,96},{160,128},{192,160},{224,192},{256... | collective-permute-start | bytes 4595720 | tf_op jit(solution)/shard_map/ppermute | solution.py:22
  265.8 36.8 %collective-permute-start.5 = (f32[22,68,256]{2,1,0:T(8,128)S(1)}, f32[22,68,256]{2,1,0:T(8,128)S(1)}, u32[]{:S(2)}, u32[]{:S(2)}) collective-permute-start(f32[22,68,256]{2,1,0:T(8,128)S(1)} %get-tuple-element.274), channel_id=1, source_target_pairs={{0,32},{32,64},{64,96},{96,128},{128,160},{160,192},{192,224},{224... | collective-permute-start | bytes 4595720 | tf_op jit(solution)/shard_map/ppermute | solution.py:22
  303.2 28.3 %collective-permute-start.6 = (f32[24,22,256]{2,0,1:T(8,128)S(1)}, f32[24,22,256]{2,0,1:T(8,128)S(1)}, u32[]{:S(2)}, u32[]{:S(2)}) collective-permute-start(f32[24,22,256]{2,0,1:T(8,128)S(1)} %copy.65), channel_id=1, source_target_pairs={{0,31},{1,0},{2,1},{3,2},{4,3},{5,4},{6,5},{7,6},{8,7},{9,8},{10,9... | collective-permute-start | bytes 1622024 | tf_op jit(solution)/shard_map/ppermute | solution.py:27
  312.5 23.1 %collective-permute-start.7 = (f32[24,22,256]{2,0,1:T(8,128)S(1)}, f32[24,22,256]{2,0,1:T(8,128)S(1)}, u32[]{:S(2)}, u32[]{:S(2)}) collective-permute-start(f32[24,22,256]{2,0,1:T(8,128)S(1)} %copy.67), channel_id=1, source_target_pairs={{0,1},{1,2},{2,3},{3,4},{4,5},{5,6},{6,7},{7,8},{8,9},{9,10},{10,1... | collective-permute-start | bytes 1622024 | tf_op jit(solution)/shard_map/ppermute | solution.py:27
where the time goes:
time: 343 us; the launch traced here: 341 us
  local copies, waits for them, and re-layouts  148 us (43%)
  waiting for transfers between devices  85.8 us (25%)
  starting transfers between devices  37.9 us (11%)
  other arithmetic  37.2 us (11%)
  matrix products  28 us (8%)
    dynamic_update_slice x6, local copies, waits for them, and re-layouts, step(): lax.dynamic_update_slice(gradient, current + grad_pair.reshape(slab_rows,...  35.8 us
    ppermute x2, waiting for transfers between devices, from_behind(): return lax.ppermute(block, axis, route)  34.5 us
    dynamic_slice x6, local copies, waits for them, and re-layouts, step(): lax.dynamic_slice(gradient, (slab_start, col_start, zero_index), (slab_ro...  33.7 us
    add x3, other arithmetic, step(): current + grad_pair.reshape(slab_rows, slab_cols, 2 * channels)  26.6 us
    ppermute x2, waiting for transfers between devices, extended_2(): lax.ppermute(tail, axis, [(i, (i + 1) % count) for i in range(ends)])  26.4 us
    concatenate x6, local copies, waits for them, and re-layouts, attend(): grad_pair = jnp.concatenate([grad_key, grad_value], axis=-1)  21.1 us
    ppermute x2, waiting for transfers between devices, from_behind_2(): lax.ppermute(value, axis, [(i, (i + by) % peers) for i in range(peers)])  17 us
    ppermute x2, starting transfers between devices, extended_2(): lax.ppermute(head, axis, [((i + 1) % count, i) for i in range(ends)])  14.5 us
  transfers between devices with their start and end apart: 8, of which 7 were waited for; matrix products, arithmetic and copies ran while one was open for 1% of the time, Pallas kernels for 0%

commit v1 on v0

v1 whole, which is shorter than its diff:
```python
import jax
import jax.numpy as jnp
from jax import lax
from jax.experimental import pallas as pl
from jax.experimental.pallas import tpu as pltpu
from jax.sharding import PartitionSpec as P

R = 22
T = 24
W = 3 * T
ROWS = T + 2 * R
BR = 8
NB = T // BR
SR = BR + 2 * R
NK = SR * W
NQ = 2 * BR * T
KR = 4
CK = KR * W
NC = SR // KR
F32 = jnp.float32
BF = jnp.bfloat16
NT = (((1,), (1,)), ((), ()))
TN = (((0,), (0,)), ((), ()))


def kernel_a(start, k_ref, aux_ref, q_ref, g_ref, p_ref, linv_ref, gs_ref, vn_ref, vm_ref, vs_ref, s_scr, acc):
    b = pl.program_id(0)
    base = pl.multiple_of(start[b] * W, 64)

    @pl.when(b == 0)
    def _():
        acc[...] = jnp.zeros_like(acc)

    q = q_ref[0]

    def scores(c, m):
        at = pl.multiple_of(base + c * CK, 32)
        lhs = jnp.concatenate([k_ref[pl.ds(at, CK), :], aux_ref[pl.ds(at, CK), :]], axis=1)
        s = lax.dot_general(lhs, q, NT, preferred_element_type=F32)
        s_scr[pl.ds(pl.multiple_of(c * CK, 32), CK), :] = s
        return jnp.maximum(m, jnp.max(s.reshape(CK // 8, 8, NQ), axis=0))

    m = lax.fori_loop(0, NC, scores, jnp.full((8, NQ), -3e38, F32))
    m = jnp.max(m, axis=0, keepdims=True)

    def expo(c, l):
        at = pl.multiple_of(c * CK, 32)
        p = jnp.exp(s_scr[pl.ds(at, CK), :] - m)
        p_ref[0, pl.ds(at, CK), :] = p.astype(BF)
        return l + jnp.sum(p.reshape(CK // 8, 8, NQ), axis=0)

    l = lax.fori_loop(0, NC, expo, jnp.zeros((8, NQ), F32))
    linv = 1.0 / jnp.sum(l, axis=0, keepdims=True)
    linv_ref[0] = jnp.broadcast_to(linv, (8, NQ))
    turned = jnp.transpose(jnp.broadcast_to(linv, (128, NQ)))
    gs = (g_ref[0].astype(F32) * turned).astype(BF)
    gs_ref[0] = gs

    def dv(c, _):
        at = pl.multiple_of(base + c * CK, 32)
        p = p_ref[0, pl.ds(pl.multiple_of(c * CK, 32), CK), :]
        acc[pl.ds(at, CK), :] += jnp.dot(p, gs, preferred_element_type=F32)
        return 0

    lax.fori_loop(0, NC, dv, 0)

    @pl.when(b == NB - 1)
    def _():
        vn_ref[...] = acc[: R * W, :].astype(BF)
        vm_ref[...] = acc[R * W : (R + T) * W, :]
        vs_ref[...] = acc[(R + T) * W :, :].astype(BF)


def kernel_b(start, k_ref, v_ref, q_ref, gs_ref, p_ref, linv_ref, o_ref, dq_ref, kn_ref, km_ref, ks_ref, ot, acc):
    b = pl.program_id(0)
    base = pl.multiple_of(start[b] * W, 64)

    @pl.when(b == 0)
    def _():
        acc[...] = jnp.zeros_like(acc)

    q = q_ref[0][:, :128]
    gs = gs_ref[0]
    ot[...] = jnp.zeros_like(ot)

    def attend(c, _):
        at = pl.multiple_of(base + c * CK, 32)
        p = p_ref[0, pl.ds(pl.multiple_of(c * CK, 32), CK), :]
        ot[...] += lax.dot_general(v_ref[pl.ds(at, CK), :], p, TN, preferred_element_type=F32)
        return 0

    lax.fori_loop(0, NC, attend, 0)
    lane = lax.broadcasted_iota(jnp.int32, (NQ // 2, 128), 1)
    o = jnp.transpose(ot[...] * linv_ref[0][:1])
    o_bf = o.astype(BF)
    o_ref[...] = jnp.where(lane < 64, o[: NQ // 2], o[NQ // 2 :]).astype(BF)
    row = jnp.sum(gs.astype(F32) * o_bf.astype(F32), axis=1, keepdims=True)
    corr = jnp.transpose(jnp.broadcast_to(row, (NQ, 128)))[:1]
    ot[...] = jnp.zeros_like(ot)

    def back(c, _):
        at = pl.multiple_of(base + c * CK, 32)
        p = p_ref[0, pl.ds(pl.multiple_of(c * CK, 32), CK), :]
        gw = lax.dot_general(v_ref[pl.ds(at, CK), :], gs, NT, preferred_element_type=F32)
        ds = (p.astype(F32) * (gw - corr)).astype(BF)
        acc[pl.ds(at, CK), :] += jnp.dot(ds, q, preferred_element_type=F32)
        ot[...] += lax.dot_general(k_ref[pl.ds(at, CK), :], ds, TN, preferred_element_type=F32)
        return 0

    lax.fori_loop(0, NC, back, 0)
    dq = jnp.transpose(ot[...] * 0.125)
    dq_ref[...] = jnp.where(lane < 64, dq[: NQ // 2], dq[NQ // 2 :]).astype(BF)

    @pl.when(b == NB - 1)
    def _():
        kn_ref[...] = acc[: R * W, :].astype(BF)
        km_ref[...] = acc[R * W : (R + T) * W, :]
        ks_ref[...] = acc[(R + T) * W :, :].astype(BF)


def whole(shape):
    return pl.BlockSpec(shape, lambda b, s: (0,) * len(shape))


def per_block(shape):
    return pl.BlockSpec((1,) + shape, lambda b, s: (b,) + (0,) * len(shape))


def sds(shape, dtype):
    return jax.ShapeDtypeStruct(shape, dtype)


grads_shape = [sds((R * W, 128), BF), sds((T * W, 128), F32), sds((R * W, 128), BF)]
grads_spec = [whole((R * W, 128)), whole((T * W, 128)), whole((R * W, 128))]


def run_a(start, k, aux, q, g):
    return pl.pallas_call(
        kernel_a,
        grid_spec=pltpu.PrefetchScalarGridSpec(
            num_scalar_prefetch=1,
            grid=(NB,),
            in_specs=[whole((ROWS * W, 128)), whole((ROWS * W, 128)), per_block((NQ, 256)), per_block((NQ, 128))],
            out_specs=[per_block((NK, NQ)), per_block((8, NQ)), per_block((NQ, 128))] + grads_spec,
            scratch_shapes=[pltpu.VMEM((NK, NQ), F32), pltpu.VMEM((ROWS * W, 128), F32)],
        ),
        out_shape=[sds((NB, NK, NQ), BF), sds((NB, 8, NQ), F32), sds((NB, NQ, 128), BF)] + grads_shape,
        compiler_params=pltpu.CompilerParams(vmem_limit_bytes=48 << 20),
        cost_estimate=pl.CostEstimate(flops=6_000_000_000, bytes_accessed=14_000_000, transcendentals=4_000_000),
        name="scores_and_dv",
    )(start, k, aux, q, g)


def run_b(start, k, v, q, gs, p, linv):
    return pl.pallas_call(
        kernel_b,
        grid_spec=pltpu.PrefetchScalarGridSpec(
            num_scalar_prefetch=1,
            grid=(NB,),
            in_specs=[whole((ROWS * W, 128)), whole((ROWS * W, 128)), per_block((NQ, 256)), per_block((NQ, 128)), per_block((NK, NQ)), per_block((8, NQ))],
            out_specs=[pl.BlockSpec((NQ // 2, 128), lambda b, s: (b, 0)), pl.BlockSpec((NQ // 2, 128), lambda b, s: (b, 0))] + grads_spec,
            scratch_shapes=[pltpu.VMEM((128, NQ), F32), pltpu.VMEM((ROWS * W, 128), F32)],
        ),
        out_shape=[sds((T * T, 128), BF), sds((T * T, 128), BF)] + grads_shape,
        compiler_params=pltpu.CompilerParams(vmem_limit_bytes=48 << 20),
        cost_estimate=pl.CostEstimate(flops=8_000_000_000, bytes_accessed=14_000_000, transcendentals=0),
        name="attended_and_dk",
    )(start, k, v, q, gs, p, linv)


def tables(first_row, height):
    i0 = first_row + BR * jnp.arange(NB, dtype=jnp.int32)
    f0 = jnp.clip(i0 - R, 0, height - 45)
    start = jnp.clip(f0 - first_row + R, 0, ROWS - SR) // 8 * 8
    krow = lax.broadcasted_iota(jnp.int32, (ROWS, W, 128), 0) + (first_row - R)
    kcol = lax.broadcasted_iota(jnp.int32, (ROWS, W, 128), 1)
    lane = lax.broadcasted_iota(jnp.int32, (ROWS, W, 128), 2)
    f = jnp.clip(first_row + lane - R, 0, height - 45)
    row_out = (lane < T) & ((krow < f) | (krow >= f + 45))
    qcol = lane - T
    col_out = (lane >= T) & (lane < 2 * T) & ((kcol < qcol + 2) | (kcol > qcol + 46))
    aux = jnp.where(row_out | col_out, -1e30, 0.0).astype(BF).reshape(ROWS * W, 128)
    return start.astype(jnp.int32), aux


def spread(x, scale):
    x = (x.reshape(NB, 1, BR * T, 128) * scale).astype(BF)
    lane = lax.broadcasted_iota(jnp.int32, (1, 2, 1, 128), 3) // 64
    head = lax.broadcasted_iota(jnp.int32, (1, 2, 1, 128), 1)
    return jnp.where(lane == head, x, jnp.zeros((), BF)).reshape(NB, NQ, 128)


def with_marks(q):
    lane = lax.broadcasted_iota(jnp.int32, (NB, 2, BR, T, 128), 4)
    row = lax.broadcasted_iota(jnp.int32, (NB, 2, BR, T, 128), 0) * BR + lax.broadcasted_iota(jnp.int32, (NB, 2, BR, T, 128), 2)
    col = lax.broadcasted_iota(jnp.int32, (NB, 2, BR, T, 128), 3)
    mark = jnp.where((lane == row) | (lane == T + col), 1.0, 0.0).astype(BF).reshape(NB, NQ, 128)
    return jnp.concatenate([spread(q, 0.125), mark], axis=2)


def shift(x, axis, by, closed):
    n = lax.axis_size(axis)
    pairs = [(i, (i + by) % n) for i in range(n) if closed or 0 <= i + by < n]
    return lax.ppermute(x, axis, pairs)


def extend(x):
    mid = jnp.concatenate([shift(x, "lon", 1, True), x, shift(x, "lon", -1, True)], axis=1)
    north = shift(mid[T - R :], "lat", 1, False)
    south = shift(mid[:R], "lat", -1, False)
    return jnp.concatenate([north, mid, south], axis=0).reshape(ROWS * W, 128)


def fold(north, mid, south):
    north = north.reshape(R, W, 128)
    south = south.reshape(R, W, 128)
    from_south = shift(north, "lat", -1, False).astype(F32)
    from_north = shift(south, "lat", 1, False).astype(F32)
    pad = ((T - R, 0), (0, 0), (0, 0)), ((0, T - R), (0, 0), (0, 0))
    mid = mid.reshape(T, W, 128) + jnp.pad(from_south, pad[0]) + jnp.pad(from_north, pad[1])
    from_east = shift(mid[:, :T].astype(BF), "lon", -1, True).astype(F32)
    from_west = shift(mid[:, 2 * T :].astype(BF), "lon", 1, True).astype(F32)
    return (mid[:, T : 2 * T] + from_east + from_west).astype(BF)


def body(queries, keys, values, out_grad):
    height = T * lax.axis_size("lat")
    start, aux = tables(lax.axis_index("lat") * T, height)
    q = with_marks(queries)
    g = spread(out_grad, 1.0)
    k = extend(keys)
    v = extend(values)
    p, linv, gs, *dv = run_a(start, k, aux, q, g)
    grad_values = fold(*dv)
    attended, grad_queries, *dk = run_b(start, k, v, q, gs, p, linv)
    grad_keys = fold(*dk)
    return attended.reshape(T, T, 128), grad_queries.reshape(T, T, 128), grad_keys, grad_values


def solution(mesh):
    spec = P("lat", "lon", None)
    return jax.shard_map(body, mesh=mesh, in_specs=(spec,) * 4, out_specs=(spec,) * 4, check_vma=False)
```

time: 343 us -> 148 us (0.43)
  local copies, waits for them, and re-layouts: 148 us -> 1.55 us
  waiting for transfers between devices: 85.8 us -> 18.3 us
  Pallas kernels: 0 us -> 57.1 us
  other arithmetic: 37.2 us -> 6.17 us
  matrix products: 28 us -> 0 us
  starting transfers between devices: 37.9 us -> 62.7 us
    ppermute x8 -> x16, waiting for transfers between devices: 85.8 us -> 18.3 us  [shift(): return lax.ppermute(x, axis, pairs)]
    pallas_call x0 -> x2, Pallas kernels: none -> 57.1 us  [the longest x1 32 us: run_b(): pl.pallas_call(kernel_b, grid_spec=pltpu.PrefetchScalarGridSpec(num_scala...]
    dynamic_slice x18 -> x0, local copies, waits for them, and re-layouts: 45.4 us -> none  [the longest x6 33.7 us: step(): lax.dynamic_slice(gradient, (slab_start, col_start, zero_index), (slab_ro...]
    dynamic_update_slice x15 -> x0, local copies, waits for them, and re-layouts: 38.4 us -> none  [the longest x6 35.8 us: step(): lax.dynamic_update_slice(gradient, current + grad_pair.reshape(slab_rows,...]
    dot_general x18 -> x0, matrix products: 28 us -> none  [the longest x3 6.65 us: attend(): jnp.einsum('qhd,khd->hqk', grad_heads, value_heads, preferred_element_typ...]
    add x14 -> x3, other arithmetic: 27 us -> 0.01 us  [the longest x1 0.01 us: tables(): qcol + 2]
    ppermute x8 -> x16, starting transfers between devices: 37.9 us -> 62.7 us  [shift(): return lax.ppermute(x, axis, pairs)]
    concatenate x7 -> x2, local copies, waits for them, and re-layouts: 22.1 us -> 0.06 us  [extend(): jnp.concatenate([shift(x, 'lon', 1, True), x, shift(x, 'lon', -1, True)],...]
  transfers between devices with their start and end apart: 8 -> 16, of which waited for: 7 -> 4; matrix products, arithmetic and copies ran while one was open for 1% -> 4% of each run, Pallas kernels for 0% -> 39%
where the time goes in v1:
time: 148 us; the launch traced here: 147 us
  starting transfers between devices  62.7 us (42%)
  Pallas kernels  57.1 us (39%)
  waiting for transfers between devices  18.3 us (12%)
  other arithmetic  6.17 us (4%)
  local copies, waits for them, and re-layouts  1.55 us (1%)
    ppermute x16, starting transfers between devices, shift(): return lax.ppermute(x, axis, pairs)  62.7 us
    pallas_call x1, Pallas kernels, run_b(): pl.pallas_call(kernel_b, grid_spec=pltpu.PrefetchScalarGridSpec(num_scala...  32 us
    pallas_call x1, Pallas kernels, run_a(): pl.pallas_call(kernel_a, grid_spec=pltpu.PrefetchScalarGridSpec(num_scala...  25.2 us
    ppermute x16, waiting for transfers between devices, shift(): return lax.ppermute(x, axis, pairs)  18.3 us
  transfers between devices with their start and end apart: 16, of which 4 were waited for; matrix products, arithmetic and copies ran while one was open for 4% of the time, Pallas kernels for 39%

profile of v1, /device:TPU:18, one launch (start us, length us, event | category | flops | bytes accessed | tf_op | source)
XLA Modules:
  0.0 147.0 jit_solution(10136015815210853912)
XLA Ops:
  0.6 4.2 %collective-permute-start = (bf16[24,24,128]{2,1,0:T(8,128)(2,1)}, bf16[24,24,128]{2,1,0:T(8,128)(2,1)S(1)}, u32[]{:S(2)}, u32[]{:S(2)}) collective-permute-start(bf16[24,24,128]{2,1,0:T(8,128)(2,1)} %param.5), channel_id=1, source_target_pairs={{0,1},{1,2},{2,3},{3,4},{4,5},{5,6},{6,7},{7,8},{8,9},{9,10},{10,1... | collective-permute-start | bytes 442376 | tf_op jit(solution)/shard_map/ppermute | solution.py:204
  4.8 10.9 %collective-permute-start.1 = (bf16[24,24,128]{2,1,0:T(8,128)(2,1)}, bf16[24,24,128]{2,1,0:T(8,128)(2,1)S(1)}, u32[]{:S(2)}, u32[]{:S(2)}) collective-permute-start(bf16[24,24,128]{2,1,0:T(8,128)(2,1)} %param.5), channel_id=1, source_target_pairs={{0,31},{1,0},{2,1},{3,2},{4,3},{5,4},{6,5},{7,6},{8,7},{9,8},{10,9... | collective-permute-start | bytes 442376 | tf_op jit(solution)/shard_map/ppermute | solution.py:204
  15.7 1.9 %collective-permute-start.4 = (bf16[24,24,128]{2,1,0:T(8,128)(2,1)}, bf16[24,24,128]{2,1,0:T(8,128)(2,1)S(1)}, u32[]{:S(2)}, u32[]{:S(2)}) collective-permute-start(bf16[24,24,128]{2,1,0:T(8,128)(2,1)} %param.6), channel_id=1, source_target_pairs={{0,1},{1,2},{2,3},{3,4},{4,5},{5,6},{6,7},{7,8},{8,9},{9,10},{10,1... | collective-permute-start | bytes 442376 | tf_op jit(solution)/shard_map/ppermute | solution.py:204
  17.6 7.5 %collective-permute-start.5 = (bf16[24,24,128]{2,1,0:T(8,128)(2,1)}, bf16[24,24,128]{2,1,0:T(8,128)(2,1)S(1)}, u32[]{:S(2)}, u32[]{:S(2)}) collective-permute-start(bf16[24,24,128]{2,1,0:T(8,128)(2,1)} %param.6), channel_id=1, source_target_pairs={{0,31},{1,0},{2,1},{3,2},{4,3},{5,4},{6,5},{7,6},{8,7},{9,8},{10,9... | collective-permute-start | bytes 442376 | tf_op jit(solution)/shard_map/ppermute | solution.py:204
  25.5 0.9 broadcast_multiply_fusion
  26.9 2.8 %select_convert_fusion.aux_ref = bf16[4896,128]{1,0:T(8,128)(2,1)S(1)} fusion(s32[128]{0:T(128)S(1)} %get-tuple-element.47, s32[128]{0:T(128)S(1)} %get-tuple-element.46, s32[128]{0:T(128)S(1)} %get-tuple-element.41, s32[128]{0:T(128)S(1)} %get-tuple-element.40, s32[4896]{0:T(1024)S(1)} %iota.136, s32[4896]{0:T(1024)S(1)} %iota.128, ...), kind=kLoop, calls=%fused_computation | loop fusion | flops 6893568 | bytes 1294848 | tf_op jit(solution)/shard_map/convert_element_type | solution.py:182
  30.8 1.9 %collective-permute-start.2 = (bf16[22,72,128]{2,1,0:T(8,128)(2,1)S(1)}, bf16[22,72,128]{2,1,0:T(8,128)(2,1)S(1)}, u32[]{:S(2)}, u32[]{:S(2)}) collective-permute-start(bf16[22,72,128]{2,1,0:T(8,128)(2,1)S(1)} %get-tuple-element.36), channel_id=1, source_target_pairs={{0,32},{32,64},{64,96},{96,128},{128,160},{160,192},{192,224},{224... | collective-permute-start | bytes 1216520 | tf_op jit(solution)/shard_map/ppermute | solution.py:204
  32.7 3.6 %collective-permute-start.3 = (bf16[22,72,128]{2,1,0:T(8,128)(2,1)S(1)}, bf16[22,72,128]{2,1,0:T(8,128)(2,1)S(1)}, u32[]{:S(2)}, u32[]{:S(2)}) collective-permute-start(bf16[22,72,128]{2,1,0:T(8,128)(2,1)S(1)} %get-tuple-element.37), channel_id=1, source_target_pairs={{32,0},{64,32},{96,64},{128,96},{160,128},{192,160},{224,192},{256... | collective-permute-start | bytes 1216520 | tf_op jit(solution)/shard_map/ppermute | solution.py:204
  36.6 2.4 %collective-permute-start.6 = (bf16[22,72,128]{2,1,0:T(8,128)(2,1)S(1)}, bf16[22,72,128]{2,1,0:T(8,128)(2,1)S(1)}, u32[]{:S(2)}, u32[]{:S(2)}) collective-permute-start(bf16[22,72,128]{2,1,0:T(8,128)(2,1)S(1)} %get-tuple-element.34), channel_id=1, source_target_pairs={{0,32},{32,64},{64,96},{96,128},{128,160},{160,192},{192,224},{224... | collective-permute-start | bytes 1216520 | tf_op jit(solution)/shard_map/ppermute | solution.py:204
  39.0 3.1 %collective-permute-start.7 = (bf16[22,72,128]{2,1,0:T(8,128)(2,1)S(1)}, bf16[22,72,128]{2,1,0:T(8,128)(2,1)S(1)}, u32[]{:S(2)}, u32[]{:S(2)}) collective-permute-start(bf16[22,72,128]{2,1,0:T(8,128)(2,1)S(1)} %get-tuple-element.35), channel_id=1, source_target_pairs={{32,0},{64,32},{96,64},{128,96},{160,128},{192,160},{224,192},{256... | collective-permute-start | bytes 1216520 | tf_op jit(solution)/shard_map/ppermute | solution.py:204
  42.2 3.8 %collective-permute-done.3 = bf16[22,72,128]{2,1,0:T(8,128)(2,1)S(1)} collective-permute-done((bf16[22,72,128]{2,1,0:T(8,128)(2,1)S(1)}, bf16[22,72,128]{2,1,0:T(8,128)(2,1)S(1)}, u32[]{:S(2)}, u32[]{:S(2)}) %collective-permute-start.3) | collective-permute-done | bytes 405536 | tf_op jit(solution)/shard_map/ppermute | solution.py:204
  46.1 25.2 %scores_and_dv.1 = (bf16[3,3744,384]{2,1,0:T(8,128)(2,1)}, f32[3,8,384]{2,1,0:T(8,128)S(1)}, bf16[3,384,128]{2,1,0:T(8,128)(2,1)S(1)}, bf16[1584,128]{1,0:T(8,12...) custom-call(s32[3]{0:T(128)S(1)} %fusion.5.start, bf16[4896,128]{1,0:T(8,128)(2,1)S(1)} %bitcast.17, ...), custom_call_target="tpu_custom_call" | custom-call | flops 6000000000 | bytes 14000000 | tf_op jit(solution)/shard_map/scores_and_dv/pallas_call | solution.py:138
  71.3 4.1 %collective-permute-start.12 = (bf16[22,72,128]{2,1,0:T(8,128)(2,1)S(1)}, bf16[22,72,128]{2,1,0:T(8,128)(2,1)S(1)}, u32[]{:S(2)}, u32[]{:S(2)}) collective-permute-start(bf16[22,72,128]{2,1,0:T(8,128)(2,1)S(1)} %bitcast.25), channel_id=1, source_target_pairs={{32,0},{64,32},{96,64},{128,96},{160,128},{192,160},{224,192},{256... | collective-permute-start | bytes 1216520 | tf_op jit(solution)/shard_map/ppermute | solution.py:204
  75.4 1.9 %collective-permute-start.13 = (bf16[22,72,128]{2,1,0:T(8,128)(2,1)S(1)}, bf16[22,72,128]{2,1,0:T(8,128)(2,1)S(1)}, u32[]{:S(2)}, u32[]{:S(2)}) collective-permute-start(bf16[22,72,128]{2,1,0:T(8,128)(2,1)S(1)} %bitcast.23), channel_id=1, source_target_pairs={{0,32},{32,64},{64,96},{96,128},{128,160},{160,192},{192,224},{224... | collective-permute-start | bytes 1216520 | tf_op jit(solution)/shard_map/ppermute | solution.py:204
  77.5 32.0 %attended_and_dk.1 = (bf16[576,128]{1,0:T(8,128)(2,1)}, bf16[576,128]{1,0:T(8,128)(2,1)}, bf16[1584,128]{1,0:T(8,128)(2,1)S(1)}, f32[1728,128]{1,0:T(8,128)S(1)}, bf16[1584,128]{1,0:T(8,128)(2,1)S(1)}) custom-call(s32[3]{0:T(128)S(1)} %fusion.5.start, bf16[4896,128]{1,0:T(8,128)(2,1)S(1)} %bitcast.18, bf16[4896,128]{1,0:T(8,128)(2,1)S(1)} %bitcast.19, ...), custom_call_target="tpu_custom_call" | custom-call | flops 8000000000 | bytes 14000000 | tf_op jit(solution)/shard_map/attended_and_dk/pallas_call | solution.py:155
  109.5 3.6 %collective-permute-start.8 = (bf16[22,72,128]{2,1,0:T(8,128)(2,1)S(1)}, bf16[22,72,128]{2,1,0:T(8,128)(2,1)S(1)}, u32[]{:S(2)}, u32[]{:S(2)}) collective-permute-start(bf16[22,72,128]{2,1,0:T(8,128)(2,1)S(1)} %bitcast.24), channel_id=1, source_target_pairs={{32,0},{64,32},{96,64},{128,96},{160,128},{192,160},{224,192},{256... | collective-permute-start | bytes 1216520 | tf_op jit(solution)/shard_map/ppermute | solution.py:204
  113.1 2.8 %collective-permute-start.9 = (bf16[22,72,128]{2,1,0:T(8,128)(2,1)S(1)}, bf16[22,72,128]{2,1,0:T(8,128)(2,1)S(1)}, u32[]{:S(2)}, u32[]{:S(2)}) collective-permute-start(bf16[22,72,128]{2,1,0:T(8,128)(2,1)S(1)} %bitcast.22), channel_id=1, source_target_pairs={{0,32},{32,64},{64,96},{96,128},{128,160},{160,192},{192,224},{224... | collective-permute-start | bytes 1216520 | tf_op jit(solution)/shard_map/ppermute | solution.py:204
  116.1 2.9 %collective-permute-start.14 = (bf16[24,24,128]{2,1,0:T(8,128)(2,1)S(1)}, bf16[24,24,128]{2,1,0:T(8,128)(2,1)S(1)}, u32[]{:S(2)}, u32[]{:S(2)}) collective-permute-start(bf16[24,24,128]{2,1,0:T(8,128)(2,1)S(1)} %get-tuple-element.30), channel_id=1, source_target_pairs={{0,31},{1,0},{2,1},{3,2},{4,3},{5,4},{6,5},{7,6},{8,7},{9,8},{10,9... | collective-permute-start | bytes 442376 | tf_op jit(solution)/shard_map/ppermute | solution.py:204
  119.1 4.4 %collective-permute-start.15 = (bf16[24,24,128]{2,1,0:T(8,128)(2,1)S(1)}, bf16[24,24,128]{2,1,0:T(8,128)(2,1)S(1)}, u32[]{:S(2)}, u32[]{:S(2)}) collective-permute-start(bf16[24,24,128]{2,1,0:T(8,128)(2,1)S(1)} %get-tuple-element.31), channel_id=1, source_target_pairs={{0,1},{1,2},{2,3},{3,4},{4,5},{5,6},{6,7},{7,8},{8,9},{9,10},{10,1... | collective-permute-start | bytes 442376 | tf_op jit(solution)/shard_map/ppermute | solution.py:204
  123.5 9.5 %collective-permute-done.9 = bf16[22,72,128]{2,1,0:T(8,128)(2,1)S(1)} collective-permute-done((bf16[22,72,128]{2,1,0:T(8,128)(2,1)S(1)}, bf16[22,72,128]{2,1,0:T(8,128)(2,1)S(1)}, u32[]{:S(2)}, u32[]{:S(2)}) %collective-permute-start.9) | collective-permute-done | bytes 405536 | tf_op jit(solution)/shard_map/ppermute | solution.py:204
  133.2 1.9 %collective-permute-start.10 = (bf16[24,24,128]{2,1,0:T(8,128)(2,1)S(1)}, bf16[24,24,128]{2,1,0:T(8,128)(2,1)S(1)}, u32[]{:S(2)}, u32[]{:S(2)}) collective-permute-start(bf16[24,24,128]{2,1,0:T(8,128)(2,1)S(1)} %get-tuple-element.32), channel_id=1, source_target_pairs={{0,31},{1,0},{2,1},{3,2},{4,3},{5,4},{6,5},{7,6},{8,7},{9,8},{10,9... | collective-permute-start | bytes 442376 | tf_op jit(solution)/shard_map/ppermute | solution.py:204
  135.1 5.4 %collective-permute-start.11 = (bf16[24,24,128]{2,1,0:T(8,128)(2,1)S(1)}, bf16[24,24,128]{2,1,0:T(8,128)(2,1)S(1)}, u32[]{:S(2)}, u32[]{:S(2)}) collective-permute-start(bf16[24,24,128]{2,1,0:T(8,128)(2,1)S(1)} %get-tuple-element.33), channel_id=1, source_target_pairs={{0,1},{1,2},{2,3},{3,4},{4,5},{5,6},{6,7},{7,8},{8,9},{9,10},{10,1... | collective-permute-start | bytes 442376 | tf_op jit(solution)/shard_map/ppermute | solution.py:204
  141.3 0.9 collective-permute-done.10
  142.2 4.0 %collective-permute-done.11 = bf16[24,24,128]{2,1,0:T(8,128)(2,1)S(1)} collective-permute-done((bf16[24,24,128]{2,1,0:T(8,128)(2,1)S(1)}, bf16[24,24,128]{2,1,0:T(8,128)(2,1)S(1)}, u32[]{:S(2)}, u32[]{:S(2)}) %collective-permute-start.11) | collective-permute-done | bytes 147488 | tf_op jit(solution)/shard_map/ppermute | solution.py:204
  (56 shorter events, 4.0 us)
Async XLA Ops:
  0.6 29.1 %copy-start = (bf16[24,24,128]{2,1,0:T(8,128)(2,1)S(1)}, bf16[24,24,128]{2,1,0:T(8,128)(2,1)}, u32[]{:S(2)}) copy-start(bf16[24,24,128]{2,1,0:T(8,128)(2,1)} %param.7) | copy-start | bytes 442372
  0.6 29.2 %collective-permute-start = (bf16[24,24,128]{2,1,0:T(8,128)(2,1)}, bf16[24,24,128]{2,1,0:T(8,128)(2,1)S(1)}, u32[]{:S(2)}, u32[]{:S(2)}) collective-permute-start(bf16[24,24,128]{2,1,0:T(8,128)(2,1)} %param.5), channel_id=1, source_target_pairs={{0,1},{1,2},{2,3},{3,4},{4,5},{5,6},{6,7},{7,8},{8,9},{9,10},{10,1... | collective-permute-start | bytes 442376 | tf_op jit(solution)/shard_map/ppermute | solution.py:204
  4.8 25.8 %collective-permute-start.1 = (bf16[24,24,128]{2,1,0:T(8,128)(2,1)}, bf16[24,24,128]{2,1,0:T(8,128)(2,1)S(1)}, u32[]{:S(2)}, u32[]{:S(2)}) collective-permute-start(bf16[24,24,128]{2,1,0:T(8,128)(2,1)} %param.5), channel_id=1, source_target_pairs={{0,31},{1,0},{2,1},{3,2},{4,3},{5,4},{6,5},{7,6},{8,7},{9,8},{10,9... | collective-permute-start | bytes 442376 | tf_op jit(solution)/shard_map/ppermute | solution.py:204
  15.7 20.7 %collective-permute-start.4 = (bf16[24,24,128]{2,1,0:T(8,128)(2,1)}, bf16[24,24,128]{2,1,0:T(8,128)(2,1)S(1)}, u32[]{:S(2)}, u32[]{:S(2)}) collective-permute-start(bf16[24,24,128]{2,1,0:T(8,128)(2,1)} %param.6), channel_id=1, source_target_pairs={{0,1},{1,2},{2,3},{3,4},{4,5},{5,6},{6,7},{7,8},{8,9},{9,10},{10,1... | collective-permute-start | bytes 442376 | tf_op jit(solution)/shard_map/ppermute | solution.py:204
  17.6 18.8 %collective-permute-start.5 = (bf16[24,24,128]{2,1,0:T(8,128)(2,1)}, bf16[24,24,128]{2,1,0:T(8,128)(2,1)S(1)}, u32[]{:S(2)}, u32[]{:S(2)}) collective-permute-start(bf16[24,24,128]{2,1,0:T(8,128)(2,1)} %param.6), channel_id=1, source_target_pairs={{0,31},{1,0},{2,1},{3,2},{4,3},{5,4},{6,5},{7,6},{8,7},{9,8},{10,9... | collective-permute-start | bytes 442376 | tf_op jit(solution)/shard_map/ppermute | solution.py:204
  29.7 0.9 copy-start.1
  30.6 5.8 %copy-start.2 = (bf16[24,24,128]{2,1,0:T(8,128)(2,1)S(1)}, bf16[24,24,128]{2,1,0:T(8,128)(2,1)}, u32[]{:S(2)}) copy-start(bf16[24,24,128]{2,1,0:T(8,128)(2,1)} %param.6) | copy-start | bytes 442372
  30.8 11.4 %collective-permute-start.2 = (bf16[22,72,128]{2,1,0:T(8,128)(2,1)S(1)}, bf16[22,72,128]{2,1,0:T(8,128)(2,1)S(1)}, u32[]{:S(2)}, u32[]{:S(2)}) collective-permute-start(bf16[22,72,128]{2,1,0:T(8,128)(2,1)S(1)} %get-tuple-element.36), channel_id=1, source_target_pairs={{0,32},{32,64},{64,96},{96,128},{128,160},{160,192},{192,224},{224... | collective-permute-start | bytes 1216520 | tf_op jit(solution)/shard_map/ppermute | solution.py:204
  32.7 13.3 %collective-permute-start.3 = (bf16[22,72,128]{2,1,0:T(8,128)(2,1)S(1)}, bf16[22,72,128]{2,1,0:T(8,128)(2,1)S(1)}, u32[]{:S(2)}, u32[]{:S(2)}) collective-permute-start(bf16[22,72,128]{2,1,0:T(8,128)(2,1)S(1)} %get-tuple-element.37), channel_id=1, source_target_pairs={{32,0},{64,32},{96,64},{128,96},{160,128},{192,160},{224,192},{256... | collective-permute-start | bytes 1216520 | tf_op jit(solution)/shard_map/ppermute | solution.py:204
  36.6 40.7 %collective-permute-start.6 = (bf16[22,72,128]{2,1,0:T(8,128)(2,1)S(1)}, bf16[22,72,128]{2,1,0:T(8,128)(2,1)S(1)}, u32[]{:S(2)}, u32[]{:S(2)}) collective-permute-start(bf16[22,72,128]{2,1,0:T(8,128)(2,1)S(1)} %get-tuple-element.34), channel_id=1, source_target_pairs={{0,32},{32,64},{64,96},{96,128},{128,160},{160,192},{192,224},{224... | collective-permute-start | bytes 1216520 | tf_op jit(solution)/shard_map/ppermute | solution.py:204
  39.0 38.3 %collective-permute-start.7 = (bf16[22,72,128]{2,1,0:T(8,128)(2,1)S(1)}, bf16[22,72,128]{2,1,0:T(8,128)(2,1)S(1)}, u32[]{:S(2)}, u32[]{:S(2)}) collective-permute-start(bf16[22,72,128]{2,1,0:T(8,128)(2,1)S(1)} %get-tuple-element.35), channel_id=1, source_target_pairs={{32,0},{64,32},{96,64},{128,96},{160,128},{192,160},{224,192},{256... | collective-permute-start | bytes 1216520 | tf_op jit(solution)/shard_map/ppermute | solution.py:204
  71.3 44.6 %collective-permute-start.12 = (bf16[22,72,128]{2,1,0:T(8,128)(2,1)S(1)}, bf16[22,72,128]{2,1,0:T(8,128)(2,1)S(1)}, u32[]{:S(2)}, u32[]{:S(2)}) collective-permute-start(bf16[22,72,128]{2,1,0:T(8,128)(2,1)S(1)} %bitcast.25), channel_id=1, source_target_pairs={{32,0},{64,32},{96,64},{128,96},{160,128},{192,160},{224,192},{256... | collective-permute-start | bytes 1216520 | tf_op jit(solution)/shard_map/ppermute | solution.py:204
  75.4 40.5 %collective-permute-start.13 = (bf16[22,72,128]{2,1,0:T(8,128)(2,1)S(1)}, bf16[22,72,128]{2,1,0:T(8,128)(2,1)S(1)}, u32[]{:S(2)}, u32[]{:S(2)}) collective-permute-start(bf16[22,72,128]{2,1,0:T(8,128)(2,1)S(1)} %bitcast.23), channel_id=1, source_target_pairs={{0,32},{32,64},{64,96},{96,128},{128,160},{160,192},{192,224},{224... | collective-permute-start | bytes 1216520 | tf_op jit(solution)/shard_map/ppermute | solution.py:204
  109.5 14.0 %collective-permute-start.8 = (bf16[22,72,128]{2,1,0:T(8,128)(2,1)S(1)}, bf16[22,72,128]{2,1,0:T(8,128)(2,1)S(1)}, u32[]{:S(2)}, u32[]{:S(2)}) collective-permute-start(bf16[22,72,128]{2,1,0:T(8,128)(2,1)S(1)} %bitcast.24), channel_id=1, source_target_pairs={{32,0},{64,32},{96,64},{128,96},{160,128},{192,160},{224,192},{256... | collective-permute-start | bytes 1216520 | tf_op jit(solution)/shard_map/ppermute | solution.py:204
  113.1 19.9 %collective-permute-start.9 = (bf16[22,72,128]{2,1,0:T(8,128)(2,1)S(1)}, bf16[22,72,128]{2,1,0:T(8,128)(2,1)S(1)}, u32[]{:S(2)}, u32[]{:S(2)}) collective-permute-start(bf16[22,72,128]{2,1,0:T(8,128)(2,1)S(1)} %bitcast.22), channel_id=1, source_target_pairs={{0,32},{32,64},{64,96},{96,128},{128,160},{160,192},{192,224},{224... | collective-permute-start | bytes 1216520 | tf_op jit(solution)/shard_map/ppermute | solution.py:204
  116.1 24.4 %collective-permute-start.14 = (bf16[24,24,128]{2,1,0:T(8,128)(2,1)S(1)}, bf16[24,24,128]{2,1,0:T(8,128)(2,1)S(1)}, u32[]{:S(2)}, u32[]{:S(2)}) collective-permute-start(bf16[24,24,128]{2,1,0:T(8,128)(2,1)S(1)} %get-tuple-element.30), channel_id=1, source_target_pairs={{0,31},{1,0},{2,1},{3,2},{4,3},{5,4},{6,5},{7,6},{8,7},{9,8},{10,9... | collective-permute-start | bytes 442376 | tf_op jit(solution)/shard_map/ppermute | solution.py:204
  119.1 21.5 %collective-permute-start.15 = (bf16[24,24,128]{2,1,0:T(8,128)(2,1)S(1)}, bf16[24,24,128]{2,1,0:T(8,128)(2,1)S(1)}, u32[]{:S(2)}, u32[]{:S(2)}) collective-permute-start(bf16[24,24,128]{2,1,0:T(8,128)(2,1)S(1)} %get-tuple-element.31), channel_id=1, source_target_pairs={{0,1},{1,2},{2,3},{3,4},{4,5},{5,6},{6,7},{7,8},{8,9},{9,10},{10,1... | collective-permute-start | bytes 442376 | tf_op jit(solution)/shard_map/ppermute | solution.py:204
  133.2 9.0 %collective-permute-start.10 = (bf16[24,24,128]{2,1,0:T(8,128)(2,1)S(1)}, bf16[24,24,128]{2,1,0:T(8,128)(2,1)S(1)}, u32[]{:S(2)}, u32[]{:S(2)}) collective-permute-start(bf16[24,24,128]{2,1,0:T(8,128)(2,1)S(1)} %get-tuple-element.32), channel_id=1, source_target_pairs={{0,31},{1,0},{2,1},{3,2},{4,3},{5,4},{6,5},{7,6},{8,7},{9,8},{10,9... | collective-permute-start | bytes 442376 | tf_op jit(solution)/shard_map/ppermute | solution.py:204
  135.1 11.1 %collective-permute-start.11 = (bf16[24,24,128]{2,1,0:T(8,128)(2,1)S(1)}, bf16[24,24,128]{2,1,0:T(8,128)(2,1)S(1)}, u32[]{:S(2)}, u32[]{:S(2)}) collective-permute-start(bf16[24,24,128]{2,1,0:T(8,128)(2,1)S(1)} %get-tuple-element.33), channel_id=1, source_target_pairs={{0,1},{1,2},{2,3},{3,4},{4,5},{5,6},{6,7},{7,8},{8,9},{9,10},{10,1... | collective-permute-start | bytes 442376 | tf_op jit(solution)/shard_map/ppermute | solution.py:204

commit v2 on v1

--- a/solution.py
+++ b/solution.py
@@ -14,9 +14,8 @@
 SR = BR + 2 * R
 NK = SR * W
 NQ = 2 * BR * T
-KR = 4
-CK = KR * W
-NC = SR // KR
+CA = SR * W // 2
+CB = SR * W
 F32 = jnp.float32
 BF = jnp.bfloat16
 NT = (((1,), (1,)), ((), ()))
@@ -34,22 +33,22 @@
     q = q_ref[0]
 
     def scores(c, m):
-        at = pl.multiple_of(base + c * CK, 32)
-        lhs = jnp.concatenate([k_ref[pl.ds(at, CK), :], aux_ref[pl.ds(at, CK), :]], axis=1)
+        at = pl.multiple_of(base + c * CA, 32)
+        lhs = jnp.concatenate([k_ref[pl.ds(at, CA), :], aux_ref[pl.ds(at, CA), :]], axis=1)
         s = lax.dot_general(lhs, q, NT, preferred_element_type=F32)
-        s_scr[pl.ds(pl.multiple_of(c * CK, 32), CK), :] = s
-        return jnp.maximum(m, jnp.max(s.reshape(CK // 8, 8, NQ), axis=0))
-
-    m = lax.fori_loop(0, NC, scores, jnp.full((8, NQ), -3e38, F32))
+        s_scr[pl.ds(pl.multiple_of(c * CA, 32), CA), :] = s
+        return jnp.maximum(m, jnp.max(s.reshape(CA // 8, 8, NQ), axis=0))
+
+    m = lax.fori_loop(0, NK // CA, scores, jnp.full((8, NQ), -3e38, F32))
     m = jnp.max(m, axis=0, keepdims=True)
 
     def expo(c, l):
-        at = pl.multiple_of(c * CK, 32)
-        p = jnp.exp(s_scr[pl.ds(at, CK), :] - m)
-        p_ref[0, pl.ds(at, CK), :] = p.astype(BF)
-        return l + jnp.sum(p.reshape(CK // 8, 8, NQ), axis=0)
-
-    l = lax.fori_loop(0, NC, expo, jnp.zeros((8, NQ), F32))
+        at = pl.multiple_of(c * CA, 32)
+        p = jnp.exp(s_scr[pl.ds(at, CA), :] - m)
+        p_ref[0, pl.ds(at, CA), :] = p.astype(BF)
+        return l + jnp.sum(p.reshape(CA // 8, 8, NQ), axis=0)
+
+    l = lax.fori_loop(0, NK // CA, expo, jnp.zeros((8, NQ), F32))
     linv = 1.0 / jnp.sum(l, axis=0, keepdims=True)
     linv_ref[0] = jnp.broadcast_to(linv, (8, NQ))
     turned = jnp.transpose(jnp.broadcast_to(linv, (128, NQ)))
@@ -57,12 +56,12 @@
     gs_ref[0] = gs
 
     def dv(c, _):
-        at = pl.multiple_of(base + c * CK, 32)
-        p = p_ref[0, pl.ds(pl.multiple_of(c * CK, 32), CK), :]
-        acc[pl.ds(at, CK), :] += jnp.dot(p, gs, preferred_element_type=F32)
+        at = pl.multiple_of(base + c * CA, 32)
+        p = p_ref[0, pl.ds(pl.multiple_of(c * CA, 32), CA), :]
+        acc[pl.ds(at, CA), :] += jnp.dot(p, gs, preferred_element_type=F32)
         return 0
 
-    lax.fori_loop(0, NC, dv, 0)
+    lax.fori_loop(0, NK // CA, dv, 0)
 
     @pl.when(b == NB - 1)
     def _():
@@ -84,12 +83,12 @@
     ot[...] = jnp.zeros_like(ot)
 
     def attend(c, _):
-        at = pl.multiple_of(base + c * CK, 32)
-        p = p_ref[0, pl.ds(pl.multiple_of(c * CK, 32), CK), :]
-        ot[...] += lax.dot_general(v_ref[pl.ds(at, CK), :], p, TN, preferred_element_type=F32)
+        at = pl.multiple_of(base + c * CB, 32)
+        p = p_ref[0, pl.ds(pl.multiple_of(c * CB, 32), CB), :]
+        ot[...] += lax.dot_general(v_ref[pl.ds(at, CB), :], p, TN, preferred_element_type=F32)
         return 0
 
-    lax.fori_loop(0, NC, attend, 0)
+    lax.fori_loop(0, NK // CB, attend, 0)
     lane = lax.broadcasted_iota(jnp.int32, (NQ // 2, 128), 1)
     o = jnp.transpose(ot[...] * linv_ref[0][:1])
     o_bf = o.astype(BF)
@@ -99,15 +98,15 @@
     ot[...] = jnp.zeros_like(ot)
 
     def back(c, _):
-        at = pl.multiple_of(base + c * CK, 32)
-        p = p_ref[0, pl.ds(pl.multiple_of(c * CK, 32), CK), :]
-        gw = lax.dot_general(v_ref[pl.ds(at, CK), :], gs, NT, preferred_element_type=F32)
+        at = pl.multiple_of(base + c * CB, 32)
+        p = p_ref[0, pl.ds(pl.multiple_of(c * CB, 32), CB), :]
+        gw = lax.dot_general(v_ref[pl.ds(at, CB), :], gs, NT, preferred_element_type=F32)
         ds = (p.astype(F32) * (gw - corr)).astype(BF)
-        acc[pl.ds(at, CK), :] += jnp.dot(ds, q, preferred_element_type=F32)
-        ot[...] += lax.dot_general(k_ref[pl.ds(at, CK), :], ds, TN, preferred_element_type=F32)
+        acc[pl.ds(at, CB), :] += jnp.dot(ds, q, preferred_element_type=F32)
+        ot[...] += lax.dot_general(k_ref[pl.ds(at, CB), :], ds, TN, preferred_element_type=F32)
         return 0
 
-    lax.fori_loop(0, NC, back, 0)
+    lax.fori_loop(0, NK // CB, back, 0)
     dq = jnp.transpose(ot[...] * 0.125)
     dq_ref[...] = jnp.where(lane < 64, dq[: NQ // 2], dq[NQ // 2 :]).astype(BF)
 
@@ -204,8 +203,11 @@
     return lax.ppermute(x, axis, pairs)
 
 
-def extend(x):
-    mid = jnp.concatenate([shift(x, "lon", 1, True), x, shift(x, "lon", -1, True)], axis=1)
+def widen(x):
+    return jnp.concatenate([shift(x, "lon", 1, True), x, shift(x, "lon", -1, True)], axis=1)
+
+
+def heighten(mid):
     north = shift(mid[T - R :], "lat", 1, False)
     south = shift(mid[:R], "lat", -1, False)
     return jnp.concatenate([north, mid, south], axis=0).reshape(ROWS * W, 128)
@@ -225,11 +227,14 @@
 
 def body(queries, keys, values, out_grad):
     height = T * lax.axis_size("lat")
-    start, aux = tables(lax.axis_index("lat") * T, height)
+    k = widen(keys)
+    v = widen(values)
+    k, first_row, queries, out_grad = lax.optimization_barrier((k, lax.axis_index("lat") * T, queries, out_grad))
+    k = heighten(k)
+    v = heighten(v)
+    start, aux = tables(first_row, height)
     q = with_marks(queries)
     g = spread(out_grad, 1.0)
-    k = extend(keys)
-    v = extend(values)
     p, linv, gs, *dv = run_a(start, k, aux, q, g)
     grad_values = fold(*dv)
     attended, grad_queries, *dk = run_b(start, k, v, q, gs, p, linv)

time: 148 us -> 113 us (0.76)
  Pallas kernels: 57.1 us -> 26.9 us
  waiting for transfers between devices: 18.3 us -> 15.1 us
    pallas_call x1, Pallas kernels: 32 us -> 13.1 us  [run_b(): pl.pallas_call(kernel_b, grid_spec=pltpu.PrefetchScalarGridSpec(num_scala...]
    pallas_call x1, Pallas kernels: 25.2 us -> 13.8 us  [run_a(): pl.pallas_call(kernel_a, grid_spec=pltpu.PrefetchScalarGridSpec(num_scala...]
    ppermute x16, waiting for transfers between devices: 18.3 us -> 15.1 us  [shift(): return lax.ppermute(x, axis, pairs)]
  transfers between devices with their start and end apart: 16 -> 16, of which waited for: 4 -> 4; matrix products, arithmetic and copies ran while one was open for 4% -> 6% of each run, Pallas kernels for 39% -> 24%
where the time goes in v2:
time: 113 us
  starting transfers between devices  62.6 us (55%)
  Pallas kernels  26.9 us (24%)
  waiting for transfers between devices  15.1 us (13%)
  other arithmetic  6.25 us (6%)
  between operations  1.14 us (1%)
    ppermute x16, starting transfers between devices, shift(): return lax.ppermute(x, axis, pairs)  62.6 us
    ppermute x16, waiting for transfers between devices, shift(): return lax.ppermute(x, axis, pairs)  15.1 us
    pallas_call x1, Pallas kernels, run_a(): pl.pallas_call(kernel_a, grid_spec=pltpu.PrefetchScalarGridSpec(num_scala...  13.8 us
    pallas_call x1, Pallas kernels, run_b(): pl.pallas_call(kernel_b, grid_spec=pltpu.PrefetchScalarGridSpec(num_scala...  13.1 us
    convert_element_type x1, other arithmetic, tables(): jnp.where(row_out | col_out, -1e+30, 0.0).astype(BF).reshape(ROWS * W, 128)  2.8 us
  transfers between devices with their start and end apart: 16, of which 4 were waited for; matrix products, arithmetic and copies ran while one was open for 6% of the time, Pallas kernels for 24%

profile of v2, /device:TPU:18, one launch (start us, length us, event | category | flops | bytes accessed | tf_op | source)
XLA Modules:
  0.0 112.8 jit_solution(13438448998454625409)
XLA Ops:
  0.6 4.0 %collective-permute-start = (bf16[24,24,128]{2,1,0:T(8,128)(2,1)}, bf16[24,24,128]{2,1,0:T(8,128)(2,1)S(1)}, u32[]{:S(2)}, u32[]{:S(2)}) collective-permute-start(bf16[24,24,128]{2,1,0:T(8,128)(2,1)} %param.5), channel_id=1, source_target_pairs={{0,1},{1,2},{2,3},{3,4},{4,5},{5,6},{6,7},{7,8},{8,9},{9,10},{10,1... | collective-permute-start | bytes 442376 | tf_op jit(solution)/shard_map/ppermute | solution.py:203
  4.7 10.9 %collective-permute-start.1 = (bf16[24,24,128]{2,1,0:T(8,128)(2,1)}, bf16[24,24,128]{2,1,0:T(8,128)(2,1)S(1)}, u32[]{:S(2)}, u32[]{:S(2)}) collective-permute-start(bf16[24,24,128]{2,1,0:T(8,128)(2,1)} %param.5), channel_id=1, source_target_pairs={{0,31},{1,0},{2,1},{3,2},{4,3},{5,4},{6,5},{7,6},{8,7},{9,8},{10,9... | collective-permute-start | bytes 442376 | tf_op jit(solution)/shard_map/ppermute | solution.py:203
  15.5 1.9 %collective-permute-start.4 = (bf16[24,24,128]{2,1,0:T(8,128)(2,1)}, bf16[24,24,128]{2,1,0:T(8,128)(2,1)S(1)}, u32[]{:S(2)}, u32[]{:S(2)}) collective-permute-start(bf16[24,24,128]{2,1,0:T(8,128)(2,1)} %param.6), channel_id=1, source_target_pairs={{0,1},{1,2},{2,3},{3,4},{4,5},{5,6},{6,7},{7,8},{8,9},{9,10},{10,1... | collective-permute-start | bytes 442376 | tf_op jit(solution)/shard_map/ppermute | solution.py:203
  17.5 7.5 %collective-permute-start.5 = (bf16[24,24,128]{2,1,0:T(8,128)(2,1)}, bf16[24,24,128]{2,1,0:T(8,128)(2,1)S(1)}, u32[]{:S(2)}, u32[]{:S(2)}) collective-permute-start(bf16[24,24,128]{2,1,0:T(8,128)(2,1)} %param.6), channel_id=1, source_target_pairs={{0,31},{1,0},{2,1},{3,2},{4,3},{5,4},{6,5},{7,6},{8,7},{9,8},{10,9... | collective-permute-start | bytes 442376 | tf_op jit(solution)/shard_map/ppermute | solution.py:203
  25.6 1.0 pad_maximum_fusion.3
  26.9 1.9 %collective-permute-start.2 = (bf16[22,72,128]{2,1,0:T(8,128)(2,1)S(1)}, bf16[22,72,128]{2,1,0:T(8,128)(2,1)S(1)}, u32[]{:S(2)}, u32[]{:S(2)}) collective-permute-start(bf16[22,72,128]{2,1,0:T(8,128)(2,1)S(1)} %get-tuple-element.44), channel_id=1, source_target_pairs={{0,32},{32,64},{64,96},{96,128},{128,160},{160,192},{192,224},{224... | collective-permute-start | bytes 1216520 | tf_op jit(solution)/shard_map/ppermute | solution.py:203
  28.8 3.6 %collective-permute-start.3 = (bf16[22,72,128]{2,1,0:T(8,128)(2,1)S(1)}, bf16[22,72,128]{2,1,0:T(8,128)(2,1)S(1)}, u32[]{:S(2)}, u32[]{:S(2)}) collective-permute-start(bf16[22,72,128]{2,1,0:T(8,128)(2,1)S(1)} %get-tuple-element.45), channel_id=1, source_target_pairs={{32,0},{64,32},{96,64},{128,96},{160,128},{192,160},{224,192},{256... | collective-permute-start | bytes 1216520 | tf_op jit(solution)/shard_map/ppermute | solution.py:203
  32.8 2.4 %collective-permute-start.6 = (bf16[22,72,128]{2,1,0:T(8,128)(2,1)S(1)}, bf16[22,72,128]{2,1,0:T(8,128)(2,1)S(1)}, u32[]{:S(2)}, u32[]{:S(2)}) collective-permute-start(bf16[22,72,128]{2,1,0:T(8,128)(2,1)S(1)} %get-tuple-element.42), channel_id=1, source_target_pairs={{0,32},{32,64},{64,96},{96,128},{128,160},{160,192},{192,224},{224... | collective-permute-start | bytes 1216520 | tf_op jit(solution)/shard_map/ppermute | solution.py:203
  35.2 3.1 %collective-permute-start.7 = (bf16[22,72,128]{2,1,0:T(8,128)(2,1)S(1)}, bf16[22,72,128]{2,1,0:T(8,128)(2,1)S(1)}, u32[]{:S(2)}, u32[]{:S(2)}) collective-permute-start(bf16[22,72,128]{2,1,0:T(8,128)(2,1)S(1)} %get-tuple-element.43), channel_id=1, source_target_pairs={{32,0},{64,32},{96,64},{128,96},{160,128},{192,160},{224,192},{256... | collective-permute-start | bytes 1216520 | tf_op jit(solution)/shard_map/ppermute | solution.py:203
  38.4 2.8 %select_convert_fusion.aux_ref = bf16[4896,128]{1,0:T(8,128)(2,1)S(1)} fusion(s32[128]{0:T(128)S(1)} %get-tuple-element.55, s32[128]{0:T(128)S(1)} %get-tuple-element.54, s32[128]{0:T(128)S(1)} %get-tuple-element.49, s32[128]{0:T(128)S(1)} %get-tuple-element.48, s32[4896]{0:T(1024)S(1)} %iota.136, s32[4896]{0:T(1024)S(1)} %iota.128, ...), kind=kLoop, calls=%fused_computation | loop fusion | flops 6893568 | bytes 1294848 | tf_op jit(solution)/shard_map/convert_element_type | solution.py:181
  42.2 13.8 %scores_and_dv.1 = (bf16[3,3744,384]{2,1,0:T(8,128)(2,1)}, f32[3,8,384]{2,1,0:T(8,128)S(1)}, bf16[3,384,128]{2,1,0:T(8,128)(2,1)S(1)}, bf16[1584,128]{1,0:T(8,12...) custom-call(s32[3]{0:T(128)S(1)} %fusion.5.start, bf16[4896,128]{1,0:T(8,128)(2,1)S(1)} %bitcast.17, ...), custom_call_target="tpu_custom_call" | custom-call | flops 6000000000 | bytes 14000000 | tf_op jit(solution)/shard_map/scores_and_dv/pallas_call | solution.py:137
  56.1 4.1 %collective-permute-start.12 = (bf16[22,72,128]{2,1,0:T(8,128)(2,1)S(1)}, bf16[22,72,128]{2,1,0:T(8,128)(2,1)S(1)}, u32[]{:S(2)}, u32[]{:S(2)}) collective-permute-start(bf16[22,72,128]{2,1,0:T(8,128)(2,1)S(1)} %bitcast.25), channel_id=1, source_target_pairs={{32,0},{64,32},{96,64},{128,96},{160,128},{192,160},{224,192},{256... | collective-permute-start | bytes 1216520 | tf_op jit(solution)/shard_map/ppermute | solution.py:203
  60.2 1.9 %collective-permute-start.13 = (bf16[22,72,128]{2,1,0:T(8,128)(2,1)S(1)}, bf16[22,72,128]{2,1,0:T(8,128)(2,1)S(1)}, u32[]{:S(2)}, u32[]{:S(2)}) collective-permute-start(bf16[22,72,128]{2,1,0:T(8,128)(2,1)S(1)} %bitcast.23), channel_id=1, source_target_pairs={{0,32},{32,64},{64,96},{96,128},{128,160},{160,192},{192,224},{224... | collective-permute-start | bytes 1216520 | tf_op jit(solution)/shard_map/ppermute | solution.py:203
  62.3 13.1 %attended_and_dk.1 = (bf16[576,128]{1,0:T(8,128)(2,1)}, bf16[576,128]{1,0:T(8,128)(2,1)}, bf16[1584,128]{1,0:T(8,128)(2,1)S(1)}, f32[1728,128]{1,0:T(8,128)S(1)}, bf16[1584,128]{1,0:T(8,128)(2,1)S(1)}) custom-call(s32[3]{0:T(128)S(1)} %fusion.5.start, bf16[4896,128]{1,0:T(8,128)(2,1)S(1)} %bitcast.18, bf16[4896,128]{1,0:T(8,128)(2,1)S(1)} %bitcast.19, ...), custom_call_target="tpu_custom_call" | custom-call | flops 8000000000 | bytes 14000000 | tf_op jit(solution)/shard_map/attended_and_dk/pallas_call | solution.py:154
  75.3 3.6 %collective-permute-start.8 = (bf16[22,72,128]{2,1,0:T(8,128)(2,1)S(1)}, bf16[22,72,128]{2,1,0:T(8,128)(2,1)S(1)}, u32[]{:S(2)}, u32[]{:S(2)}) collective-permute-start(bf16[22,72,128]{2,1,0:T(8,128)(2,1)S(1)} %bitcast.24), channel_id=1, source_target_pairs={{32,0},{64,32},{96,64},{128,96},{160,128},{192,160},{224,192},{256... | collective-permute-start | bytes 1216520 | tf_op jit(solution)/shard_map/ppermute | solution.py:203
  79.0 2.8 %collective-permute-start.9 = (bf16[22,72,128]{2,1,0:T(8,128)(2,1)S(1)}, bf16[22,72,128]{2,1,0:T(8,128)(2,1)S(1)}, u32[]{:S(2)}, u32[]{:S(2)}) collective-permute-start(bf16[22,72,128]{2,1,0:T(8,128)(2,1)S(1)} %bitcast.22), channel_id=1, source_target_pairs={{0,32},{32,64},{64,96},{96,128},{128,160},{160,192},{192,224},{224... | collective-permute-start | bytes 1216520 | tf_op jit(solution)/shard_map/ppermute | solution.py:203
  82.0 2.9 %collective-permute-start.14 = (bf16[24,24,128]{2,1,0:T(8,128)(2,1)S(1)}, bf16[24,24,128]{2,1,0:T(8,128)(2,1)S(1)}, u32[]{:S(2)}, u32[]{:S(2)}) collective-permute-start(bf16[24,24,128]{2,1,0:T(8,128)(2,1)S(1)} %get-tuple-element.38), channel_id=1, source_target_pairs={{0,31},{1,0},{2,1},{3,2},{4,3},{5,4},{6,5},{7,6},{8,7},{9,8},{10,9... | collective-permute-start | bytes 442376 | tf_op jit(solution)/shard_map/ppermute | solution.py:203
  84.9 4.4 %collective-permute-start.15 = (bf16[24,24,128]{2,1,0:T(8,128)(2,1)S(1)}, bf16[24,24,128]{2,1,0:T(8,128)(2,1)S(1)}, u32[]{:S(2)}, u32[]{:S(2)}) collective-permute-start(bf16[24,24,128]{2,1,0:T(8,128)(2,1)S(1)} %get-tuple-element.39), channel_id=1, source_target_pairs={{0,1},{1,2},{2,3},{3,4},{4,5},{5,6},{6,7},{7,8},{8,9},{9,10},{10,1... | collective-permute-start | bytes 442376 | tf_op jit(solution)/shard_map/ppermute | solution.py:203
  89.4 9.5 %collective-permute-done.9 = bf16[22,72,128]{2,1,0:T(8,128)(2,1)S(1)} collective-permute-done((bf16[22,72,128]{2,1,0:T(8,128)(2,1)S(1)}, bf16[22,72,128]{2,1,0:T(8,128)(2,1)S(1)}, u32[]{:S(2)}, u32[]{:S(2)}) %collective-permute-start.9) | collective-permute-done | bytes 405536 | tf_op jit(solution)/shard_map/ppermute | solution.py:203
  99.1 1.9 %collective-permute-start.10 = (bf16[24,24,128]{2,1,0:T(8,128)(2,1)S(1)}, bf16[24,24,128]{2,1,0:T(8,128)(2,1)S(1)}, u32[]{:S(2)}, u32[]{:S(2)}) collective-permute-start(bf16[24,24,128]{2,1,0:T(8,128)(2,1)S(1)} %get-tuple-element.40), channel_id=1, source_target_pairs={{0,31},{1,0},{2,1},{3,2},{4,3},{5,4},{6,5},{7,6},{8,7},{9,8},{10,9... | collective-permute-start | bytes 442376 | tf_op jit(solution)/shard_map/ppermute | solution.py:203
  101.0 5.4 %collective-permute-start.11 = (bf16[24,24,128]{2,1,0:T(8,128)(2,1)S(1)}, bf16[24,24,128]{2,1,0:T(8,128)(2,1)S(1)}, u32[]{:S(2)}, u32[]{:S(2)}) collective-permute-start(bf16[24,24,128]{2,1,0:T(8,128)(2,1)S(1)} %get-tuple-element.41), channel_id=1, source_target_pairs={{0,1},{1,2},{2,3},{3,4},{4,5},{5,6},{6,7},{7,8},{8,9},{9,10},{10,1... | collective-permute-start | bytes 442376 | tf_op jit(solution)/shard_map/ppermute | solution.py:203
  107.2 0.9 collective-permute-done.10
  108.1 4.0 %collective-permute-done.11 = bf16[24,24,128]{2,1,0:T(8,128)(2,1)S(1)} collective-permute-done((bf16[24,24,128]{2,1,0:T(8,128)(2,1)S(1)}, bf16[24,24,128]{2,1,0:T(8,128)(2,1)S(1)}, u32[]{:S(2)}, u32[]{:S(2)}) %collective-permute-start.11) | collective-permute-done | bytes 147488 | tf_op jit(solution)/shard_map/ppermute | solution.py:203
  112.1 0.7 fusion.4
  (54 shorter events, 3.3 us)
Async XLA Ops:
  0.6 25.0 %collective-permute-start = (bf16[24,24,128]{2,1,0:T(8,128)(2,1)}, bf16[24,24,128]{2,1,0:T(8,128)(2,1)S(1)}, u32[]{:S(2)}, u32[]{:S(2)}) collective-permute-start(bf16[24,24,128]{2,1,0:T(8,128)(2,1)} %param.5), channel_id=1, source_target_pairs={{0,1},{1,2},{2,3},{3,4},{4,5},{5,6},{6,7},{7,8},{8,9},{9,10},{10,1... | collective-permute-start | bytes 442376 | tf_op jit(solution)/shard_map/ppermute | solution.py:203
  4.7 20.9 %collective-permute-start.1 = (bf16[24,24,128]{2,1,0:T(8,128)(2,1)}, bf16[24,24,128]{2,1,0:T(8,128)(2,1)S(1)}, u32[]{:S(2)}, u32[]{:S(2)}) collective-permute-start(bf16[24,24,128]{2,1,0:T(8,128)(2,1)} %param.5), channel_id=1, source_target_pairs={{0,31},{1,0},{2,1},{3,2},{4,3},{5,4},{6,5},{7,6},{8,7},{9,8},{10,9... | collective-permute-start | bytes 442376 | tf_op jit(solution)/shard_map/ppermute | solution.py:203
  15.5 17.0 %collective-permute-start.4 = (bf16[24,24,128]{2,1,0:T(8,128)(2,1)}, bf16[24,24,128]{2,1,0:T(8,128)(2,1)S(1)}, u32[]{:S(2)}, u32[]{:S(2)}) collective-permute-start(bf16[24,24,128]{2,1,0:T(8,128)(2,1)} %param.6), channel_id=1, source_target_pairs={{0,1},{1,2},{2,3},{3,4},{4,5},{5,6},{6,7},{7,8},{8,9},{9,10},{10,1... | collective-permute-start | bytes 442376 | tf_op jit(solution)/shard_map/ppermute | solution.py:203
  17.5 15.1 %collective-permute-start.5 = (bf16[24,24,128]{2,1,0:T(8,128)(2,1)}, bf16[24,24,128]{2,1,0:T(8,128)(2,1)S(1)}, u32[]{:S(2)}, u32[]{:S(2)}) collective-permute-start(bf16[24,24,128]{2,1,0:T(8,128)(2,1)} %param.6), channel_id=1, source_target_pairs={{0,31},{1,0},{2,1},{3,2},{4,3},{5,4},{6,5},{7,6},{8,7},{9,8},{10,9... | collective-permute-start | bytes 442376 | tf_op jit(solution)/shard_map/ppermute | solution.py:203
  25.6 7.0 %copy-start.1 = (bf16[24,24,128]{2,1,0:T(8,128)(2,1)S(1)}, bf16[24,24,128]{2,1,0:T(8,128)(2,1)}, u32[]{:S(2)}) copy-start(bf16[24,24,128]{2,1,0:T(8,128)(2,1)} %param.6) | copy-start | bytes 442372
  26.9 14.5 %collective-permute-start.2 = (bf16[22,72,128]{2,1,0:T(8,128)(2,1)S(1)}, bf16[22,72,128]{2,1,0:T(8,128)(2,1)S(1)}, u32[]{:S(2)}, u32[]{:S(2)}) collective-permute-start(bf16[22,72,128]{2,1,0:T(8,128)(2,1)S(1)} %get-tuple-element.44), channel_id=1, source_target_pairs={{0,32},{32,64},{64,96},{96,128},{128,160},{160,192},{192,224},{224... | collective-permute-start | bytes 1216520 | tf_op jit(solution)/shard_map/ppermute | solution.py:203
  28.8 13.2 %collective-permute-start.3 = (bf16[22,72,128]{2,1,0:T(8,128)(2,1)S(1)}, bf16[22,72,128]{2,1,0:T(8,128)(2,1)S(1)}, u32[]{:S(2)}, u32[]{:S(2)}) collective-permute-start(bf16[22,72,128]{2,1,0:T(8,128)(2,1)S(1)} %get-tuple-element.45), channel_id=1, source_target_pairs={{32,0},{64,32},{96,64},{128,96},{160,128},{192,160},{224,192},{256... | collective-permute-start | bytes 1216520 | tf_op jit(solution)/shard_map/ppermute | solution.py:203
  32.6 8.5 %copy-start.2 = (bf16[24,24,128]{2,1,0:T(8,128)(2,1)S(1)}, bf16[24,24,128]{2,1,0:T(8,128)(2,1)}, u32[]{:S(2)}) copy-start(bf16[24,24,128]{2,1,0:T(8,128)(2,1)} %param.4) | copy-start | bytes 442372
  32.7 8.6 %copy-start = (bf16[24,24,128]{2,1,0:T(8,128)(2,1)S(1)}, bf16[24,24,128]{2,1,0:T(8,128)(2,1)}, u32[]{:S(2)}) copy-start(bf16[24,24,128]{2,1,0:T(8,128)(2,1)} %param.7) | copy-start | bytes 442372
  32.8 29.3 %collective-permute-start.6 = (bf16[22,72,128]{2,1,0:T(8,128)(2,1)S(1)}, bf16[22,72,128]{2,1,0:T(8,128)(2,1)S(1)}, u32[]{:S(2)}, u32[]{:S(2)}) collective-permute-start(bf16[22,72,128]{2,1,0:T(8,128)(2,1)S(1)} %get-tuple-element.42), channel_id=1, source_target_pairs={{0,32},{32,64},{64,96},{96,128},{128,160},{160,192},{192,224},{224... | collective-permute-start | bytes 1216520 | tf_op jit(solution)/shard_map/ppermute | solution.py:203
  35.2 26.9 %collective-permute-start.7 = (bf16[22,72,128]{2,1,0:T(8,128)(2,1)S(1)}, bf16[22,72,128]{2,1,0:T(8,128)(2,1)S(1)}, u32[]{:S(2)}, u32[]{:S(2)}) collective-permute-start(bf16[22,72,128]{2,1,0:T(8,128)(2,1)S(1)} %get-tuple-element.43), channel_id=1, source_target_pairs={{32,0},{64,32},{96,64},{128,96},{160,128},{192,160},{224,192},{256... | collective-permute-start | bytes 1216520 | tf_op jit(solution)/shard_map/ppermute | solution.py:203
  56.1 25.7 %collective-permute-start.12 = (bf16[22,72,128]{2,1,0:T(8,128)(2,1)S(1)}, bf16[22,72,128]{2,1,0:T(8,128)(2,1)S(1)}, u32[]{:S(2)}, u32[]{:S(2)}) collective-permute-start(bf16[22,72,128]{2,1,0:T(8,128)(2,1)S(1)} %bitcast.25), channel_id=1, source_target_pairs={{32,0},{64,32},{96,64},{128,96},{160,128},{192,160},{224,192},{256... | collective-permute-start | bytes 1216520 | tf_op jit(solution)/shard_map/ppermute | solution.py:203
  60.2 21.6 %collective-permute-start.13 = (bf16[22,72,128]{2,1,0:T(8,128)(2,1)S(1)}, bf16[22,72,128]{2,1,0:T(8,128)(2,1)S(1)}, u32[]{:S(2)}, u32[]{:S(2)}) collective-permute-start(bf16[22,72,128]{2,1,0:T(8,128)(2,1)S(1)} %bitcast.23), channel_id=1, source_target_pairs={{0,32},{32,64},{64,96},{96,128},{128,160},{160,192},{192,224},{224... | collective-permute-start | bytes 1216520 | tf_op jit(solution)/shard_map/ppermute | solution.py:203
  75.3 14.0 %collective-permute-start.8 = (bf16[22,72,128]{2,1,0:T(8,128)(2,1)S(1)}, bf16[22,72,128]{2,1,0:T(8,128)(2,1)S(1)}, u32[]{:S(2)}, u32[]{:S(2)}) collective-permute-start(bf16[22,72,128]{2,1,0:T(8,128)(2,1)S(1)} %bitcast.24), channel_id=1, source_target_pairs={{32,0},{64,32},{96,64},{128,96},{160,128},{192,160},{224,192},{256... | collective-permute-start | bytes 1216520 | tf_op jit(solution)/shard_map/ppermute | solution.py:203
  79.0 19.9 %collective-permute-start.9 = (bf16[22,72,128]{2,1,0:T(8,128)(2,1)S(1)}, bf16[22,72,128]{2,1,0:T(8,128)(2,1)S(1)}, u32[]{:S(2)}, u32[]{:S(2)}) collective-permute-start(bf16[22,72,128]{2,1,0:T(8,128)(2,1)S(1)} %bitcast.22), channel_id=1, source_target_pairs={{0,32},{32,64},{64,96},{96,128},{128,160},{160,192},{192,224},{224... | collective-permute-start | bytes 1216520 | tf_op jit(solution)/shard_map/ppermute | solution.py:203
  82.0 24.4 %collective-permute-start.14 = (bf16[24,24,128]{2,1,0:T(8,128)(2,1)S(1)}, bf16[24,24,128]{2,1,0:T(8,128)(2,1)S(1)}, u32[]{:S(2)}, u32[]{:S(2)}) collective-permute-start(bf16[24,24,128]{2,1,0:T(8,128)(2,1)S(1)} %get-tuple-element.38), channel_id=1, source_target_pairs={{0,31},{1,0},{2,1},{3,2},{4,3},{5,4},{6,5},{7,6},{8,7},{9,8},{10,9... | collective-permute-start | bytes 442376 | tf_op jit(solution)/shard_map/ppermute | solution.py:203
  84.9 21.5 %collective-permute-start.15 = (bf16[24,24,128]{2,1,0:T(8,128)(2,1)S(1)}, bf16[24,24,128]{2,1,0:T(8,128)(2,1)S(1)}, u32[]{:S(2)}, u32[]{:S(2)}) collective-permute-start(bf16[24,24,128]{2,1,0:T(8,128)(2,1)S(1)} %get-tuple-element.39), channel_id=1, source_target_pairs={{0,1},{1,2},{2,3},{3,4},{4,5},{5,6},{6,7},{7,8},{8,9},{9,10},{10,1... | collective-permute-start | bytes 442376 | tf_op jit(solution)/shard_map/ppermute | solution.py:203
  99.1 9.0 %collective-permute-start.10 = (bf16[24,24,128]{2,1,0:T(8,128)(2,1)S(1)}, bf16[24,24,128]{2,1,0:T(8,128)(2,1)S(1)}, u32[]{:S(2)}, u32[]{:S(2)}) collective-permute-start(bf16[24,24,128]{2,1,0:T(8,128)(2,1)S(1)} %get-tuple-element.40), channel_id=1, source_target_pairs={{0,31},{1,0},{2,1},{3,2},{4,3},{5,4},{6,5},{7,6},{8,7},{9,8},{10,9... | collective-permute-start | bytes 442376 | tf_op jit(solution)/shard_map/ppermute | solution.py:203
  101.0 11.1 %collective-permute-start.11 = (bf16[24,24,128]{2,1,0:T(8,128)(2,1)S(1)}, bf16[24,24,128]{2,1,0:T(8,128)(2,1)S(1)}, u32[]{:S(2)}, u32[]{:S(2)}) collective-permute-start(bf16[24,24,128]{2,1,0:T(8,128)(2,1)S(1)} %get-tuple-element.41), channel_id=1, source_target_pairs={{0,1},{1,2},{2,3},{3,4},{4,5},{5,6},{6,7},{7,8},{8,9},{9,10},{10,1... | collective-permute-start | bytes 442376 | tf_op jit(solution)/shard_map/ppermute | solution.py:203

commit v3 on v2

--- a/solution.py
+++ b/solution.py
@@ -22,48 +22,78 @@
 TN = (((0,), (0,)), ((), ()))
 
 
-def kernel_a(start, k_ref, aux_ref, q_ref, g_ref, p_ref, linv_ref, gs_ref, vn_ref, vm_ref, vs_ref, s_scr, acc):
+def kernel_a(start, k_ref, aux_ref, q_ref, g_ref, p_ref, linv_ref, gs_ref, vn_ref, vm_ref, vs_ref, s_scr, m_scr, acc):
     b = pl.program_id(0)
-    base = pl.multiple_of(start[b] * W, 64)
+    here = lax.rem(b, 2)
+    prior = jnp.maximum(b - 1, 0)
+    base = pl.multiple_of(start[jnp.minimum(b, NB - 1)] * W, 64)
+    prior_base = pl.multiple_of(start[prior] * W, 64)
+
+    def rows(c, n=CA):
+        return pl.ds(pl.multiple_of(c * n, 16), n)
+
+    def scores(c, m, n=CA):
+        at = pl.multiple_of(base + c * n, 16)
+        lhs = jnp.concatenate([k_ref[pl.ds(at, n), :], aux_ref[pl.ds(at, n), :]], axis=1)
+        s = lax.dot_general(lhs, q_ref[0], NT, preferred_element_type=F32)
+        s_scr[here, rows(c, n), :] = s
+        return jnp.maximum(m, jnp.max(s.reshape(n // 8, 8, NQ), axis=0))
+
+    def expo(c, m, l, n=CA):
+        p = jnp.exp(s_scr[1 - here, rows(c, n), :] - m)
+        p_ref[0, rows(c, n), :] = p.astype(BF)
+        return l + jnp.sum(p.reshape(n // 8, 8, NQ), axis=0)
+
+    def close(m):
+        m_scr[...] = jnp.broadcast_to(jnp.max(m, axis=0, keepdims=True), (8, NQ))
+
+    c_parts = 13
+    low = jnp.full((8, NQ), -3e38, F32)
+    zero = jnp.zeros((8, NQ), F32)
+
+    def finish(l):
+        linv = 1.0 / jnp.sum(l, axis=0, keepdims=True)
+        linv_ref[0] = jnp.broadcast_to(linv, (8, NQ))
+        turned = jnp.transpose(jnp.broadcast_to(linv, (128, NQ)))
+        gs_ref[0] = (g_ref[0].astype(F32) * turned).astype(BF)
 
     @pl.when(b == 0)
     def _():
         acc[...] = jnp.zeros_like(acc)
-
-    q = q_ref[0]
-
-    def scores(c, m):
-        at = pl.multiple_of(base + c * CA, 32)
-        lhs = jnp.concatenate([k_ref[pl.ds(at, CA), :], aux_ref[pl.ds(at, CA), :]], axis=1)
-        s = lax.dot_general(lhs, q, NT, preferred_element_type=F32)
-        s_scr[pl.ds(pl.multiple_of(c * CA, 32), CA), :] = s
-        return jnp.maximum(m, jnp.max(s.reshape(CA // 8, 8, NQ), axis=0))
-
-    m = lax.fori_loop(0, NK // CA, scores, jnp.full((8, NQ), -3e38, F32))
-    m = jnp.max(m, axis=0, keepdims=True)
-
-    def expo(c, l):
-        at = pl.multiple_of(c * CA, 32)
-        p = jnp.exp(s_scr[pl.ds(at, CA), :] - m)
-        p_ref[0, pl.ds(at, CA), :] = p.astype(BF)
-        return l + jnp.sum(p.reshape(CA // 8, 8, NQ), axis=0)
-
-    l = lax.fori_loop(0, NK // CA, expo, jnp.zeros((8, NQ), F32))
-    linv = 1.0 / jnp.sum(l, axis=0, keepdims=True)
-    linv_ref[0] = jnp.broadcast_to(linv, (8, NQ))
-    turned = jnp.transpose(jnp.broadcast_to(linv, (128, NQ)))
-    gs = (g_ref[0].astype(F32) * turned).astype(BF)
-    gs_ref[0] = gs
-
-    def dv(c, _):
-        at = pl.multiple_of(base + c * CA, 32)
-        p = p_ref[0, pl.ds(pl.multiple_of(c * CA, 32), CA), :]
-        acc[pl.ds(at, CA), :] += jnp.dot(p, gs, preferred_element_type=F32)
-        return 0
-
-    lax.fori_loop(0, NK // CA, dv, 0)
-
-    @pl.when(b == NB - 1)
+        close(lax.fori_loop(0, NK // CA, scores, low))
+
+    @pl.when((b > 0) & (b < NB))
+    def _():
+        m = m_scr[:1]
+
+        def both(c, carry):
+            fresh, l = carry
+            for part in range(c_parts):
+                fresh = scores(c * c_parts + part, fresh, CA // c_parts)
+                l = expo(c * c_parts + part, m, l, CA // c_parts)
+            return fresh, l
+
+        fresh, l = lax.fori_loop(0, NK // CA, both, (low, zero))
+        close(fresh)
+        finish(l)
+
+    @pl.when(b == NB)
+    def _():
+        m = m_scr[:1]
+        finish(lax.fori_loop(0, NK // CA, lambda c, l: expo(c, m, l), zero))
+
+    @pl.when(b > 0)
+    def _():
+        gs = gs_ref[0]
+
+        def dv(c, _):
+            at = pl.multiple_of(prior_base + c * CA, 16)
+            acc[pl.ds(at, CA), :] += jnp.dot(p_ref[0, rows(c), :], gs, preferred_element_type=F32)
+            return 0
+
+        lax.fori_loop(0, NK // CA, dv, 0)
+
+    @pl.when(b == NB)
     def _():
         vn_ref[...] = acc[: R * W, :].astype(BF)
         vm_ref[...] = acc[R * W : (R + T) * W, :]
@@ -134,14 +164,20 @@
 
 
 def run_a(start, k, aux, q, g):
+    def ahead(shape):
+        return pl.BlockSpec((1,) + shape, lambda b, s: (jnp.minimum(b, NB - 1),) + (0,) * len(shape))
+
+    def behind(shape):
+        return pl.BlockSpec((1,) + shape, lambda b, s: (jnp.maximum(b - 1, 0),) + (0,) * len(shape))
+
     return pl.pallas_call(
         kernel_a,
         grid_spec=pltpu.PrefetchScalarGridSpec(
             num_scalar_prefetch=1,
-            grid=(NB,),
-            in_specs=[whole((ROWS * W, 128)), whole((ROWS * W, 128)), per_block((NQ, 256)), per_block((NQ, 128))],
-            out_specs=[per_block((NK, NQ)), per_block((8, NQ)), per_block((NQ, 128))] + grads_spec,
-            scratch_shapes=[pltpu.VMEM((NK, NQ), F32), pltpu.VMEM((ROWS * W, 128), F32)],
+            grid=(NB + 1,),
+            in_specs=[whole((ROWS * W, 128)), whole((ROWS * W, 128)), ahead((NQ, 256)), behind((NQ, 128))],
+            out_specs=[behind((NK, NQ)), behind((8, NQ)), behind((NQ, 128))] + grads_spec,
+            scratch_shapes=[pltpu.VMEM((2, NK, NQ), F32), pltpu.VMEM((8, NQ), F32), pltpu.VMEM((ROWS * W, 128), F32)],
         ),
         out_shape=[sds((NB, NK, NQ), BF), sds((NB, 8, NQ), F32), sds((NB, NQ, 128), BF)] + grads_shape,
         compiler_params=pltpu.CompilerParams(vmem_limit_bytes=48 << 20),
@@ -228,9 +264,11 @@
 def body(queries, keys, values, out_grad):
     height = T * lax.axis_size("lat")
     k = widen(keys)
+    k, values, first_row, queries, out_grad = lax.optimization_barrier(
+        (k, values, lax.axis_index("lat") * T, queries, out_grad)
+    )
+    k = heighten(k)
     v = widen(values)
-    k, first_row, queries, out_grad = lax.optimization_barrier((k, lax.axis_index("lat") * T, queries, out_grad))
-    k = heighten(k)
     v = heighten(v)
     start, aux = tables(first_row, height)
     q = with_marks(queries)

time: 113 us -> 114 us (level)
  the two profiles are of different devices: /device:TPU:18 before, /device:TPU:10 now
where the time goes in v3:
time: 114 us
  starting transfers between devices  62.6 us (55%)
  Pallas kernels  26.4 us (23%)
  waiting for transfers between devices  16.7 us (15%)
  other arithmetic  6.21 us (5%)
    ppermute x16, starting transfers between devices, shift(): return lax.ppermute(x, axis, pairs)  62.6 us
    ppermute x16, waiting for transfers between devices, shift(): return lax.ppermute(x, axis, pairs)  16.7 us
    pallas_call x1, Pallas kernels, run_a(): pl.pallas_call(kernel_a, grid_spec=pltpu.PrefetchScalarGridSpec(num_scala...  13.4 us
    pallas_call x1, Pallas kernels, run_b(): pl.pallas_call(kernel_b, grid_spec=pltpu.PrefetchScalarGridSpec(num_scala...  13.1 us
    convert_element_type x1, other arithmetic, tables(): jnp.where(row_out | col_out, -1e+30, 0.0).astype(BF).reshape(ROWS * W, 128)  2.8 us
  transfers between devices with their start and end apart: 16, of which 5 were waited for; matrix products, arithmetic and copies ran while one was open for 5% of the time, Pallas kernels for 23%

profile of v3, /device:TPU:10, one launch (start us, length us, event | category | flops | bytes accessed | tf_op | source)
XLA Modules:
  0.0 113.9 jit_solution(17897063609080223296)
XLA Ops:
  0.6 4.2 %collective-permute-start = (bf16[24,24,128]{2,1,0:T(8,128)(2,1)}, bf16[24,24,128]{2,1,0:T(8,128)(2,1)S(1)}, u32[]{:S(2)}, u32[]{:S(2)}) collective-permute-start(bf16[24,24,128]{2,1,0:T(8,128)(2,1)} %param.5), channel_id=1, source_target_pairs={{0,1},{1,2},{2,3},{3,4},{4,5},{5,6},{6,7},{7,8},{8,9},{9,10},{10,1... | collective-permute-start | bytes 442376 | tf_op jit(solution)/shard_map/ppermute | solution.py:239
  4.8 10.9 %collective-permute-start.1 = (bf16[24,24,128]{2,1,0:T(8,128)(2,1)}, bf16[24,24,128]{2,1,0:T(8,128)(2,1)S(1)}, u32[]{:S(2)}, u32[]{:S(2)}) collective-permute-start(bf16[24,24,128]{2,1,0:T(8,128)(2,1)} %param.5), channel_id=1, source_target_pairs={{0,31},{1,0},{2,1},{3,2},{4,3},{5,4},{6,5},{7,6},{8,7},{9,8},{10,9... | collective-permute-start | bytes 442376 | tf_op jit(solution)/shard_map/ppermute | solution.py:239
  16.3 1.5 %collective-permute-done = bf16[24,24,128]{2,1,0:T(8,128)(2,1)S(1)} collective-permute-done((bf16[24,24,128]{2,1,0:T(8,128)(2,1)}, bf16[24,24,128]{2,1,0:T(8,128)(2,1)S(1)}, u32[]{:S(2)}, u32[]{:S(2)}) %collective-permute-start) | collective-permute-done | bytes 147488 | tf_op jit(solution)/shard_map/ppermute | solution.py:239
  17.8 1.3 %collective-permute-done.1 = bf16[24,24,128]{2,1,0:T(8,128)(2,1)S(1)} collective-permute-done((bf16[24,24,128]{2,1,0:T(8,128)(2,1)}, bf16[24,24,128]{2,1,0:T(8,128)(2,1)S(1)}, u32[]{:S(2)}, u32[]{:S(2)}) %collective-permute-start.1) | collective-permute-done | bytes 147488 | tf_op jit(solution)/shard_map/ppermute | solution.py:239
  20.1 1.9 %collective-permute-start.4 = (bf16[24,24,128]{2,1,0:T(8,128)(2,1)S(1)}, bf16[24,24,128]{2,1,0:T(8,128)(2,1)S(1)}, u32[]{:S(2)}, u32[]{:S(2)}) collective-permute-start(bf16[24,24,128]{2,1,0:T(8,128)(2,1)S(1)} %copy-done.2), channel_id=1, source_target_pairs={{0,1},{1,2},{2,3},{3,4},{4,5},{5,6},{6,7},{7,8},{8,9},{9,10},{10,1... | collective-permute-start | bytes 442376 | tf_op jit(solution)/shard_map/ppermute | solution.py:239
  22.0 7.9 %collective-permute-start.5 = (bf16[24,24,128]{2,1,0:T(8,128)(2,1)S(1)}, bf16[24,24,128]{2,1,0:T(8,128)(2,1)S(1)}, u32[]{:S(2)}, u32[]{:S(2)}) collective-permute-start(bf16[24,24,128]{2,1,0:T(8,128)(2,1)S(1)} %copy-done.2), channel_id=1, source_target_pairs={{0,31},{1,0},{2,1},{3,2},{4,3},{5,4},{6,5},{7,6},{8,7},{9,8},{10,9... | collective-permute-start | bytes 442376 | tf_op jit(solution)/shard_map/ppermute | solution.py:239
  30.2 1.9 %collective-permute-start.2 = (bf16[22,72,128]{2,1,0:T(8,128)(2,1)S(1)}, bf16[22,72,128]{2,1,0:T(8,128)(2,1)S(1)}, u32[]{:S(2)}, u32[]{:S(2)}) collective-permute-start(bf16[22,72,128]{2,1,0:T(8,128)(2,1)S(1)} %get-tuple-element.46), channel_id=1, source_target_pairs={{0,32},{32,64},{64,96},{96,128},{128,160},{160,192},{192,224},{224... | collective-permute-start | bytes 1216520 | tf_op jit(solution)/shard_map/ppermute | solution.py:239
  32.2 3.6 %collective-permute-start.3 = (bf16[22,72,128]{2,1,0:T(8,128)(2,1)S(1)}, bf16[22,72,128]{2,1,0:T(8,128)(2,1)S(1)}, u32[]{:S(2)}, u32[]{:S(2)}) collective-permute-start(bf16[22,72,128]{2,1,0:T(8,128)(2,1)S(1)} %get-tuple-element.47), channel_id=1, source_target_pairs={{32,0},{64,32},{96,64},{128,96},{160,128},{192,160},{224,192},{256... | collective-permute-start | bytes 1216520 | tf_op jit(solution)/shard_map/ppermute | solution.py:239
  35.8 2.8 %select_convert_fusion.aux_ref = bf16[4896,128]{1,0:T(8,128)(2,1)S(1)} fusion(s32[128]{0:T(128)S(1)} %get-tuple-element.57, s32[128]{0:T(128)S(1)} %get-tuple-element.56, s32[128]{0:T(128)S(1)} %get-tuple-element.51, s32[128]{0:T(128)S(1)} %get-tuple-element.50, s32[4896]{0:T(1024)S(1)} %iota.136, s32[4896]{0:T(1024)S(1)} %iota.128, ...), kind=kLoop, calls=%fused_computation | loop fusion | flops 6893568 | bytes 1294848 | tf_op jit(solution)/shard_map/convert_element_type | solution.py:217
  39.1 2.7 %collective-permute-start.6 = (bf16[22,72,128]{2,1,0:T(8,128)(2,1)S(1)}, bf16[22,72,128]{2,1,0:T(8,128)(2,1)S(1)}, u32[]{:S(2)}, u32[]{:S(2)}) collective-permute-start(bf16[22,72,128]{2,1,0:T(8,128)(2,1)S(1)} %get-tuple-element.44), channel_id=1, source_target_pairs={{0,32},{32,64},{64,96},{96,128},{128,160},{160,192},{192,224},{224... | collective-permute-start | bytes 1216520 | tf_op jit(solution)/shard_map/ppermute | solution.py:239
  41.8 2.8 %collective-permute-start.7 = (bf16[22,72,128]{2,1,0:T(8,128)(2,1)S(1)}, bf16[22,72,128]{2,1,0:T(8,128)(2,1)S(1)}, u32[]{:S(2)}, u32[]{:S(2)}) collective-permute-start(bf16[22,72,128]{2,1,0:T(8,128)(2,1)S(1)} %get-tuple-element.45), channel_id=1, source_target_pairs={{32,0},{64,32},{96,64},{128,96},{160,128},{192,160},{224,192},{256... | collective-permute-start | bytes 1216520 | tf_op jit(solution)/shard_map/ppermute | solution.py:239
  44.8 13.4 %scores_and_dv.1 = (bf16[3,3744,384]{2,1,0:T(8,128)(2,1)}, f32[3,8,384]{2,1,0:T(8,128)S(1)}, bf16[3,384,128]{2,1,0:T(8,128)(2,1)S(1)}, bf16[1584,128]{1,0:T(8,12...) custom-call(s32[3]{0:T(128)S(1)} %fusion.5.start, bf16[4896,128]{1,0:T(8,128)(2,1)S(1)} %bitcast.17, ...), custom_call_target="tpu_custom_call" | custom-call | flops 6000000000 | bytes 14000000 | tf_op jit(solution)/shard_map/scores_and_dv/pallas_call | solution.py:173
  58.2 2.9 %collective-permute-start.12 = (bf16[22,72,128]{2,1,0:T(8,128)(2,1)S(1)}, bf16[22,72,128]{2,1,0:T(8,128)(2,1)S(1)}, u32[]{:S(2)}, u32[]{:S(2)}) collective-permute-start(bf16[22,72,128]{2,1,0:T(8,128)(2,1)S(1)} %bitcast.25), channel_id=1, source_target_pairs={{32,0},{64,32},{96,64},{128,96},{160,128},{192,160},{224,192},{256... | collective-permute-start | bytes 1216520 | tf_op jit(solution)/shard_map/ppermute | solution.py:239
  61.1 2.6 %collective-permute-start.13 = (bf16[22,72,128]{2,1,0:T(8,128)(2,1)S(1)}, bf16[22,72,128]{2,1,0:T(8,128)(2,1)S(1)}, u32[]{:S(2)}, u32[]{:S(2)}) collective-permute-start(bf16[22,72,128]{2,1,0:T(8,128)(2,1)S(1)} %bitcast.23), channel_id=1, source_target_pairs={{0,32},{32,64},{64,96},{96,128},{128,160},{160,192},{192,224},{224... | collective-permute-start | bytes 1216520 | tf_op jit(solution)/shard_map/ppermute | solution.py:239
  63.9 13.1 %attended_and_dk.1 = (bf16[576,128]{1,0:T(8,128)(2,1)}, bf16[576,128]{1,0:T(8,128)(2,1)}, bf16[1584,128]{1,0:T(8,128)(2,1)S(1)}, f32[1728,128]{1,0:T(8,128)S(1)}, bf16[1584,128]{1,0:T(8,128)(2,1)S(1)}) custom-call(s32[3]{0:T(128)S(1)} %fusion.5.start, bf16[4896,128]{1,0:T(8,128)(2,1)S(1)} %bitcast.18, bf16[4896,128]{1,0:T(8,128)(2,1)S(1)} %bitcast.19, ...), custom_call_target="tpu_custom_call" | custom-call | flops 8000000000 | bytes 14000000 | tf_op jit(solution)/shard_map/attended_and_dk/pallas_call | solution.py:190
  77.0 3.5 %collective-permute-start.8 = (bf16[22,72,128]{2,1,0:T(8,128)(2,1)S(1)}, bf16[22,72,128]{2,1,0:T(8,128)(2,1)S(1)}, u32[]{:S(2)}, u32[]{:S(2)}) collective-permute-start(bf16[22,72,128]{2,1,0:T(8,128)(2,1)S(1)} %bitcast.24), channel_id=1, source_target_pairs={{32,0},{64,32},{96,64},{128,96},{160,128},{192,160},{224,192},{256... | collective-permute-start | bytes 1216520 | tf_op jit(solution)/shard_map/ppermute | solution.py:239
  80.5 2.9 %collective-permute-start.9 = (bf16[22,72,128]{2,1,0:T(8,128)(2,1)S(1)}, bf16[22,72,128]{2,1,0:T(8,128)(2,1)S(1)}, u32[]{:S(2)}, u32[]{:S(2)}) collective-permute-start(bf16[22,72,128]{2,1,0:T(8,128)(2,1)S(1)} %bitcast.22), channel_id=1, source_target_pairs={{0,32},{32,64},{64,96},{96,128},{128,160},{160,192},{192,224},{224... | collective-permute-start | bytes 1216520 | tf_op jit(solution)/shard_map/ppermute | solution.py:239
  83.7 4.8 %collective-permute-start.14 = (bf16[24,24,128]{2,1,0:T(8,128)(2,1)S(1)}, bf16[24,24,128]{2,1,0:T(8,128)(2,1)S(1)}, u32[]{:S(2)}, u32[]{:S(2)}) collective-permute-start(bf16[24,24,128]{2,1,0:T(8,128)(2,1)S(1)} %get-tuple-element.40), channel_id=1, source_target_pairs={{0,31},{1,0},{2,1},{3,2},{4,3},{5,4},{6,5},{7,6},{8,7},{9,8},{10,9... | collective-permute-start | bytes 442376 | tf_op jit(solution)/shard_map/ppermute | solution.py:239
  88.5 2.5 %collective-permute-start.15 = (bf16[24,24,128]{2,1,0:T(8,128)(2,1)S(1)}, bf16[24,24,128]{2,1,0:T(8,128)(2,1)S(1)}, u32[]{:S(2)}, u32[]{:S(2)}) collective-permute-start(bf16[24,24,128]{2,1,0:T(8,128)(2,1)S(1)} %get-tuple-element.41), channel_id=1, source_target_pairs={{0,1},{1,2},{2,3},{3,4},{4,5},{5,6},{6,7},{7,8},{8,9},{9,10},{10,1... | collective-permute-start | bytes 442376 | tf_op jit(solution)/shard_map/ppermute | solution.py:239
  91.0 9.3 %collective-permute-done.9 = bf16[22,72,128]{2,1,0:T(8,128)(2,1)S(1)} collective-permute-done((bf16[22,72,128]{2,1,0:T(8,128)(2,1)S(1)}, bf16[22,72,128]{2,1,0:T(8,128)(2,1)S(1)}, u32[]{:S(2)}, u32[]{:S(2)}) %collective-permute-start.9) | collective-permute-done | bytes 405536 | tf_op jit(solution)/shard_map/ppermute | solution.py:239
  100.6 1.9 %collective-permute-start.10 = (bf16[24,24,128]{2,1,0:T(8,128)(2,1)S(1)}, bf16[24,24,128]{2,1,0:T(8,128)(2,1)S(1)}, u32[]{:S(2)}, u32[]{:S(2)}) collective-permute-start(bf16[24,24,128]{2,1,0:T(8,128)(2,1)S(1)} %get-tuple-element.42), channel_id=1, source_target_pairs={{0,31},{1,0},{2,1},{3,2},{4,3},{5,4},{6,5},{7,6},{8,7},{9,8},{10,9... | collective-permute-start | bytes 442376 | tf_op jit(solution)/shard_map/ppermute | solution.py:239
  102.5 5.4 %collective-permute-start.11 = (bf16[24,24,128]{2,1,0:T(8,128)(2,1)S(1)}, bf16[24,24,128]{2,1,0:T(8,128)(2,1)S(1)}, u32[]{:S(2)}, u32[]{:S(2)}) collective-permute-start(bf16[24,24,128]{2,1,0:T(8,128)(2,1)S(1)} %get-tuple-element.43), channel_id=1, source_target_pairs={{0,1},{1,2},{2,3},{3,4},{4,5},{5,6},{6,7},{7,8},{8,9},{9,10},{10,1... | collective-permute-start | bytes 442376 | tf_op jit(solution)/shard_map/ppermute | solution.py:239
  108.7 2.0 %collective-permute-done.10 = bf16[24,24,128]{2,1,0:T(8,128)(2,1)S(1)} collective-permute-done((bf16[24,24,128]{2,1,0:T(8,128)(2,1)S(1)}, bf16[24,24,128]{2,1,0:T(8,128)(2,1)S(1)}, u32[]{:S(2)}, u32[]{:S(2)}) %collective-permute-start.10) | collective-permute-done | bytes 147488 | tf_op jit(solution)/shard_map/ppermute | solution.py:239
  110.7 2.5 %collective-permute-done.11 = bf16[24,24,128]{2,1,0:T(8,128)(2,1)S(1)} collective-permute-done((bf16[24,24,128]{2,1,0:T(8,128)(2,1)S(1)}, bf16[24,24,128]{2,1,0:T(8,128)(2,1)S(1)}, u32[]{:S(2)}, u32[]{:S(2)}) %collective-permute-start.11) | collective-permute-done | bytes 147488 | tf_op jit(solution)/shard_map/ppermute | solution.py:239
  (54 shorter events, 4.2 us)
Async XLA Ops:
  0.6 19.4 %copy-start.2 = (bf16[24,24,128]{2,1,0:T(8,128)(2,1)S(1)}, bf16[24,24,128]{2,1,0:T(8,128)(2,1)}, u32[]{:S(2)}) copy-start(bf16[24,24,128]{2,1,0:T(8,128)(2,1)} %param.6) | copy-start | bytes 442372
  0.6 17.1 %collective-permute-start = (bf16[24,24,128]{2,1,0:T(8,128)(2,1)}, bf16[24,24,128]{2,1,0:T(8,128)(2,1)S(1)}, u32[]{:S(2)}, u32[]{:S(2)}) collective-permute-start(bf16[24,24,128]{2,1,0:T(8,128)(2,1)} %param.5), channel_id=1, source_target_pairs={{0,1},{1,2},{2,3},{3,4},{4,5},{5,6},{6,7},{7,8},{8,9},{9,10},{10,1... | collective-permute-start | bytes 442376 | tf_op jit(solution)/shard_map/ppermute | solution.py:239
  4.8 14.3 %collective-permute-start.1 = (bf16[24,24,128]{2,1,0:T(8,128)(2,1)}, bf16[24,24,128]{2,1,0:T(8,128)(2,1)S(1)}, u32[]{:S(2)}, u32[]{:S(2)}) collective-permute-start(bf16[24,24,128]{2,1,0:T(8,128)(2,1)} %param.5), channel_id=1, source_target_pairs={{0,31},{1,0},{2,1},{3,2},{4,3},{5,4},{6,5},{7,6},{8,7},{9,8},{10,9... | collective-permute-start | bytes 442376 | tf_op jit(solution)/shard_map/ppermute | solution.py:239
  20.1 18.8 %collective-permute-start.4 = (bf16[24,24,128]{2,1,0:T(8,128)(2,1)S(1)}, bf16[24,24,128]{2,1,0:T(8,128)(2,1)S(1)}, u32[]{:S(2)}, u32[]{:S(2)}) collective-permute-start(bf16[24,24,128]{2,1,0:T(8,128)(2,1)S(1)} %copy-done.2), channel_id=1, source_target_pairs={{0,1},{1,2},{2,3},{3,4},{4,5},{5,6},{6,7},{7,8},{8,9},{9,10},{10,1... | collective-permute-start | bytes 442376 | tf_op jit(solution)/shard_map/ppermute | solution.py:239
  22.0 16.9 %collective-permute-start.5 = (bf16[24,24,128]{2,1,0:T(8,128)(2,1)S(1)}, bf16[24,24,128]{2,1,0:T(8,128)(2,1)S(1)}, u32[]{:S(2)}, u32[]{:S(2)}) collective-permute-start(bf16[24,24,128]{2,1,0:T(8,128)(2,1)S(1)} %copy-done.2), channel_id=1, source_target_pairs={{0,31},{1,0},{2,1},{3,2},{4,3},{5,4},{6,5},{7,6},{8,7},{9,8},{10,9... | collective-permute-start | bytes 442376 | tf_op jit(solution)/shard_map/ppermute | solution.py:239
  30.1 8.5 %copy-start.1 = (bf16[24,24,128]{2,1,0:T(8,128)(2,1)S(1)}, bf16[24,24,128]{2,1,0:T(8,128)(2,1)}, u32[]{:S(2)}) copy-start(bf16[24,24,128]{2,1,0:T(8,128)(2,1)} %param.4) | copy-start | bytes 442372
  30.1 8.6 %copy-start = (bf16[24,24,128]{2,1,0:T(8,128)(2,1)S(1)}, bf16[24,24,128]{2,1,0:T(8,128)(2,1)}, u32[]{:S(2)}) copy-start(bf16[24,24,128]{2,1,0:T(8,128)(2,1)} %param.7) | copy-start | bytes 442372
  30.2 14.4 %collective-permute-start.2 = (bf16[22,72,128]{2,1,0:T(8,128)(2,1)S(1)}, bf16[22,72,128]{2,1,0:T(8,128)(2,1)S(1)}, u32[]{:S(2)}, u32[]{:S(2)}) collective-permute-start(bf16[22,72,128]{2,1,0:T(8,128)(2,1)S(1)} %get-tuple-element.46), channel_id=1, source_target_pairs={{0,32},{32,64},{64,96},{96,128},{128,160},{160,192},{192,224},{224... | collective-permute-start | bytes 1216520 | tf_op jit(solution)/shard_map/ppermute | solution.py:239
  32.2 12.5 %collective-permute-start.3 = (bf16[22,72,128]{2,1,0:T(8,128)(2,1)S(1)}, bf16[22,72,128]{2,1,0:T(8,128)(2,1)S(1)}, u32[]{:S(2)}, u32[]{:S(2)}) collective-permute-start(bf16[22,72,128]{2,1,0:T(8,128)(2,1)S(1)} %get-tuple-element.47), channel_id=1, source_target_pairs={{32,0},{64,32},{96,64},{128,96},{160,128},{192,160},{224,192},{256... | collective-permute-start | bytes 1216520 | tf_op jit(solution)/shard_map/ppermute | solution.py:239
  39.1 24.7 %collective-permute-start.6 = (bf16[22,72,128]{2,1,0:T(8,128)(2,1)S(1)}, bf16[22,72,128]{2,1,0:T(8,128)(2,1)S(1)}, u32[]{:S(2)}, u32[]{:S(2)}) collective-permute-start(bf16[22,72,128]{2,1,0:T(8,128)(2,1)S(1)} %get-tuple-element.44), channel_id=1, source_target_pairs={{0,32},{32,64},{64,96},{96,128},{128,160},{160,192},{192,224},{224... | collective-permute-start | bytes 1216520 | tf_op jit(solution)/shard_map/ppermute | solution.py:239
  41.8 21.9 %collective-permute-start.7 = (bf16[22,72,128]{2,1,0:T(8,128)(2,1)S(1)}, bf16[22,72,128]{2,1,0:T(8,128)(2,1)S(1)}, u32[]{:S(2)}, u32[]{:S(2)}) collective-permute-start(bf16[22,72,128]{2,1,0:T(8,128)(2,1)S(1)} %get-tuple-element.45), channel_id=1, source_target_pairs={{32,0},{64,32},{96,64},{128,96},{160,128},{192,160},{224,192},{256... | collective-permute-start | bytes 1216520 | tf_op jit(solution)/shard_map/ppermute | solution.py:239
  58.2 25.2 %collective-permute-start.12 = (bf16[22,72,128]{2,1,0:T(8,128)(2,1)S(1)}, bf16[22,72,128]{2,1,0:T(8,128)(2,1)S(1)}, u32[]{:S(2)}, u32[]{:S(2)}) collective-permute-start(bf16[22,72,128]{2,1,0:T(8,128)(2,1)S(1)} %bitcast.25), channel_id=1, source_target_pairs={{32,0},{64,32},{96,64},{128,96},{160,128},{192,160},{224,192},{256... | collective-permute-start | bytes 1216520 | tf_op jit(solution)/shard_map/ppermute | solution.py:239
  61.1 22.4 %collective-permute-start.13 = (bf16[22,72,128]{2,1,0:T(8,128)(2,1)S(1)}, bf16[22,72,128]{2,1,0:T(8,128)(2,1)S(1)}, u32[]{:S(2)}, u32[]{:S(2)}) collective-permute-start(bf16[22,72,128]{2,1,0:T(8,128)(2,1)S(1)} %bitcast.23), channel_id=1, source_target_pairs={{0,32},{32,64},{64,96},{96,128},{128,160},{160,192},{192,224},{224... | collective-permute-start | bytes 1216520 | tf_op jit(solution)/shard_map/ppermute | solution.py:239
  77.0 14.1 %collective-permute-start.8 = (bf16[22,72,128]{2,1,0:T(8,128)(2,1)S(1)}, bf16[22,72,128]{2,1,0:T(8,128)(2,1)S(1)}, u32[]{:S(2)}, u32[]{:S(2)}) collective-permute-start(bf16[22,72,128]{2,1,0:T(8,128)(2,1)S(1)} %bitcast.24), channel_id=1, source_target_pairs={{32,0},{64,32},{96,64},{128,96},{160,128},{192,160},{224,192},{256... | collective-permute-start | bytes 1216520 | tf_op jit(solution)/shard_map/ppermute | solution.py:239
  80.5 19.9 %collective-permute-start.9 = (bf16[22,72,128]{2,1,0:T(8,128)(2,1)S(1)}, bf16[22,72,128]{2,1,0:T(8,128)(2,1)S(1)}, u32[]{:S(2)}, u32[]{:S(2)}) collective-permute-start(bf16[22,72,128]{2,1,0:T(8,128)(2,1)S(1)} %bitcast.22), channel_id=1, source_target_pairs={{0,32},{32,64},{64,96},{96,128},{128,160},{160,192},{192,224},{224... | collective-permute-start | bytes 1216520 | tf_op jit(solution)/shard_map/ppermute | solution.py:239
  83.7 24.3 %collective-permute-start.14 = (bf16[24,24,128]{2,1,0:T(8,128)(2,1)S(1)}, bf16[24,24,128]{2,1,0:T(8,128)(2,1)S(1)}, u32[]{:S(2)}, u32[]{:S(2)}) collective-permute-start(bf16[24,24,128]{2,1,0:T(8,128)(2,1)S(1)} %get-tuple-element.40), channel_id=1, source_target_pairs={{0,31},{1,0},{2,1},{3,2},{4,3},{5,4},{6,5},{7,6},{8,7},{9,8},{10,9... | collective-permute-start | bytes 442376 | tf_op jit(solution)/shard_map/ppermute | solution.py:239
  88.5 19.5 %collective-permute-start.15 = (bf16[24,24,128]{2,1,0:T(8,128)(2,1)S(1)}, bf16[24,24,128]{2,1,0:T(8,128)(2,1)S(1)}, u32[]{:S(2)}, u32[]{:S(2)}) collective-permute-start(bf16[24,24,128]{2,1,0:T(8,128)(2,1)S(1)} %get-tuple-element.41), channel_id=1, source_target_pairs={{0,1},{1,2},{2,3},{3,4},{4,5},{5,6},{6,7},{7,8},{8,9},{9,10},{10,1... | collective-permute-start | bytes 442376 | tf_op jit(solution)/shard_map/ppermute | solution.py:239
  100.6 10.1 %collective-permute-start.10 = (bf16[24,24,128]{2,1,0:T(8,128)(2,1)S(1)}, bf16[24,24,128]{2,1,0:T(8,128)(2,1)S(1)}, u32[]{:S(2)}, u32[]{:S(2)}) collective-permute-start(bf16[24,24,128]{2,1,0:T(8,128)(2,1)S(1)} %get-tuple-element.42), channel_id=1, source_target_pairs={{0,31},{1,0},{2,1},{3,2},{4,3},{5,4},{6,5},{7,6},{8,7},{9,8},{10,9... | collective-permute-start | bytes 442376 | tf_op jit(solution)/shard_map/ppermute | solution.py:239
  102.5 10.7 %collective-permute-start.11 = (bf16[24,24,128]{2,1,0:T(8,128)(2,1)S(1)}, bf16[24,24,128]{2,1,0:T(8,128)(2,1)S(1)}, u32[]{:S(2)}, u32[]{:S(2)}) collective-permute-start(bf16[24,24,128]{2,1,0:T(8,128)(2,1)S(1)} %get-tuple-element.43), channel_id=1, source_target_pairs={{0,1},{1,2},{2,3},{3,4},{4,5},{5,6},{6,7},{7,8},{8,9},{9,10},{10,1... | collective-permute-start | bytes 442376 | tf_op jit(solution)/shard_map/ppermute | solution.py:239

commit v4 on v3

--- a/solution.py
+++ b/solution.py
@@ -4,6 +4,7 @@
 from jax.experimental import pallas as pl
 from jax.experimental.pallas import tpu as pltpu
 from jax.sharding import PartitionSpec as P
+
 
 R = 22
 T = 24
@@ -233,51 +234,57 @@
     return jnp.concatenate([spread(q, 0.125), mark], axis=2)
 
 
-def shift(x, axis, by, closed):
-    n = lax.axis_size(axis)
-    pairs = [(i, (i + by) % n) for i in range(n) if closed or 0 <= i + by < n]
-    return lax.ppermute(x, axis, pairs)
-
-
-def widen(x):
-    return jnp.concatenate([shift(x, "lon", 1, True), x, shift(x, "lon", -1, True)], axis=1)
+def shift(x, by):
+    n = lax.axis_size("lat")
+    return lax.ppermute(x, "lat", [(i, i + by) for i in range(n) if 0 <= i + by < n])
+
+
+def swap(x, first):
+    n = lax.axis_size("lon")
+    pairs = [(i % n, (i + 1) % n) for i in range(first, n + first, 2)]
+    return lax.ppermute(x, "lon", pairs + [(b, a) for a, b in pairs])
 
 
 def heighten(mid):
-    north = shift(mid[T - R :], "lat", 1, False)
-    south = shift(mid[:R], "lat", -1, False)
+    north = shift(mid[T - R :], 1)
+    south = shift(mid[:R], -1)
     return jnp.concatenate([north, mid, south], axis=0).reshape(ROWS * W, 128)
 
 
-def fold(north, mid, south):
-    north = north.reshape(R, W, 128)
-    south = south.reshape(R, W, 128)
-    from_south = shift(north, "lat", -1, False).astype(F32)
-    from_north = shift(south, "lat", 1, False).astype(F32)
+def fold_lat(north, mid, south):
+    from_south = shift(north.reshape(R, W, 128), -1).astype(F32)
+    from_north = shift(south.reshape(R, W, 128), 1).astype(F32)
     pad = ((T - R, 0), (0, 0), (0, 0)), ((0, T - R), (0, 0), (0, 0))
-    mid = mid.reshape(T, W, 128) + jnp.pad(from_south, pad[0]) + jnp.pad(from_north, pad[1])
-    from_east = shift(mid[:, :T].astype(BF), "lon", -1, True).astype(F32)
-    from_west = shift(mid[:, 2 * T :].astype(BF), "lon", 1, True).astype(F32)
-    return (mid[:, T : 2 * T] + from_east + from_west).astype(BF)
+    return mid.reshape(T, W, 128) + jnp.pad(from_south, pad[0]) + jnp.pad(from_north, pad[1])
 
 
 def body(queries, keys, values, out_grad):
     height = T * lax.axis_size("lat")
-    k = widen(keys)
-    k, values, first_row, queries, out_grad = lax.optimization_barrier(
-        (k, values, lax.axis_index("lat") * T, queries, out_grad)
-    )
+    even = lax.axis_index("lon") % 2 == 0
+    pair = jnp.stack([keys, values])
+    near, far = swap(pair, 0), swap(pair, 1)
+
+    def widen(x, i):
+        return jnp.concatenate([jnp.where(even, far[i], near[i]), x, jnp.where(even, near[i], far[i])], axis=1)
+
+    k = widen(keys, 0)
+    v = widen(values, 1)
+    k, first_row, queries, out_grad = lax.optimization_barrier((k, lax.axis_index("lat") * T, queries, out_grad))
     k = heighten(k)
-    v = widen(values)
     v = heighten(v)
     start, aux = tables(first_row, height)
     q = with_marks(queries)
     g = spread(out_grad, 1.0)
     p, linv, gs, *dv = run_a(start, k, aux, q, g)
-    grad_values = fold(*dv)
+    dv = fold_lat(*dv)
     attended, grad_queries, *dk = run_b(start, k, v, q, gs, p, linv)
-    grad_keys = fold(*dk)
-    return attended.reshape(T, T, 128), grad_queries.reshape(T, T, 128), grad_keys, grad_values
+    dk = fold_lat(*dk)
+    west = [x[:, :T].astype(BF) for x in (dk, dv)]
+    east = [x[:, 2 * T :].astype(BF) for x in (dk, dv)]
+    near = swap(jnp.stack([jnp.where(even, e, w) for e, w in zip(east, west)]), 0)
+    far = swap(jnp.stack([jnp.where(even, w, e) for e, w in zip(east, west)]), 1)
+    grads = [(x[:, T : 2 * T] + near[i].astype(F32) + far[i].astype(F32)).astype(BF) for i, x in enumerate((dk, dv))]
+    return attended.reshape(T, T, 128), grad_queries.reshape(T, T, 128), grads[0], grads[1]
 
 
 def solution(mesh):

time: 114 us -> 123 us (1.079)
  the two profiles are of different devices: /device:TPU:10 before, /device:TPU:8 now
where the time goes in v4:
time: 123 us
  starting transfers between devices  47.2 us (38%)
  waiting for transfers between devices  40.5 us (33%)
  Pallas kernels  26.4 us (21%)
  other arithmetic  6.85 us (6%)
    ppermute x8, starting transfers between devices, shift(): lax.ppermute(x, 'lat', [(i, i + by) for i in range(n) if 0 <= i + by < n])  26 us
    ppermute x8, waiting for transfers between devices, shift(): lax.ppermute(x, 'lat', [(i, i + by) for i in range(n) if 0 <= i + by < n])  22.3 us
    ppermute x4, starting transfers between devices, swap(): return lax.ppermute(x, 'lon', pairs + [(b, a) for a, b in pairs])  21.2 us
    ppermute x4, waiting for transfers between devices, swap(): return lax.ppermute(x, 'lon', pairs + [(b, a) for a, b in pairs])  18.2 us
    pallas_call x1, Pallas kernels, run_a(): pl.pallas_call(kernel_a, grid_spec=pltpu.PrefetchScalarGridSpec(num_scala...  13.4 us
    pallas_call x1, Pallas kernels, run_b(): pl.pallas_call(kernel_b, grid_spec=pltpu.PrefetchScalarGridSpec(num_scala...  13.1 us
    convert_element_type x1, other arithmetic, tables(): jnp.where(row_out | col_out, -1e+30, 0.0).astype(BF).reshape(ROWS * W, 128)  2.8 us
  transfers between devices with their start and end apart: 12, of which 9 were waited for; matrix products, arithmetic and copies ran while one was open for 3% of the time, Pallas kernels for 11%

profile of v4, /device:TPU:8, one launch (start us, length us, event | category | flops | bytes accessed | tf_op | source)
XLA Modules:
  0.0 122.7 jit_solution(6814948959256134892)
XLA Ops:
  0.6 1.0 pad_maximum_fusion.5
  1.7 4.9 %collective-permute-start.1 = (bf16[2,24,24,128]{3,2,1,0:T(8,128)(2,1)S(1)}, bf16[2,24,24,128]{3,2,1,0:T(8,128)(2,1)S(1)}, u32[]{:S(2)}, u32[]{:S(2)}) collective-permute-start(bf16[2,24,24,128]{3,2,1,0:T(8,128)(2,1)S(1)} %pad_maximum_fusion.5), channel_id=1, source_target_pairs={{0,1},{2,3},{4,5},{6,7},{8,9},{10,11},{12,13},{14,15},{16,17},{18,... | collective-permute-start | bytes 884744 | tf_op jit(solution)/shard_map/ppermute | solution.py:245
  6.6 11.3 %collective-permute-start = (bf16[2,24,24,128]{3,2,1,0:T(8,128)(2,1)S(1)}, bf16[2,24,24,128]{3,2,1,0:T(8,128)(2,1)S(1)}, u32[]{:S(2)}, u32[]{:S(2)}) collective-permute-start(bf16[2,24,24,128]{3,2,1,0:T(8,128)(2,1)S(1)} %pad_maximum_fusion.5), channel_id=1, source_target_pairs={{1,2},{3,4},{5,6},{7,8},{9,10},{11,12},{13,14},{15,16},{17,18},{19... | collective-permute-start | bytes 884744 | tf_op jit(solution)/shard_map/ppermute | solution.py:245
  19.2 5.5 %collective-permute-done = bf16[2,24,24,128]{3,2,1,0:T(8,128)(2,1)S(1)} collective-permute-done((bf16[2,24,24,128]{3,2,1,0:T(8,128)(2,1)S(1)}, bf16[2,24,24,128]{3,2,1,0:T(8,128)(2,1)S(1)}, u32[]{:S(2)}, u32[]{:S(2)}) %collective-permute-start) | collective-permute-done | bytes 294944 | tf_op jit(solution)/shard_map/ppermute | solution.py:245
  24.7 1.0 pad_maximum_fusion.3
  26.1 1.9 %collective-permute-start.4 = (bf16[22,72,128]{2,1,0:T(8,128)(2,1)S(1)}, bf16[22,72,128]{2,1,0:T(8,128)(2,1)S(1)}, u32[]{:S(2)}, u32[]{:S(2)}) collective-permute-start(bf16[22,72,128]{2,1,0:T(8,128)(2,1)S(1)} %get-tuple-element.48), channel_id=1, source_target_pairs={{0,32},{32,64},{64,96},{96,128},{128,160},{160,192},{192,224},{224... | collective-permute-start | bytes 1216520 | tf_op jit(solution)/shard_map/ppermute | solution.py:239
  28.0 4.5 %collective-permute-start.5 = (bf16[22,72,128]{2,1,0:T(8,128)(2,1)S(1)}, bf16[22,72,128]{2,1,0:T(8,128)(2,1)S(1)}, u32[]{:S(2)}, u32[]{:S(2)}) collective-permute-start(bf16[22,72,128]{2,1,0:T(8,128)(2,1)S(1)} %get-tuple-element.49), channel_id=1, source_target_pairs={{32,0},{64,32},{96,64},{128,96},{160,128},{192,160},{224,192},{256... | collective-permute-start | bytes 1216520 | tf_op jit(solution)/shard_map/ppermute | solution.py:239
  32.7 1.9 %collective-permute-start.2 = (bf16[22,72,128]{2,1,0:T(8,128)(2,1)S(1)}, bf16[22,72,128]{2,1,0:T(8,128)(2,1)S(1)}, u32[]{:S(2)}, u32[]{:S(2)}) collective-permute-start(bf16[22,72,128]{2,1,0:T(8,128)(2,1)S(1)} %get-tuple-element.50), channel_id=1, source_target_pairs={{0,32},{32,64},{64,96},{96,128},{128,160},{160,192},{192,224},{224... | collective-permute-start | bytes 1216520 | tf_op jit(solution)/shard_map/ppermute | solution.py:239
  34.6 4.5 %collective-permute-start.3 = (bf16[22,72,128]{2,1,0:T(8,128)(2,1)S(1)}, bf16[22,72,128]{2,1,0:T(8,128)(2,1)S(1)}, u32[]{:S(2)}, u32[]{:S(2)}) collective-permute-start(bf16[22,72,128]{2,1,0:T(8,128)(2,1)S(1)} %get-tuple-element.51), channel_id=1, source_target_pairs={{32,0},{64,32},{96,64},{128,96},{160,128},{192,160},{224,192},{256... | collective-permute-start | bytes 1216520 | tf_op jit(solution)/shard_map/ppermute | solution.py:239
  39.2 2.8 %select_convert_fusion.aux_ref = bf16[4896,128]{1,0:T(8,128)(2,1)S(1)} fusion(s32[128]{0:T(128)S(1)} %iota_add_fusion.1, s32[128]{0:T(128)S(1)} %iota_add_fusion, s32[128]{0:T(128)S(1)} %broadcast_add_fusion, s32[128]{0:T(128)S(1)} %add_clamp_fusion, s32[4896]{0:T(1024)S(1)} %iota.136, s32[4896]{0:T(1024)S(1)} %iota.128, pred[128]{0:T(512)(128)(4,1)S(1)} %compare_and_fusion, ...), kind=kLoop, calls=%fused_computation | loop fusion | flops 6893568 | bytes 1294848 | tf_op jit(solution)/shard_map/convert_element_type | solution.py:218
  42.2 4.9 %collective-permute-done.2 = bf16[22,72,128]{2,1,0:T(8,128)(2,1)S(1)} collective-permute-done((bf16[22,72,128]{2,1,0:T(8,128)(2,1)S(1)}, bf16[22,72,128]{2,1,0:T(8,128)(2,1)S(1)}, u32[]{:S(2)}, u32[]{:S(2)}) %collective-permute-start.2) | collective-permute-done | bytes 405536 | tf_op jit(solution)/shard_map/ppermute | solution.py:239
  47.5 13.4 %scores_and_dv.1 = (bf16[3,3744,384]{2,1,0:T(8,128)(2,1)}, f32[3,8,384]{2,1,0:T(8,128)S(1)}, bf16[3,384,128]{2,1,0:T(8,128)(2,1)S(1)}, bf16[1584,128]{1,0:T(8,12...) custom-call(s32[3]{0:T(128)S(1)} %fusion.5.start, bf16[4896,128]{1,0:T(8,128)(2,1)S(1)} %bitcast.55, ...), custom_call_target="tpu_custom_call" | custom-call | flops 6000000000 | bytes 14000000 | tf_op jit(solution)/shard_map/scores_and_dv/pallas_call | solution.py:174
  61.0 13.1 %attended_and_dk.1 = (bf16[576,128]{1,0:T(8,128)(2,1)}, bf16[576,128]{1,0:T(8,128)(2,1)}, bf16[1584,128]{1,0:T(8,128)(2,1)S(1)}, f32[1728,128]{1,0:T(8,128)S(1)}, bf16[1584,128]{1,0:T(8,128)(2,1)S(1)}) custom-call(s32[3]{0:T(128)S(1)} %fusion.5.start, bf16[4896,128]{1,0:T(8,128)(2,1)S(1)} %bitcast.56, bf16[4896,128]{1,0:T(8,128)(2,1)S(1)} %bitcast.57, ...), custom_call_target="tpu_custom_call" | custom-call | flops 8000000000 | bytes 14000000 | tf_op jit(solution)/shard_map/attended_and_dk/pallas_call | solution.py:191
  74.1 4.7 %collective-permute-start.6 = (bf16[22,72,128]{2,1,0:T(8,128)(2,1)S(1)}, bf16[22,72,128]{2,1,0:T(8,128)(2,1)S(1)}, u32[]{:S(2)}, u32[]{:S(2)}) collective-permute-start(bf16[22,72,128]{2,1,0:T(8,128)(2,1)S(1)} %bitcast.63), channel_id=1, source_target_pairs={{32,0},{64,32},{96,64},{128,96},{160,128},{192,160},{224,192},{256... | collective-permute-start | bytes 1216520 | tf_op jit(solution)/shard_map/ppermute | solution.py:239
  78.8 1.9 %collective-permute-start.7 = (bf16[22,72,128]{2,1,0:T(8,128)(2,1)S(1)}, bf16[22,72,128]{2,1,0:T(8,128)(2,1)S(1)}, u32[]{:S(2)}, u32[]{:S(2)}) collective-permute-start(bf16[22,72,128]{2,1,0:T(8,128)(2,1)S(1)} %bitcast.62), channel_id=1, source_target_pairs={{0,32},{32,64},{64,96},{96,128},{128,160},{160,192},{192,224},{224... | collective-permute-start | bytes 1216520 | tf_op jit(solution)/shard_map/ppermute | solution.py:239
  80.7 4.5 %collective-permute-start.8 = (bf16[22,72,128]{2,1,0:T(8,128)(2,1)S(1)}, bf16[22,72,128]{2,1,0:T(8,128)(2,1)S(1)}, u32[]{:S(2)}, u32[]{:S(2)}) collective-permute-start(bf16[22,72,128]{2,1,0:T(8,128)(2,1)S(1)} %bitcast.61), channel_id=1, source_target_pairs={{32,0},{64,32},{96,64},{128,96},{160,128},{192,160},{224,192},{256... | collective-permute-start | bytes 1216520 | tf_op jit(solution)/shard_map/ppermute | solution.py:239
  85.3 1.9 %collective-permute-start.9 = (bf16[22,72,128]{2,1,0:T(8,128)(2,1)S(1)}, bf16[22,72,128]{2,1,0:T(8,128)(2,1)S(1)}, u32[]{:S(2)}, u32[]{:S(2)}) collective-permute-start(bf16[22,72,128]{2,1,0:T(8,128)(2,1)S(1)} %bitcast.60), channel_id=1, source_target_pairs={{0,32},{32,64},{64,96},{96,128},{128,160},{160,192},{192,224},{224... | collective-permute-start | bytes 1216520 | tf_op jit(solution)/shard_map/ppermute | solution.py:239
  87.2 5.4 %collective-permute-done.7 = bf16[22,72,128]{2,1,0:T(8,128)(2,1)S(1)} collective-permute-done((bf16[22,72,128]{2,1,0:T(8,128)(2,1)S(1)}, bf16[22,72,128]{2,1,0:T(8,128)(2,1)S(1)}, u32[]{:S(2)}, u32[]{:S(2)}) %collective-permute-start.7) | collective-permute-done | bytes 405536 | tf_op jit(solution)/shard_map/ppermute | solution.py:239
  92.8 2.4 %collective-permute-done.8 = bf16[22,72,128]{2,1,0:T(8,128)(2,1)S(1)} collective-permute-done((bf16[22,72,128]{2,1,0:T(8,128)(2,1)S(1)}, bf16[22,72,128]{2,1,0:T(8,128)(2,1)S(1)}, u32[]{:S(2)}, u32[]{:S(2)}) %collective-permute-start.8) | collective-permute-done | bytes 405536 | tf_op jit(solution)/shard_map/ppermute | solution.py:239
  95.2 9.3 %collective-permute-done.9 = bf16[22,72,128]{2,1,0:T(8,128)(2,1)S(1)} collective-permute-done((bf16[22,72,128]{2,1,0:T(8,128)(2,1)S(1)}, bf16[22,72,128]{2,1,0:T(8,128)(2,1)S(1)}, u32[]{:S(2)}, u32[]{:S(2)}) %collective-permute-start.9) | collective-permute-done | bytes 405536 | tf_op jit(solution)/shard_map/ppermute | solution.py:239
  104.8 3.0 %collective-permute-start.11 = (bf16[2,24,24,128]{3,2,1,0:T(8,128)(2,1)S(1)}, bf16[2,24,24,128]{3,2,1,0:T(8,128)(2,1)S(1)}, u32[]{:S(2)}, u32[]{:S(2)}) collective-permute-start(bf16[2,24,24,128]{3,2,1,0:T(8,128)(2,1)S(1)} %pad_maximum_fusion.7), channel_id=1, source_target_pairs={{1,2},{3,4},{5,6},{7,8},{9,10},{11,12},{13,14},{15,16},{17,18},{19... | collective-permute-start | bytes 884744 | tf_op jit(solution)/shard_map/ppermute | solution.py:245
  107.9 1.9 %collective-permute-start.10 = (bf16[2,24,24,128]{3,2,1,0:T(8,128)(2,1)S(1)}, bf16[2,24,24,128]{3,2,1,0:T(8,128)(2,1)S(1)}, u32[]{:S(2)}, u32[]{:S(2)}) collective-permute-start(bf16[2,24,24,128]{3,2,1,0:T(8,128)(2,1)S(1)} %pad_maximum_fusion.6), channel_id=1, source_target_pairs={{0,1},{2,3},{4,5},{6,7},{8,9},{10,11},{12,13},{14,15},{16,17},{18,... | collective-permute-start | bytes 884744 | tf_op jit(solution)/shard_map/ppermute | solution.py:245
  109.8 7.4 %collective-permute-done.11 = bf16[2,24,24,128]{3,2,1,0:T(8,128)(2,1)S(1)} collective-permute-done((bf16[2,24,24,128]{3,2,1,0:T(8,128)(2,1)S(1)}, bf16[2,24,24,128]{3,2,1,0:T(8,128)(2,1)S(1)}, u32[]{:S(2)}, u32[]{:S(2)}) %collective-permute-start.11) | collective-permute-done | bytes 294944 | tf_op jit(solution)/shard_map/ppermute | solution.py:245
  117.2 4.7 %collective-permute-done.10 = bf16[2,24,24,128]{3,2,1,0:T(8,128)(2,1)S(1)} collective-permute-done((bf16[2,24,24,128]{3,2,1,0:T(8,128)(2,1)S(1)}, bf16[2,24,24,128]{3,2,1,0:T(8,128)(2,1)S(1)}, u32[]{:S(2)}, u32[]{:S(2)}) %collective-permute-start.10) | collective-permute-done | bytes 294944 | tf_op jit(solution)/shard_map/ppermute | solution.py:245
  (50 shorter events, 3.5 us)
Async XLA Ops:
  0.6 25.3 %copy-start = (bf16[24,24,128]{2,1,0:T(8,128)(2,1)S(1)}, bf16[24,24,128]{2,1,0:T(8,128)(2,1)}, u32[]{:S(2)}) copy-start(bf16[24,24,128]{2,1,0:T(8,128)(2,1)} %param.6) | copy-start | bytes 442372
  1.7 17.5 %collective-permute-start.1 = (bf16[2,24,24,128]{3,2,1,0:T(8,128)(2,1)S(1)}, bf16[2,24,24,128]{3,2,1,0:T(8,128)(2,1)S(1)}, u32[]{:S(2)}, u32[]{:S(2)}) collective-permute-start(bf16[2,24,24,128]{3,2,1,0:T(8,128)(2,1)S(1)} %pad_maximum_fusion.5), channel_id=1, source_target_pairs={{0,1},{2,3},{4,5},{6,7},{8,9},{10,11},{12,13},{14,15},{16,17},{18,... | collective-permute-start | bytes 884744 | tf_op jit(solution)/shard_map/ppermute | solution.py:245
  6.6 18.1 %collective-permute-start = (bf16[2,24,24,128]{3,2,1,0:T(8,128)(2,1)S(1)}, bf16[2,24,24,128]{3,2,1,0:T(8,128)(2,1)S(1)}, u32[]{:S(2)}, u32[]{:S(2)}) collective-permute-start(bf16[2,24,24,128]{3,2,1,0:T(8,128)(2,1)S(1)} %pad_maximum_fusion.5), channel_id=1, source_target_pairs={{1,2},{3,4},{5,6},{7,8},{9,10},{11,12},{13,14},{15,16},{17,18},{19... | collective-permute-start | bytes 884744 | tf_op jit(solution)/shard_map/ppermute | solution.py:245
  25.9 16.1 %copy-start.2 = (bf16[24,24,128]{2,1,0:T(8,128)(2,1)S(1)}, bf16[24,24,128]{2,1,0:T(8,128)(2,1)}, u32[]{:S(2)}) copy-start(bf16[24,24,128]{2,1,0:T(8,128)(2,1)} %param.4) | copy-start | bytes 442372
  26.0 16.1 %copy-start.1 = (bf16[24,24,128]{2,1,0:T(8,128)(2,1)S(1)}, bf16[24,24,128]{2,1,0:T(8,128)(2,1)}, u32[]{:S(2)}) copy-start(bf16[24,24,128]{2,1,0:T(8,128)(2,1)} %param.7) | copy-start | bytes 442372
  26.1 34.8 %collective-permute-start.4 = (bf16[22,72,128]{2,1,0:T(8,128)(2,1)S(1)}, bf16[22,72,128]{2,1,0:T(8,128)(2,1)S(1)}, u32[]{:S(2)}, u32[]{:S(2)}) collective-permute-start(bf16[22,72,128]{2,1,0:T(8,128)(2,1)S(1)} %get-tuple-element.48), channel_id=1, source_target_pairs={{0,32},{32,64},{64,96},{96,128},{128,160},{160,192},{192,224},{224... | collective-permute-start | bytes 1216520 | tf_op jit(solution)/shard_map/ppermute | solution.py:239
  28.0 32.8 %collective-permute-start.5 = (bf16[22,72,128]{2,1,0:T(8,128)(2,1)S(1)}, bf16[22,72,128]{2,1,0:T(8,128)(2,1)S(1)}, u32[]{:S(2)}, u32[]{:S(2)}) collective-permute-start(bf16[22,72,128]{2,1,0:T(8,128)(2,1)S(1)} %get-tuple-element.49), channel_id=1, source_target_pairs={{32,0},{64,32},{96,64},{128,96},{160,128},{192,160},{224,192},{256... | collective-permute-start | bytes 1216520 | tf_op jit(solution)/shard_map/ppermute | solution.py:239
  32.7 14.5 %collective-permute-start.2 = (bf16[22,72,128]{2,1,0:T(8,128)(2,1)S(1)}, bf16[22,72,128]{2,1,0:T(8,128)(2,1)S(1)}, u32[]{:S(2)}, u32[]{:S(2)}) collective-permute-start(bf16[22,72,128]{2,1,0:T(8,128)(2,1)S(1)} %get-tuple-element.50), channel_id=1, source_target_pairs={{0,32},{32,64},{64,96},{96,128},{128,160},{160,192},{192,224},{224... | collective-permute-start | bytes 1216520 | tf_op jit(solution)/shard_map/ppermute | solution.py:239
  34.6 12.8 %collective-permute-start.3 = (bf16[22,72,128]{2,1,0:T(8,128)(2,1)S(1)}, bf16[22,72,128]{2,1,0:T(8,128)(2,1)S(1)}, u32[]{:S(2)}, u32[]{:S(2)}) collective-permute-start(bf16[22,72,128]{2,1,0:T(8,128)(2,1)S(1)} %get-tuple-element.51), channel_id=1, source_target_pairs={{32,0},{64,32},{96,64},{128,96},{160,128},{192,160},{224,192},{256... | collective-permute-start | bytes 1216520 | tf_op jit(solution)/shard_map/ppermute | solution.py:239
  74.1 13.1 %collective-permute-start.6 = (bf16[22,72,128]{2,1,0:T(8,128)(2,1)S(1)}, bf16[22,72,128]{2,1,0:T(8,128)(2,1)S(1)}, u32[]{:S(2)}, u32[]{:S(2)}) collective-permute-start(bf16[22,72,128]{2,1,0:T(8,128)(2,1)S(1)} %bitcast.63), channel_id=1, source_target_pairs={{32,0},{64,32},{96,64},{128,96},{160,128},{192,160},{224,192},{256... | collective-permute-start | bytes 1216520 | tf_op jit(solution)/shard_map/ppermute | solution.py:239
  78.8 13.9 %collective-permute-start.7 = (bf16[22,72,128]{2,1,0:T(8,128)(2,1)S(1)}, bf16[22,72,128]{2,1,0:T(8,128)(2,1)S(1)}, u32[]{:S(2)}, u32[]{:S(2)}) collective-permute-start(bf16[22,72,128]{2,1,0:T(8,128)(2,1)S(1)} %bitcast.62), channel_id=1, source_target_pairs={{0,32},{32,64},{64,96},{96,128},{128,160},{160,192},{192,224},{224... | collective-permute-start | bytes 1216520 | tf_op jit(solution)/shard_map/ppermute | solution.py:239
  80.7 14.5 %collective-permute-start.8 = (bf16[22,72,128]{2,1,0:T(8,128)(2,1)S(1)}, bf16[22,72,128]{2,1,0:T(8,128)(2,1)S(1)}, u32[]{:S(2)}, u32[]{:S(2)}) collective-permute-start(bf16[22,72,128]{2,1,0:T(8,128)(2,1)S(1)} %bitcast.61), channel_id=1, source_target_pairs={{32,0},{64,32},{96,64},{128,96},{160,128},{192,160},{224,192},{256... | collective-permute-start | bytes 1216520 | tf_op jit(solution)/shard_map/ppermute | solution.py:239
  85.3 19.3 %collective-permute-start.9 = (bf16[22,72,128]{2,1,0:T(8,128)(2,1)S(1)}, bf16[22,72,128]{2,1,0:T(8,128)(2,1)S(1)}, u32[]{:S(2)}, u32[]{:S(2)}) collective-permute-start(bf16[22,72,128]{2,1,0:T(8,128)(2,1)S(1)} %bitcast.60), channel_id=1, source_target_pairs={{0,32},{32,64},{64,96},{96,128},{128,160},{160,192},{192,224},{224... | collective-permute-start | bytes 1216520 | tf_op jit(solution)/shard_map/ppermute | solution.py:239
  104.8 12.3 %collective-permute-start.11 = (bf16[2,24,24,128]{3,2,1,0:T(8,128)(2,1)S(1)}, bf16[2,24,24,128]{3,2,1,0:T(8,128)(2,1)S(1)}, u32[]{:S(2)}, u32[]{:S(2)}) collective-permute-start(bf16[2,24,24,128]{3,2,1,0:T(8,128)(2,1)S(1)} %pad_maximum_fusion.7), channel_id=1, source_target_pairs={{1,2},{3,4},{5,6},{7,8},{9,10},{11,12},{13,14},{15,16},{17,18},{19... | collective-permute-start | bytes 884744 | tf_op jit(solution)/shard_map/ppermute | solution.py:245
  107.9 14.0 %collective-permute-start.10 = (bf16[2,24,24,128]{3,2,1,0:T(8,128)(2,1)S(1)}, bf16[2,24,24,128]{3,2,1,0:T(8,128)(2,1)S(1)}, u32[]{:S(2)}, u32[]{:S(2)}) collective-permute-start(bf16[2,24,24,128]{3,2,1,0:T(8,128)(2,1)S(1)} %pad_maximum_fusion.6), channel_id=1, source_target_pairs={{0,1},{2,3},{4,5},{6,7},{8,9},{10,11},{12,13},{14,15},{16,17},{18,... | collective-permute-start | bytes 884744 | tf_op jit(solution)/shard_map/ppermute | solution.py:245

commit v5 on v4

v5 whole, which is shorter than its diff:
```python
import jax
import jax.numpy as jnp
from jax import lax
from jax.experimental import pallas as pl
from jax.experimental.pallas import tpu as pltpu
from jax.sharding import PartitionSpec as P


R = 22
T = 24
W = 3 * T
BR = 8
NB = T // BR
SR = BR + 2 * R
NQ = 2 * BR * T
MID = T * W
EDGE = R * W
FAR = (SR - T) * W
NK = MID + FAR
PART = 2 * W
F32 = jnp.float32
BF = jnp.bfloat16
NT = (((1,), (1,)), ((), ()))
TN = (((0,), (0,)), ((), ()))


def far_base(start, b):
    return pl.multiple_of(start[b] * W, 64)


def kernel_a(start, km_ref, kf_ref, am_ref, af_ref, q_ref, g_ref, pm_ref, pf_ref, linv_ref, gs_ref, vf_ref, s_scr, m_scr, acc):
    b = pl.program_id(0)
    here = lax.rem(b, 2)
    base = far_base(start, jnp.minimum(b, NB - 1))
    prior_base = far_base(start, jnp.maximum(b - 1, 0))

    def scores(part, at, n, m):
        at = pl.multiple_of(at, 16)
        if part == 0:
            rows = pl.ds(at, n)
            lhs = jnp.concatenate([km_ref[rows, :], am_ref[rows, :]], axis=1)
        else:
            rows = pl.ds(pl.multiple_of(base + at, 16), n)
            lhs = jnp.concatenate([kf_ref[rows, :], af_ref[rows, :]], axis=1)
        s = lax.dot_general(lhs, q_ref[0], NT, preferred_element_type=F32)
        s_scr[here, pl.ds(at + part * MID, n), :] = s
        return jnp.maximum(m, jnp.max(s.reshape(n // 8, 8, NQ), axis=0))

    def expo(part, at, n, m, l):
        at = pl.multiple_of(at, 16)
        p = jnp.exp(s_scr[1 - here, pl.ds(at + part * MID, n), :] - m)
        (pm_ref, pf_ref)[part][0, pl.ds(at, n), :] = p.astype(BF)
        return l + jnp.sum(p.reshape(n // 8, 8, NQ), axis=0)

    def close(m):
        m_scr[...] = jnp.broadcast_to(jnp.max(m, axis=0, keepdims=True), (8, NQ))

    def finish(l):
        linv = 1.0 / jnp.sum(l, axis=0, keepdims=True)
        linv_ref[0] = jnp.broadcast_to(linv, (8, NQ))
        turned = jnp.transpose(jnp.broadcast_to(linv, (128, NQ)))
        gs_ref[0] = (g_ref[0].astype(F32) * turned).astype(BF)

    low = jnp.full((8, NQ), -3e38, F32)
    zero = jnp.zeros((8, NQ), F32)

    @pl.when(b == 0)
    def _():
        acc[...] = jnp.zeros_like(acc)
        close(scores(1, 0, FAR, scores(0, 0, MID, low)))

    @pl.when((b > 0) & (b < NB))
    def _():
        m = m_scr[:1]
        carry = low, zero
        for part, many, parts in ((0, MID // PART, 6), (1, FAR // PART, 7)):

            def both(c, carry, part=part, parts=parts):
                fresh, l = carry
                for i in range(parts):
                    fresh = scores(part, (c * parts + i) * PART, PART, fresh)
                    l = expo(part, (c * parts + i) * PART, PART, m, l)
                return fresh, l

            carry = lax.fori_loop(0, many // parts, both, carry)
        close(carry[0])
        finish(carry[1])

    @pl.when(b == NB)
    def _():
        m, l = m_scr[:1], zero
        for part, n in ((0, MID // 2), (1, FAR // 2)):
            l = lax.fori_loop(0, 2, lambda c, l, part=part, n=n: expo(part, c * n, n, m, l), l)
        finish(l)

    @pl.when(b > 0)
    def _():
        acc[pl.ds(prior_base, FAR), :] += jnp.dot(pf_ref[0], gs_ref[0], preferred_element_type=F32)

    @pl.when(b == NB)
    def _():
        vf_ref[...] = acc[...].astype(BF)


def score_grads(p, v, gs, corr):
    gw = lax.dot_general(v, gs, NT, preferred_element_type=F32)
    return (p.astype(F32) * (gw - corr)).astype(BF)


def kernel_far(start, kf_ref, vm_ref, vf_ref, q_ref, gs_ref, pm_ref, pf_ref, linv_ref, dvf_ref, o_ref, corr_ref, dqt_ref, north_ref, south_ref, acc):
    b = pl.program_id(0)
    rows = pl.ds(far_base(start, b), FAR)

    @pl.when(b == 0)
    def _():
        acc[...] = jnp.zeros_like(acc)
        north_ref[1] = dvf_ref[:EDGE, :]
        south_ref[1] = dvf_ref[EDGE:, :]

    gs = gs_ref[0]
    ot = lax.dot_general(vm_ref[...], pm_ref[0], TN, preferred_element_type=F32)
    ot += lax.dot_general(vf_ref[rows, :], pf_ref[0], TN, preferred_element_type=F32)
    lane = lax.broadcasted_iota(jnp.int32, (NQ // 2, 128), 1)
    o = jnp.transpose(ot * linv_ref[0][:1])
    o_ref[...] = jnp.where(lane < 64, o[: NQ // 2], o[NQ // 2 :]).astype(BF)
    row = jnp.sum(gs.astype(F32) * o.astype(BF).astype(F32), axis=1, keepdims=True)
    corr = jnp.transpose(jnp.broadcast_to(row, (NQ, 128)))
    corr_ref[0] = corr[:8]
    ds = score_grads(pf_ref[0], vf_ref[rows, :], gs, corr[:1])
    acc[rows, :] += jnp.dot(ds, q_ref[0][:, :128], preferred_element_type=F32)
    dqt_ref[0] = lax.dot_general(kf_ref[rows, :], ds, TN, preferred_element_type=F32)

    @pl.when(b == NB - 1)
    def _():
        north_ref[0] = acc[:EDGE, :].astype(BF)
        south_ref[0] = acc[EDGE:, :].astype(BF)


def kernel_mid(start, km_ref, vm_ref, q_ref, gs_ref, pm_ref, corr_ref, dqt_ref, dq_ref, grads_ref):
    b = pl.program_id(0)

    @pl.when(b == 0)
    def _():
        grads_ref[...] = jnp.zeros_like(grads_ref)

    gs = gs_ref[0]
    ds = score_grads(pm_ref[0], vm_ref[...], gs, corr_ref[0][:1])
    grads_ref[0] += jnp.dot(ds, q_ref[0][:, :128], preferred_element_type=F32)
    dqt = dqt_ref[0] + lax.dot_general(km_ref[...], ds, TN, preferred_element_type=F32)
    grads_ref[1] += jnp.dot(pm_ref[0], gs, preferred_element_type=F32)
    lane = lax.broadcasted_iota(jnp.int32, (NQ // 2, 128), 1)
    dq = jnp.transpose(dqt * 0.125)
    dq_ref[...] = jnp.where(lane < 64, dq[: NQ // 2], dq[NQ // 2 :]).astype(BF)


def whole(*shape):
    return pl.BlockSpec(shape, lambda b, s: (0,) * len(shape))


def per_block(*shape, at=lambda b: b):
    return pl.BlockSpec((1,) + shape, lambda b, s: (at(b),) + (0,) * len(shape))


def rows_of_block():
    return pl.BlockSpec((NQ // 2, 128), lambda b, s: (b, 0))


def sds(*shape, dtype=BF):
    return jax.ShapeDtypeStruct(shape, dtype)


def call(kernel, grid, in_specs, out_specs, out_shape, scratch, flops):
    return pl.pallas_call(
        kernel,
        grid_spec=pltpu.PrefetchScalarGridSpec(
            num_scalar_prefetch=1, grid=(grid,), in_specs=in_specs, out_specs=out_specs, scratch_shapes=scratch
        ),
        out_shape=out_shape,
        compiler_params=pltpu.CompilerParams(vmem_limit_bytes=48 << 20),
        cost_estimate=pl.CostEstimate(flops=flops, bytes_accessed=14_000_000, transcendentals=0),
    )


def run_a(start, km, kf, am, af, q, g):
    ahead = lambda b: jnp.minimum(b, NB - 1)
    behind = lambda b: jnp.maximum(b - 1, 0)
    return call(
        kernel_a,
        NB + 1,
        [whole(MID, 128), whole(2 * EDGE, 128)] * 2 + [per_block(NQ, 256, at=ahead), per_block(NQ, 128, at=behind)],
        [per_block(*x, at=behind) for x in ((MID, NQ), (FAR, NQ), (8, NQ), (NQ, 128))] + [whole(2 * EDGE, 128)],
        [sds(NB, MID, NQ), sds(NB, FAR, NQ), sds(NB, 8, NQ, dtype=F32), sds(NB, NQ, 128), sds(2 * EDGE, 128)],
        [pltpu.VMEM((2, NK, NQ), F32), pltpu.VMEM((8, NQ), F32), pltpu.VMEM((2 * EDGE, 128), F32)],
        5_000_000_000,
    )(start, km, kf, am, af, q, g)


def run_far(start, kf, vm, vf, q, gs, pm, pf, linv, dvf):
    return call(
        kernel_far,
        NB,
        [whole(2 * EDGE, 128), whole(MID, 128), whole(2 * EDGE, 128), per_block(NQ, 256), per_block(NQ, 128)]
        + [per_block(MID, NQ), per_block(FAR, NQ), per_block(8, NQ), whole(2 * EDGE, 128)],
        [rows_of_block(), per_block(8, NQ), per_block(128, NQ), whole(2, EDGE, 128), whole(2, EDGE, 128)],
        [sds(T * T, 128), sds(NB, 8, NQ, dtype=F32), sds(NB, 128, NQ, dtype=F32), sds(2, EDGE, 128), sds(2, EDGE, 128)],
        [pltpu.VMEM((2 * EDGE, 128), F32)],
        5_000_000_000,
    )(start, kf, vm, vf, q, gs, pm, pf, linv, dvf)


def run_mid(start, km, vm, q, gs, pm, corr, dqt):
    return call(
        kernel_mid,
        NB,
        [whole(MID, 128), whole(MID, 128), per_block(NQ, 256), per_block(NQ, 128), per_block(MID, NQ)]
        + [per_block(8, NQ), per_block(128, NQ)],
        [rows_of_block(), whole(2, MID, 128)],
        [sds(T * T, 128), sds(2, MID, 128, dtype=F32)],
        [],
        5_000_000_000,
    )(start, km, vm, q, gs, pm, corr, dqt)


def tables(first_row, height):
    i0 = first_row + BR * jnp.arange(NB, dtype=jnp.int32)
    f0 = jnp.clip(i0 - R, 0, height - 45)
    start = jnp.clip(f0 - first_row + R, 0, T - BR) // 8 * 8

    def lanes(krow, n):
        krow = krow + (first_row - R)
        kcol = lax.broadcasted_iota(jnp.int32, (n, W, 128), 1)
        lane = lax.broadcasted_iota(jnp.int32, (n, W, 128), 2)
        f = jnp.clip(first_row + lane - R, 0, height - 45)
        row_out = (lane < T) & ((krow < f) | (krow >= f + 45))
        qcol = lane - T
        col_out = (lane >= T) & (lane < 2 * T) & ((kcol < qcol + 2) | (kcol > qcol + 46))
        return jnp.where(row_out | col_out, -1e30, 0.0).astype(BF).reshape(n * W, 128)

    far = lax.broadcasted_iota(jnp.int32, (2 * R, W, 128), 0)
    mid = lax.broadcasted_iota(jnp.int32, (T, W, 128), 0) + R
    return start.astype(jnp.int32), lanes(mid, T), lanes(far + jnp.where(far >= R, T, 0), 2 * R)


def spread(x, scale):
    x = (x.reshape(NB, 1, BR * T, 128) * scale).astype(BF)
    lane = lax.broadcasted_iota(jnp.int32, (1, 2, 1, 128), 3) // 64
    head = lax.broadcasted_iota(jnp.int32, (1, 2, 1, 128), 1)
    return jnp.where(lane == head, x, jnp.zeros((), BF)).reshape(NB, NQ, 128)


def with_marks(q):
    lane = lax.broadcasted_iota(jnp.int32, (NB, 2, BR, T, 128), 4)
    row = lax.broadcasted_iota(jnp.int32, (NB, 2, BR, T, 128), 0) * BR + lax.broadcasted_iota(jnp.int32, (NB, 2, BR, T, 128), 2)
    col = lax.broadcasted_iota(jnp.int32, (NB, 2, BR, T, 128), 3)
    mark = jnp.where((lane == row) | (lane == T + col), 1.0, 0.0).astype(BF).reshape(NB, NQ, 128)
    return jnp.concatenate([spread(q, 0.125), mark], axis=2)


def shift(x, by):
    n = lax.axis_size("lat")
    return lax.ppermute(x, "lat", [(i, i + by) for i in range(n) if 0 <= i + by < n])


def swap(x, first):
    n = lax.axis_size("lon")
    pairs = [(i % n, (i + 1) % n) for i in range(first, n + first, 2)]
    return lax.ppermute(x, "lon", pairs + [(b, a) for a, b in pairs])


def far_rows(mid):
    return jnp.concatenate([shift(mid[T - R :], 1), shift(mid[:R], -1)], axis=0).reshape(2 * EDGE, 128)


def body(queries, keys, values, out_grad):
    height = T * lax.axis_size("lat")
    even = lax.axis_index("lon") % 2 == 0
    start, am, af = tables(lax.axis_index("lat") * T, height)
    q = with_marks(queries)
    g = spread(out_grad, 1.0)
    pair = jnp.stack([keys, values])
    near, far = swap(pair, 0), swap(pair, 1)

    def widen(x, i):
        return jnp.concatenate([jnp.where(even, far[i], near[i]), x, jnp.where(even, near[i], far[i])], axis=1)

    km = widen(keys, 0)
    vm = widen(values, 1)
    kf = far_rows(km)
    vf = far_rows(vm)
    km = km.reshape(MID, 128)
    vm = vm.reshape(MID, 128)
    pm, pf, linv, gs, dvf = run_a(start, km, kf, am, af, q, g)
    attended, corr, dqt, north, south = run_far(start, kf, vm, vf, q, gs, pm, pf, linv, dvf)
    from_south = shift(north, -1).reshape(2, R, W, 128)
    from_north = shift(south, 1).reshape(2, R, W, 128)
    grad_queries, mid = run_mid(start, km, vm, q, gs, pm, corr, dqt)
    none = (0, 0)
    mid = mid.reshape(2, T, W, 128)
    mid = mid + jnp.pad(from_south.astype(F32), (none, (T - R, 0), none, none))
    mid = mid + jnp.pad(from_north.astype(F32), (none, (0, T - R), none, none))
    west = mid[:, :, :T].astype(BF)
    east = mid[:, :, 2 * T :].astype(BF)
    near = swap(jnp.where(even, east, west), 0)
    far = swap(jnp.where(even, west, east), 1)
    grads = [(mid[i, :, T : 2 * T] + near[i].astype(F32) + far[i].astype(F32)).astype(BF) for i in range(2)]
    return attended.reshape(T, T, 128), grad_queries.reshape(T, T, 128), grads[0], grads[1]


def solution(mesh):
    spec = P("lat", "lon", None)
    return jax.shard_map(body, mesh=mesh, in_specs=(spec,) * 4, out_specs=(spec,) * 4, check_vma=False)
```

time: 123 us -> 106 us (0.86)
  the two profiles are of different devices: /device:TPU:8 before, /device:TPU:10 now
where the time goes in v5:
time: 106 us
  starting transfers between devices  45.6 us (43%)
  Pallas kernels  28.3 us (27%)
  waiting for transfers between devices  22.9 us (22%)
  other arithmetic  6.83 us (6%)
    ppermute x4, starting transfers between devices, swap(): return lax.ppermute(x, 'lon', pairs + [(b, a) for a, b in pairs])  28 us
    ppermute x6, starting transfers between devices, shift(): lax.ppermute(x, 'lat', [(i, i + by) for i in range(n) if 0 <= i + by < n])  17.6 us
    ppermute x6, waiting for transfers between devices, shift(): lax.ppermute(x, 'lat', [(i, i + by) for i in range(n) if 0 <= i + by < n])  14.7 us
    pallas_call x1, Pallas kernels, run_a(): call(kernel_a, NB + 1, [whole(MID, 128), whole(2 * EDGE, 128)] * 2 + [per...  11.5 us
    pallas_call x1, Pallas kernels, run_far(): call(kernel_far, NB, [whole(2 * EDGE, 128), whole(MID, 128), whole(2 * ED...  9.77 us
    ppermute x4, waiting for transfers between devices, swap(): return lax.ppermute(x, 'lon', pairs + [(b, a) for a, b in pairs])  8.19 us
    pallas_call x1, Pallas kernels, run_mid(): call(kernel_mid, NB, [whole(MID, 128), whole(MID, 128), per_block(NQ, 256...  7.06 us
    convert_element_type x2, other arithmetic, lanes(): jnp.where(row_out | col_out, -1e+30, 0.0).astype(BF).reshape(n * W, 128)  2.92 us
  transfers between devices with their start and end apart: 10, of which 6 were waited for; matrix products, arithmetic and copies ran while one was open for 5% of the time, Pallas kernels for 18%

profile of v5, /device:TPU:10, one launch (start us, length us, event | category | flops | bytes accessed | tf_op | source)
XLA Modules:
  0.0 105.6 jit_solution(18347859623812913936)
XLA Ops:
  0.6 1.0 pad_maximum_fusion.5
  1.7 4.0 %collective-permute-start.1 = (bf16[2,24,24,128]{3,2,1,0:T(8,128)(2,1)S(1)}, bf16[2,24,24,128]{3,2,1,0:T(8,128)(2,1)S(1)}, u32[]{:S(2)}, u32[]{:S(2)}) collective-permute-start(bf16[2,24,24,128]{3,2,1,0:T(8,128)(2,1)S(1)} %pad_maximum_fusion.5), channel_id=1, source_target_pairs={{0,1},{2,3},{4,5},{6,7},{8,9},{10,11},{12,13},{14,15},{16,17},{18,... | collective-permute-start | bytes 884744 | tf_op jit(solution)/shard_map/ppermute | solution.py:267
  5.7 12.2 %collective-permute-start = (bf16[2,24,24,128]{3,2,1,0:T(8,128)(2,1)S(1)}, bf16[2,24,24,128]{3,2,1,0:T(8,128)(2,1)S(1)}, u32[]{:S(2)}, u32[]{:S(2)}) collective-permute-start(bf16[2,24,24,128]{3,2,1,0:T(8,128)(2,1)S(1)} %pad_maximum_fusion.5), channel_id=1, source_target_pairs={{1,2},{3,4},{5,6},{7,8},{9,10},{11,12},{13,14},{15,16},{17,18},{19... | collective-permute-start | bytes 884744 | tf_op jit(solution)/shard_map/ppermute | solution.py:267
  18.8 0.9 broadcast_multiply_fusion
  20.2 1.8 %select_convert_fusion.af_ref = bf16[3168,128]{1,0:T(8,128)(2,1)S(1)} fusion(s32[128]{0:T(128)S(1)} %get-tuple-element.51, s32[128]{0:T(128)S(1)} %get-tuple-element.50, s32[128]{0:T(128)S(1)} %get-tuple-element.45, s32[128]{0:T(128)S(1)} %get-tuple-element.44, s32[3168]{0:T(1024)S(1)} %iota.188, s32[3168]{0:T(1024)S(1)} %add.163, ...), kind=kLoop, calls=%fused_computation.1 | loop fusion | flops 4460544 | bytes 838656 | tf_op jit(solution)/shard_map/convert_element_type | solution.py:237
  22.0 1.1 %select_convert_fusion.1.am_ref = bf16[1728,128]{1,0:T(8,128)(2,1)S(1)} fusion(s32[128]{0:T(128)S(1)} %get-tuple-element.51, s32[128]{0:T(128)S(1)} %get-tuple-element.50, s32[128]{0:T(128)S(1)} %get-tuple-element.45, s32[128]{0:T(128)S(1)} %get-tuple-element.44, s32[1728]{0:T(1024)S(1)} %iota.175, s32[1728]{0:T(1024)S(1)} %add.152, ...), kind=kLoop, calls=%fused_computation.2 | loop fusion | flops 2433024 | bytes 458496 | tf_op jit(solution)/shard_map/convert_element_type | solution.py:237
  23.1 1.6 %collective-permute-done = bf16[2,24,24,128]{3,2,1,0:T(8,128)(2,1)S(1)} collective-permute-done((bf16[2,24,24,128]{3,2,1,0:T(8,128)(2,1)S(1)}, bf16[2,24,24,128]{3,2,1,0:T(8,128)(2,1)S(1)}, u32[]{:S(2)}, u32[]{:S(2)}) %collective-permute-start) | collective-permute-done | bytes 294944 | tf_op jit(solution)/shard_map/ppermute | solution.py:267
  24.9 1.9 %collective-permute-start.2 = (bf16[22,72,128]{2,1,0:T(8,128)(2,1)S(1)}, bf16[22,72,128]{2,1,0:T(8,128)(2,1)S(1)}, u32[]{:S(2)}, u32[]{:S(2)}) collective-permute-start(bf16[22,72,128]{2,1,0:T(8,128)(2,1)S(1)} %get-tuple-element.40), channel_id=1, source_target_pairs={{0,32},{32,64},{64,96},{96,128},{128,160},{160,192},{192,224},{224... | collective-permute-start | bytes 1216520 | tf_op jit(solution)/shard_map/ppermute | solution.py:261
  26.8 3.6 %collective-permute-start.3 = (bf16[22,72,128]{2,1,0:T(8,128)(2,1)S(1)}, bf16[22,72,128]{2,1,0:T(8,128)(2,1)S(1)}, u32[]{:S(2)}, u32[]{:S(2)}) collective-permute-start(bf16[22,72,128]{2,1,0:T(8,128)(2,1)S(1)} %get-tuple-element.41), channel_id=1, source_target_pairs={{32,0},{64,32},{96,64},{128,96},{160,128},{192,160},{224,192},{256... | collective-permute-start | bytes 1216520 | tf_op jit(solution)/shard_map/ppermute | solution.py:261
  30.7 1.9 %collective-permute-start.4 = (bf16[22,72,128]{2,1,0:T(8,128)(2,1)S(1)}, bf16[22,72,128]{2,1,0:T(8,128)(2,1)S(1)}, u32[]{:S(2)}, u32[]{:S(2)}) collective-permute-start(bf16[22,72,128]{2,1,0:T(8,128)(2,1)S(1)} %get-tuple-element.38), channel_id=1, source_target_pairs={{0,32},{32,64},{64,96},{96,128},{128,160},{160,192},{192,224},{224... | collective-permute-start | bytes 1216520 | tf_op jit(solution)/shard_map/ppermute | solution.py:261
  32.6 3.6 %collective-permute-start.5 = (bf16[22,72,128]{2,1,0:T(8,128)(2,1)S(1)}, bf16[22,72,128]{2,1,0:T(8,128)(2,1)S(1)}, u32[]{:S(2)}, u32[]{:S(2)}) collective-permute-start(bf16[22,72,128]{2,1,0:T(8,128)(2,1)S(1)} %get-tuple-element.39), channel_id=1, source_target_pairs={{32,0},{64,32},{96,64},{128,96},{160,128},{192,160},{224,192},{256... | collective-permute-start | bytes 1216520 | tf_op jit(solution)/shard_map/ppermute | solution.py:261
  36.3 3.3 %collective-permute-done.3 = bf16[22,72,128]{2,1,0:T(8,128)(2,1)S(1)} collective-permute-done((bf16[22,72,128]{2,1,0:T(8,128)(2,1)S(1)}, bf16[22,72,128]{2,1,0:T(8,128)(2,1)S(1)}, u32[]{:S(2)}, u32[]{:S(2)}) %collective-permute-start.3) | collective-permute-done | bytes 405536 | tf_op jit(solution)/shard_map/ppermute | solution.py:261
  39.6 11.5 %shard_map.75 = (bf16[3,1728,384]{2,1,0:T(8,128)(2,1)}, bf16[3,2016,384]{2,1,0:T(8,128)(2,1)}, f32[3,8,384]{2,1,0:T(8,128)S(1)}, bf16[3,384,128]{2,1,0:T(8,128)(2,1)S(1)}, bf16[3168,128]{1,0:T(8,128)(2,1)S(1)}) custom-call(s32[3]{0:T(128)S(1)} %fusion.7.start, bf16[1728,128]{1,0:T(8,128)(2,1)S(1)} %bitcast.30, bf16[3168,128]{1,0:T(8,128)(2,1)S(1)} %bitcast.35, ...), custom_call_target="tpu_custom_call" | custom-call | flops 5000000000 | bytes 14000000 | tf_op jit(solution)/shard_map/pallas_call | solution.py:187
  51.2 9.8 %shard_map.76 = (bf16[576,128]{1,0:T(8,128)(2,1)}, f32[3,8,384]{2,1,0:T(8,128)S(1)}, f32[3,128,384]{2,1,0:T(8,128)S(1)}, bf16[2,1584,128]{2,1,0:T(8,128)(2,1)S(1)}, bf16[2,1584,128]{2,1,0:T(8,128)(2,1)S(1)}) custom-call(s32[3]{0:T(128)S(1)} %fusion.7.start, bf16[3168,128]{1,0:T(8,128)(2,1)S(1)} %bitcast.36, bf16[1728,128]{1,0:T(8,128)(2,1)S(1)} %bitcast.32, ...), custom_call_target="tpu_custom_call" | custom-call | flops 5000000000 | bytes 14000000 | tf_op jit(solution)/shard_map/pallas_call | solution.py:199
  61.0 4.1 %collective-permute-start.6 = (bf16[2,1584,128]{2,1,0:T(8,128)(2,1)S(1)}, bf16[2,1584,128]{2,1,0:T(8,128)(2,1)S(1)}, u32[]{:S(2)}, u32[]{:S(2)}) collective-permute-start(bf16[2,1584,128]{2,1,0:T(8,128)(2,1)S(1)} %get-tuple-element.26), channel_id=1, source_target_pairs={{32,0},{64,32},{96,64},{128,96},{160,128},{192,160},{224,192},{256... | collective-permute-start | bytes 2433032 | tf_op jit(solution)/shard_map/ppermute | solution.py:261
  65.1 2.4 %collective-permute-start.7 = (bf16[2,1584,128]{2,1,0:T(8,128)(2,1)S(1)}, bf16[2,1584,128]{2,1,0:T(8,128)(2,1)S(1)}, u32[]{:S(2)}, u32[]{:S(2)}) collective-permute-start(bf16[2,1584,128]{2,1,0:T(8,128)(2,1)S(1)} %get-tuple-element.27), channel_id=1, source_target_pairs={{0,32},{32,64},{64,96},{96,128},{128,160},{160,192},{192,224},{224... | collective-permute-start | bytes 2433032 | tf_op jit(solution)/shard_map/ppermute | solution.py:261
  67.5 7.1 %shard_map.77 = (bf16[576,128]{1,0:T(8,128)(2,1)}, f32[2,1728,128]{2,1,0:T(8,128)S(1)}) custom-call(s32[3]{0:T(128)S(1)} %fusion.7.start, bf16[1728,128]{1,0:T(8,128)(2,1)S(1)} %bitcast.31, bf16[1728,128]{1,0:T(8,128)(2,1)S(1)} %bitcast.33, bf16[3,384,256]{2,1,0:T(8,128)(2,1)S(1)} %pad_maximum_fusion.2.q_ref, ...), custom_call_target="tpu_custom_call" | custom-call | flops 5000000000 | bytes 14000000 | tf_op jit(solution)/shard_map/pallas_call | solution.py:212
  74.6 4.6 %collective-permute-done.6 = bf16[2,1584,128]{2,1,0:T(8,128)(2,1)S(1)} collective-permute-done((bf16[2,1584,128]{2,1,0:T(8,128)(2,1)S(1)}, bf16[2,1584,128]{2,1,0:T(8,128)(2,1)S(1)}, u32[]{:S(2)}, u32[]{:S(2)}) %collective-permute-start.6) | collective-permute-done | bytes 811040 | tf_op jit(solution)/shard_map/ppermute | solution.py:261
  79.2 6.8 %collective-permute-done.7 = bf16[2,1584,128]{2,1,0:T(8,128)(2,1)S(1)} collective-permute-done((bf16[2,1584,128]{2,1,0:T(8,128)(2,1)S(1)}, bf16[2,1584,128]{2,1,0:T(8,128)(2,1)S(1)}, u32[]{:S(2)}, u32[]{:S(2)}) %collective-permute-start.7) | collective-permute-done | bytes 811040 | tf_op jit(solution)/shard_map/ppermute | solution.py:261
  86.4 1.9 %collective-permute-start.8 = (bf16[2,24,24,128]{3,2,1,0:T(8,128)(2,1)S(1)}, bf16[2,24,24,128]{3,2,1,0:T(8,128)(2,1)S(1)}, u32[]{:S(2)}, u32[]{:S(2)}) collective-permute-start(bf16[2,24,24,128]{3,2,1,0:T(8,128)(2,1)S(1)} %get-tuple-element.32), channel_id=1, source_target_pairs={{0,1},{2,3},{4,5},{6,7},{8,9},{10,11},{12,13},{14,15},{16,17},{18,... | collective-permute-start | bytes 884744 | tf_op jit(solution)/shard_map/ppermute | solution.py:267
  88.3 9.8 %collective-permute-start.9 = (bf16[2,24,24,128]{3,2,1,0:T(8,128)(2,1)S(1)}, bf16[2,24,24,128]{3,2,1,0:T(8,128)(2,1)S(1)}, u32[]{:S(2)}, u32[]{:S(2)}) collective-permute-start(bf16[2,24,24,128]{3,2,1,0:T(8,128)(2,1)S(1)} %get-tuple-element.33), channel_id=1, source_target_pairs={{1,2},{3,4},{5,6},{7,8},{9,10},{11,12},{13,14},{15,16},{17,18},{19... | collective-permute-start | bytes 884744 | tf_op jit(solution)/shard_map/ppermute | solution.py:267
  98.1 3.0 %collective-permute-done.8 = bf16[2,24,24,128]{3,2,1,0:T(8,128)(2,1)S(1)} collective-permute-done((bf16[2,24,24,128]{3,2,1,0:T(8,128)(2,1)S(1)}, bf16[2,24,24,128]{3,2,1,0:T(8,128)(2,1)S(1)}, u32[]{:S(2)}, u32[]{:S(2)}) %collective-permute-start.8) | collective-permute-done | bytes 294944 | tf_op jit(solution)/shard_map/ppermute | solution.py:267
  101.1 3.7 %collective-permute-done.9 = bf16[2,24,24,128]{3,2,1,0:T(8,128)(2,1)S(1)} collective-permute-done((bf16[2,24,24,128]{3,2,1,0:T(8,128)(2,1)S(1)}, bf16[2,24,24,128]{3,2,1,0:T(8,128)(2,1)S(1)}, u32[]{:S(2)}, u32[]{:S(2)}) %collective-permute-start.9) | collective-permute-done | bytes 294944 | tf_op jit(solution)/shard_map/ppermute | solution.py:267
  104.8 0.8 fusion.6
  (46 shorter events, 2.0 us)
Async XLA Ops:
  0.6 19.4 %copy-start.2 = (bf16[24,24,128]{2,1,0:T(8,128)(2,1)S(1)}, bf16[24,24,128]{2,1,0:T(8,128)(2,1)}, u32[]{:S(2)}) copy-start(bf16[24,24,128]{2,1,0:T(8,128)(2,1)} %param.7) | copy-start | bytes 442372
  1.7 21.4 %collective-permute-start.1 = (bf16[2,24,24,128]{3,2,1,0:T(8,128)(2,1)S(1)}, bf16[2,24,24,128]{3,2,1,0:T(8,128)(2,1)S(1)}, u32[]{:S(2)}, u32[]{:S(2)}) collective-permute-start(bf16[2,24,24,128]{3,2,1,0:T(8,128)(2,1)S(1)} %pad_maximum_fusion.5), channel_id=1, source_target_pairs={{0,1},{2,3},{4,5},{6,7},{8,9},{10,11},{12,13},{14,15},{16,17},{18,... | collective-permute-start | bytes 884744 | tf_op jit(solution)/shard_map/ppermute | solution.py:267
  5.7 19.0 %collective-permute-start = (bf16[2,24,24,128]{3,2,1,0:T(8,128)(2,1)S(1)}, bf16[2,24,24,128]{3,2,1,0:T(8,128)(2,1)S(1)}, u32[]{:S(2)}, u32[]{:S(2)}) collective-permute-start(bf16[2,24,24,128]{3,2,1,0:T(8,128)(2,1)S(1)} %pad_maximum_fusion.5), channel_id=1, source_target_pairs={{1,2},{3,4},{5,6},{7,8},{9,10},{11,12},{13,14},{15,16},{17,18},{19... | collective-permute-start | bytes 884744 | tf_op jit(solution)/shard_map/ppermute | solution.py:267
  20.1 4.7 %copy-start = (bf16[24,24,128]{2,1,0:T(8,128)(2,1)S(1)}, bf16[24,24,128]{2,1,0:T(8,128)(2,1)}, u32[]{:S(2)}) copy-start(bf16[24,24,128]{2,1,0:T(8,128)(2,1)} %param.5) | copy-start | bytes 442372
  23.1 7.4 %copy-start.1 = (bf16[24,24,128]{2,1,0:T(8,128)(2,1)S(1)}, bf16[24,24,128]{2,1,0:T(8,128)(2,1)}, u32[]{:S(2)}) copy-start(bf16[24,24,128]{2,1,0:T(8,128)(2,1)} %param.6) | copy-start | bytes 442372
  24.9 11.4 %collective-permute-start.2 = (bf16[22,72,128]{2,1,0:T(8,128)(2,1)S(1)}, bf16[22,72,128]{2,1,0:T(8,128)(2,1)S(1)}, u32[]{:S(2)}, u32[]{:S(2)}) collective-permute-start(bf16[22,72,128]{2,1,0:T(8,128)(2,1)S(1)} %get-tuple-element.40), channel_id=1, source_target_pairs={{0,32},{32,64},{64,96},{96,128},{128,160},{160,192},{192,224},{224... | collective-permute-start | bytes 1216520 | tf_op jit(solution)/shard_map/ppermute | solution.py:261
  26.8 12.7 %collective-permute-start.3 = (bf16[22,72,128]{2,1,0:T(8,128)(2,1)S(1)}, bf16[22,72,128]{2,1,0:T(8,128)(2,1)S(1)}, u32[]{:S(2)}, u32[]{:S(2)}) collective-permute-start(bf16[22,72,128]{2,1,0:T(8,128)(2,1)S(1)} %get-tuple-element.41), channel_id=1, source_target_pairs={{32,0},{64,32},{96,64},{128,96},{160,128},{192,160},{224,192},{256... | collective-permute-start | bytes 1216520 | tf_op jit(solution)/shard_map/ppermute | solution.py:261
  30.7 20.5 %collective-permute-start.4 = (bf16[22,72,128]{2,1,0:T(8,128)(2,1)S(1)}, bf16[22,72,128]{2,1,0:T(8,128)(2,1)S(1)}, u32[]{:S(2)}, u32[]{:S(2)}) collective-permute-start(bf16[22,72,128]{2,1,0:T(8,128)(2,1)S(1)} %get-tuple-element.38), channel_id=1, source_target_pairs={{0,32},{32,64},{64,96},{96,128},{128,160},{160,192},{192,224},{224... | collective-permute-start | bytes 1216520 | tf_op jit(solution)/shard_map/ppermute | solution.py:261
  32.6 18.5 %collective-permute-start.5 = (bf16[22,72,128]{2,1,0:T(8,128)(2,1)S(1)}, bf16[22,72,128]{2,1,0:T(8,128)(2,1)S(1)}, u32[]{:S(2)}, u32[]{:S(2)}) collective-permute-start(bf16[22,72,128]{2,1,0:T(8,128)(2,1)S(1)} %get-tuple-element.39), channel_id=1, source_target_pairs={{32,0},{64,32},{96,64},{128,96},{160,128},{192,160},{224,192},{256... | collective-permute-start | bytes 1216520 | tf_op jit(solution)/shard_map/ppermute | solution.py:261
  61.0 18.2 %collective-permute-start.6 = (bf16[2,1584,128]{2,1,0:T(8,128)(2,1)S(1)}, bf16[2,1584,128]{2,1,0:T(8,128)(2,1)S(1)}, u32[]{:S(2)}, u32[]{:S(2)}) collective-permute-start(bf16[2,1584,128]{2,1,0:T(8,128)(2,1)S(1)} %get-tuple-element.26), channel_id=1, source_target_pairs={{32,0},{64,32},{96,64},{128,96},{160,128},{192,160},{224,192},{256... | collective-permute-start | bytes 2433032 | tf_op jit(solution)/shard_map/ppermute | solution.py:261
  65.1 20.9 %collective-permute-start.7 = (bf16[2,1584,128]{2,1,0:T(8,128)(2,1)S(1)}, bf16[2,1584,128]{2,1,0:T(8,128)(2,1)S(1)}, u32[]{:S(2)}, u32[]{:S(2)}) collective-permute-start(bf16[2,1584,128]{2,1,0:T(8,128)(2,1)S(1)} %get-tuple-element.27), channel_id=1, source_target_pairs={{0,32},{32,64},{64,96},{96,128},{128,160},{160,192},{192,224},{224... | collective-permute-start | bytes 2433032 | tf_op jit(solution)/shard_map/ppermute | solution.py:261
  86.4 14.7 %collective-permute-start.8 = (bf16[2,24,24,128]{3,2,1,0:T(8,128)(2,1)S(1)}, bf16[2,24,24,128]{3,2,1,0:T(8,128)(2,1)S(1)}, u32[]{:S(2)}, u32[]{:S(2)}) collective-permute-start(bf16[2,24,24,128]{3,2,1,0:T(8,128)(2,1)S(1)} %get-tuple-element.32), channel_id=1, source_target_pairs={{0,1},{2,3},{4,5},{6,7},{8,9},{10,11},{12,13},{14,15},{16,17},{18,... | collective-permute-start | bytes 884744 | tf_op jit(solution)/shard_map/ppermute | solution.py:267
  88.3 16.5 %collective-permute-start.9 = (bf16[2,24,24,128]{3,2,1,0:T(8,128)(2,1)S(1)}, bf16[2,24,24,128]{3,2,1,0:T(8,128)(2,1)S(1)}, u32[]{:S(2)}, u32[]{:S(2)}) collective-permute-start(bf16[2,24,24,128]{3,2,1,0:T(8,128)(2,1)S(1)} %get-tuple-element.33), channel_id=1, source_target_pairs={{1,2},{3,4},{5,6},{7,8},{9,10},{11,12},{13,14},{15,16},{17,18},{19... | collective-permute-start | bytes 884744 | tf_op jit(solution)/shard_map/ppermute | solution.py:267

commit v6 on v5

--- a/solution.py
+++ b/solution.py
@@ -28,7 +28,7 @@
     return pl.multiple_of(start[b] * W, 64)
 
 
-def kernel_a(start, km_ref, kf_ref, am_ref, af_ref, q_ref, g_ref, pm_ref, pf_ref, linv_ref, gs_ref, vf_ref, s_scr, m_scr, acc):
+def kernel_a(start, km_ref, kf_ref, am_ref, af_ref, q_ref, g_ref, pm_ref, pf_ref, linv_ref, gs_ref, north_ref, south_ref, s_scr, m_scr, acc):
     b = pl.program_id(0)
     here = lax.rem(b, 2)
     base = far_base(start, jnp.minimum(b, NB - 1))
@@ -99,7 +99,8 @@
 
     @pl.when(b == NB)
     def _():
-        vf_ref[...] = acc[...].astype(BF)
+        north_ref[...] = acc[:EDGE, :].astype(BF)
+        south_ref[...] = acc[EDGE:, :].astype(BF)
 
 
 def score_grads(p, v, gs, corr):
@@ -107,15 +108,13 @@
     return (p.astype(F32) * (gw - corr)).astype(BF)
 
 
-def kernel_far(start, kf_ref, vm_ref, vf_ref, q_ref, gs_ref, pm_ref, pf_ref, linv_ref, dvf_ref, o_ref, corr_ref, dqt_ref, north_ref, south_ref, acc):
+def kernel_far(start, vm_ref, vf_ref, q_ref, gs_ref, pm_ref, pf_ref, linv_ref, o_ref, corr_ref, ds_ref, north_ref, south_ref, acc):
     b = pl.program_id(0)
     rows = pl.ds(far_base(start, b), FAR)
 
     @pl.when(b == 0)
     def _():
         acc[...] = jnp.zeros_like(acc)
-        north_ref[1] = dvf_ref[:EDGE, :]
-        south_ref[1] = dvf_ref[EDGE:, :]
 
     gs = gs_ref[0]
     ot = lax.dot_general(vm_ref[...], pm_ref[0], TN, preferred_element_type=F32)
@@ -127,16 +126,16 @@
     corr = jnp.transpose(jnp.broadcast_to(row, (NQ, 128)))
     corr_ref[0] = corr[:8]
     ds = score_grads(pf_ref[0], vf_ref[rows, :], gs, corr[:1])
+    ds_ref[0] = ds
     acc[rows, :] += jnp.dot(ds, q_ref[0][:, :128], preferred_element_type=F32)
-    dqt_ref[0] = lax.dot_general(kf_ref[rows, :], ds, TN, preferred_element_type=F32)
 
     @pl.when(b == NB - 1)
     def _():
-        north_ref[0] = acc[:EDGE, :].astype(BF)
-        south_ref[0] = acc[EDGE:, :].astype(BF)
-
-
-def kernel_mid(start, km_ref, vm_ref, q_ref, gs_ref, pm_ref, corr_ref, dqt_ref, dq_ref, grads_ref):
+        north_ref[...] = acc[:EDGE, :].astype(BF)
+        south_ref[...] = acc[EDGE:, :].astype(BF)
+
+
+def kernel_mid(start, km_ref, kf_ref, vm_ref, q_ref, gs_ref, pm_ref, corr_ref, ds_ref, dq_ref, grads_ref):
     b = pl.program_id(0)
 
     @pl.when(b == 0)
@@ -146,7 +145,8 @@
     gs = gs_ref[0]
     ds = score_grads(pm_ref[0], vm_ref[...], gs, corr_ref[0][:1])
     grads_ref[0] += jnp.dot(ds, q_ref[0][:, :128], preferred_element_type=F32)
-    dqt = dqt_ref[0] + lax.dot_general(km_ref[...], ds, TN, preferred_element_type=F32)
+    dqt = lax.dot_general(km_ref[...], ds, TN, preferred_element_type=F32)
+    dqt += lax.dot_general(kf_ref[pl.ds(far_base(start, b), FAR), :], ds_ref[0], TN, preferred_element_type=F32)
     grads_ref[1] += jnp.dot(pm_ref[0], gs, preferred_element_type=F32)
     lane = lax.broadcasted_iota(jnp.int32, (NQ // 2, 128), 1)
     dq = jnp.transpose(dqt * 0.125)
@@ -176,7 +176,7 @@
             num_scalar_prefetch=1, grid=(grid,), in_specs=in_specs, out_specs=out_specs, scratch_shapes=scratch
         ),
         out_shape=out_shape,
-        compiler_params=pltpu.CompilerParams(vmem_limit_bytes=48 << 20),
+        compiler_params=pltpu.CompilerParams(vmem_limit_bytes=30 << 20),
         cost_estimate=pl.CostEstimate(flops=flops, bytes_accessed=14_000_000, transcendentals=0),
     )
 
@@ -188,37 +188,37 @@
         kernel_a,
         NB + 1,
         [whole(MID, 128), whole(2 * EDGE, 128)] * 2 + [per_block(NQ, 256, at=ahead), per_block(NQ, 128, at=behind)],
-        [per_block(*x, at=behind) for x in ((MID, NQ), (FAR, NQ), (8, NQ), (NQ, 128))] + [whole(2 * EDGE, 128)],
-        [sds(NB, MID, NQ), sds(NB, FAR, NQ), sds(NB, 8, NQ, dtype=F32), sds(NB, NQ, 128), sds(2 * EDGE, 128)],
+        [per_block(*x, at=behind) for x in ((MID, NQ), (FAR, NQ), (8, NQ), (NQ, 128))] + [whole(EDGE, 128)] * 2,
+        [sds(NB, MID, NQ), sds(NB, FAR, NQ), sds(NB, 8, NQ, dtype=F32), sds(NB, NQ, 128)] + [sds(EDGE, 128)] * 2,
         [pltpu.VMEM((2, NK, NQ), F32), pltpu.VMEM((8, NQ), F32), pltpu.VMEM((2 * EDGE, 128), F32)],
         5_000_000_000,
     )(start, km, kf, am, af, q, g)
 
 
-def run_far(start, kf, vm, vf, q, gs, pm, pf, linv, dvf):
+def run_far(start, vm, vf, q, gs, pm, pf, linv):
     return call(
         kernel_far,
         NB,
-        [whole(2 * EDGE, 128), whole(MID, 128), whole(2 * EDGE, 128), per_block(NQ, 256), per_block(NQ, 128)]
-        + [per_block(MID, NQ), per_block(FAR, NQ), per_block(8, NQ), whole(2 * EDGE, 128)],
-        [rows_of_block(), per_block(8, NQ), per_block(128, NQ), whole(2, EDGE, 128), whole(2, EDGE, 128)],
-        [sds(T * T, 128), sds(NB, 8, NQ, dtype=F32), sds(NB, 128, NQ, dtype=F32), sds(2, EDGE, 128), sds(2, EDGE, 128)],
+        [whole(MID, 128), whole(2 * EDGE, 128), per_block(NQ, 256), per_block(NQ, 128)]
+        + [per_block(MID, NQ), per_block(FAR, NQ), per_block(8, NQ)],
+        [rows_of_block(), per_block(8, NQ), per_block(FAR, NQ)] + [whole(EDGE, 128)] * 2,
+        [sds(T * T, 128), sds(NB, 8, NQ, dtype=F32), sds(NB, FAR, NQ)] + [sds(EDGE, 128)] * 2,
         [pltpu.VMEM((2 * EDGE, 128), F32)],
         5_000_000_000,
-    )(start, kf, vm, vf, q, gs, pm, pf, linv, dvf)
-
-
-def run_mid(start, km, vm, q, gs, pm, corr, dqt):
+    )(start, vm, vf, q, gs, pm, pf, linv)
+
+
+def run_mid(start, km, kf, vm, q, gs, pm, corr, ds):
     return call(
         kernel_mid,
         NB,
-        [whole(MID, 128), whole(MID, 128), per_block(NQ, 256), per_block(NQ, 128), per_block(MID, NQ)]
-        + [per_block(8, NQ), per_block(128, NQ)],
+        [whole(MID, 128), whole(2 * EDGE, 128), whole(MID, 128), per_block(NQ, 256), per_block(NQ, 128)]
+        + [per_block(MID, NQ), per_block(8, NQ), per_block(FAR, NQ)],
         [rows_of_block(), whole(2, MID, 128)],
         [sds(T * T, 128), sds(2, MID, 128, dtype=F32)],
         [],
         5_000_000_000,
-    )(start, km, vm, q, gs, pm, corr, dqt)
+    )(start, km, kf, vm, q, gs, pm, corr, ds)
 
 
 def tables(first_row, height):
@@ -271,6 +271,13 @@
     return jnp.concatenate([shift(mid[T - R :], 1), shift(mid[:R], -1)], axis=0).reshape(2 * EDGE, 128)
 
 
+def from_lat(north, south):
+    from_south = shift(north, -1).reshape(R, W, 128).astype(F32)
+    from_north = shift(south, 1).reshape(R, W, 128).astype(F32)
+    pad = ((T - R, 0), (0, 0), (0, 0)), ((0, T - R), (0, 0), (0, 0))
+    return jnp.pad(from_south, pad[0]) + jnp.pad(from_north, pad[1])
+
+
 def body(queries, keys, values, out_grad):
     height = T * lax.axis_size("lat")
     even = lax.axis_index("lon") % 2 == 0
@@ -289,15 +296,12 @@
     vf = far_rows(vm)
     km = km.reshape(MID, 128)
     vm = vm.reshape(MID, 128)
-    pm, pf, linv, gs, dvf = run_a(start, km, kf, am, af, q, g)
-    attended, corr, dqt, north, south = run_far(start, kf, vm, vf, q, gs, pm, pf, linv, dvf)
-    from_south = shift(north, -1).reshape(2, R, W, 128)
-    from_north = shift(south, 1).reshape(2, R, W, 128)
-    grad_queries, mid = run_mid(start, km, vm, q, gs, pm, corr, dqt)
-    none = (0, 0)
-    mid = mid.reshape(2, T, W, 128)
-    mid = mid + jnp.pad(from_south.astype(F32), (none, (T - R, 0), none, none))
-    mid = mid + jnp.pad(from_north.astype(F32), (none, (0, T - R), none, none))
+    pm, pf, linv, gs, *dvf = run_a(start, km, kf, am, af, q, g)
+    dvf = from_lat(*dvf)
+    attended, corr, ds, *dkf = run_far(start, vm, vf, q, gs, pm, pf, linv)
+    dkf = from_lat(*dkf)
+    grad_queries, mid = run_mid(start, km, kf, vm, q, gs, pm, corr, ds)
+    mid = mid.reshape(2, T, W, 128) + jnp.stack([dkf, dvf])
     west = mid[:, :, :T].astype(BF)
     east = mid[:, :, 2 * T :].astype(BF)
     near = swap(jnp.where(even, east, west), 0)

time: 106 us -> 102 us (0.962)
  starting transfers between devices: 45.6 us -> 52.1 us
  waiting for transfers between devices: 22.9 us -> 16.6 us
  Pallas kernels: 28.3 us -> 24 us
    ppermute x6 -> x8, starting transfers between devices: 17.6 us -> 24.1 us  [shift(): lax.ppermute(x, 'lat', [(i, i + by) for i in range(n) if 0 <= i + by < n])]
    ppermute x6 -> x8, waiting for transfers between devices: 14.7 us -> 8.27 us  [shift(): lax.ppermute(x, 'lat', [(i, i + by) for i in range(n) if 0 <= i + by < n])]
    pallas_call x2, Pallas kernels: 16.8 us -> 14.2 us  [the longest x1 7.5 us: run_far(): call(kernel_far, NB, [whole(MID, 128), whole(2 * EDGE, 128), per_block(NQ...]
    pallas_call x1, Pallas kernels: 11.5 us -> 9.86 us  [run_a(): call(kernel_a, NB + 1, [whole(MID, 128), whole(2 * EDGE, 128)] * 2 + [per...]
  transfers between devices with their start and end apart: 10 -> 12, of which waited for: 6 -> 5; matrix products, arithmetic and copies ran while one was open for 5% -> 5% of each run, Pallas kernels for 18% -> 16%
where the time goes in v6:
time: 102 us
  starting transfers between devices  52.1 us (51%)
  Pallas kernels  24 us (24%)
  waiting for transfers between devices  16.6 us (16%)
  other arithmetic  6.95 us (7%)
  between operations  1.09 us (1%)
    ppermute x4, starting transfers between devices, swap(): return lax.ppermute(x, 'lon', pairs + [(b, a) for a, b in pairs])  28 us
    ppermute x8, starting transfers between devices, shift(): lax.ppermute(x, 'lat', [(i, i + by) for i in range(n) if 0 <= i + by < n])  24.1 us
    pallas_call x1, Pallas kernels, run_a(): call(kernel_a, NB + 1, [whole(MID, 128), whole(2 * EDGE, 128)] * 2 + [per...  9.86 us
    ppermute x4, waiting for transfers between devices, swap(): return lax.ppermute(x, 'lon', pairs + [(b, a) for a, b in pairs])  8.38 us
    ppermute x8, waiting for transfers between devices, shift(): lax.ppermute(x, 'lat', [(i, i + by) for i in range(n) if 0 <= i + by < n])  8.27 us
    pallas_call x1, Pallas kernels, run_far(): call(kernel_far, NB, [whole(MID, 128), whole(2 * EDGE, 128), per_block(NQ...  7.5 us
    pallas_call x1, Pallas kernels, run_mid(): call(kernel_mid, NB, [whole(MID, 128), whole(2 * EDGE, 128), whole(MID, 1...  6.68 us
    convert_element_type x2, other arithmetic, lanes(): jnp.where(row_out | col_out, -1e+30, 0.0).astype(BF).reshape(n * W, 128)  2.92 us
  transfers between devices with their start and end apart: 12, of which 5 were waited for; matrix products, arithmetic and copies ran while one was open for 5% of the time, Pallas kernels for 16%

profile of v6, /device:TPU:10, one launch (start us, length us, event | category | flops | bytes accessed | tf_op | source)
XLA Modules:
  0.0 101.6 jit_solution(13162068868560198102)
XLA Ops:
  0.6 1.0 pad_maximum_fusion.5
  1.6 4.0 %collective-permute-start.1 = (bf16[2,24,24,128]{3,2,1,0:T(8,128)(2,1)S(1)}, bf16[2,24,24,128]{3,2,1,0:T(8,128)(2,1)S(1)}, u32[]{:S(2)}, u32[]{:S(2)}) collective-permute-start(bf16[2,24,24,128]{3,2,1,0:T(8,128)(2,1)S(1)} %pad_maximum_fusion.5), channel_id=1, source_target_pairs={{0,1},{2,3},{4,5},{6,7},{8,9},{10,11},{12,13},{14,15},{16,17},{18,... | collective-permute-start | bytes 884744 | tf_op jit(solution)/shard_map/ppermute | solution.py:267
  5.7 12.2 %collective-permute-start = (bf16[2,24,24,128]{3,2,1,0:T(8,128)(2,1)S(1)}, bf16[2,24,24,128]{3,2,1,0:T(8,128)(2,1)S(1)}, u32[]{:S(2)}, u32[]{:S(2)}) collective-permute-start(bf16[2,24,24,128]{3,2,1,0:T(8,128)(2,1)S(1)} %pad_maximum_fusion.5), channel_id=1, source_target_pairs={{1,2},{3,4},{5,6},{7,8},{9,10},{11,12},{13,14},{15,16},{17,18},{19... | collective-permute-start | bytes 884744 | tf_op jit(solution)/shard_map/ppermute | solution.py:267
  18.8 0.9 broadcast_multiply_fusion
  19.7 1.1 %select_convert_fusion.1.am_ref = bf16[1728,128]{1,0:T(8,128)(2,1)S(1)} fusion(s32[128]{0:T(128)S(1)} %get-tuple-element.55, s32[128]{0:T(128)S(1)} %get-tuple-element.54, s32[128]{0:T(128)S(1)} %get-tuple-element.47, s32[128]{0:T(128)S(1)} %get-tuple-element.46, s32[1728]{0:T(1024)S(1)} %iota.175, s32[1728]{0:T(1024)S(1)} %add.159, ...), kind=kLoop, calls=%fused_computation.4 | loop fusion | flops 2433024 | bytes 458496 | tf_op jit(solution)/shard_map/convert_element_type | solution.py:237
  20.8 1.8 %select_convert_fusion.af_ref = bf16[3168,128]{1,0:T(8,128)(2,1)S(1)} fusion(s32[128]{0:T(128)S(1)} %get-tuple-element.55, s32[128]{0:T(128)S(1)} %get-tuple-element.54, s32[128]{0:T(128)S(1)} %get-tuple-element.47, s32[128]{0:T(128)S(1)} %get-tuple-element.46, s32[3168]{0:T(1024)S(1)} %iota.188, s32[3168]{0:T(1024)S(1)} %add.170, ...), kind=kLoop, calls=%fused_computation.1 | loop fusion | flops 4460544 | bytes 838656 | tf_op jit(solution)/shard_map/convert_element_type | solution.py:237
  22.9 1.7 %collective-permute-done = bf16[2,24,24,128]{3,2,1,0:T(8,128)(2,1)S(1)} collective-permute-done((bf16[2,24,24,128]{3,2,1,0:T(8,128)(2,1)S(1)}, bf16[2,24,24,128]{3,2,1,0:T(8,128)(2,1)S(1)}, u32[]{:S(2)}, u32[]{:S(2)}) %collective-permute-start) | collective-permute-done | bytes 294944 | tf_op jit(solution)/shard_map/ppermute | solution.py:267
  24.9 1.9 %collective-permute-start.4 = (bf16[22,72,128]{2,1,0:T(8,128)(2,1)S(1)}, bf16[22,72,128]{2,1,0:T(8,128)(2,1)S(1)}, u32[]{:S(2)}, u32[]{:S(2)}) collective-permute-start(bf16[22,72,128]{2,1,0:T(8,128)(2,1)S(1)} %get-tuple-element.40), channel_id=1, source_target_pairs={{0,32},{32,64},{64,96},{96,128},{128,160},{160,192},{192,224},{224... | collective-permute-start | bytes 1216520 | tf_op jit(solution)/shard_map/ppermute | solution.py:261
  26.9 3.6 %collective-permute-start.5 = (bf16[22,72,128]{2,1,0:T(8,128)(2,1)S(1)}, bf16[22,72,128]{2,1,0:T(8,128)(2,1)S(1)}, u32[]{:S(2)}, u32[]{:S(2)}) collective-permute-start(bf16[22,72,128]{2,1,0:T(8,128)(2,1)S(1)} %get-tuple-element.41), channel_id=1, source_target_pairs={{32,0},{64,32},{96,64},{128,96},{160,128},{192,160},{224,192},{256... | collective-permute-start | bytes 1216520 | tf_op jit(solution)/shard_map/ppermute | solution.py:261
  30.8 1.9 %collective-permute-start.2 = (bf16[22,72,128]{2,1,0:T(8,128)(2,1)S(1)}, bf16[22,72,128]{2,1,0:T(8,128)(2,1)S(1)}, u32[]{:S(2)}, u32[]{:S(2)}) collective-permute-start(bf16[22,72,128]{2,1,0:T(8,128)(2,1)S(1)} %get-tuple-element.42), channel_id=1, source_target_pairs={{0,32},{32,64},{64,96},{96,128},{128,160},{160,192},{192,224},{224... | collective-permute-start | bytes 1216520 | tf_op jit(solution)/shard_map/ppermute | solution.py:261
  32.8 3.6 %collective-permute-start.3 = (bf16[22,72,128]{2,1,0:T(8,128)(2,1)S(1)}, bf16[22,72,128]{2,1,0:T(8,128)(2,1)S(1)}, u32[]{:S(2)}, u32[]{:S(2)}) collective-permute-start(bf16[22,72,128]{2,1,0:T(8,128)(2,1)S(1)} %get-tuple-element.43), channel_id=1, source_target_pairs={{32,0},{64,32},{96,64},{128,96},{160,128},{192,160},{224,192},{256... | collective-permute-start | bytes 1216520 | tf_op jit(solution)/shard_map/ppermute | solution.py:261
  36.4 3.1 %collective-permute-done.5 = bf16[22,72,128]{2,1,0:T(8,128)(2,1)S(1)} collective-permute-done((bf16[22,72,128]{2,1,0:T(8,128)(2,1)S(1)}, bf16[22,72,128]{2,1,0:T(8,128)(2,1)S(1)}, u32[]{:S(2)}, u32[]{:S(2)}) %collective-permute-start.5) | collective-permute-done | bytes 405536 | tf_op jit(solution)/shard_map/ppermute | solution.py:261
  39.6 9.9 %shard_map.75 = (bf16[3,1728,384]{2,1,0:T(8,128)(2,1)S(1)}, bf16[3,2016,384]{2,1,0:T(8,128)(2,1)S(1)}, f32[3,8,384]{2,1,0:T(8,128)S(1)}, bf16[3,384,128]{2,1,0:T...) custom-call(s32[3]{0:T(128)S(1)} %fusion.7.start, bf16[1728,128]{1,0:T(8,128)(2,1)S(1)} %bitcast.38, ...), custom_call_target="tpu_custom_call" | custom-call | flops 5000000000 | bytes 14000000 | tf_op jit(solution)/shard_map/pallas_call | solution.py:187
  49.5 7.5 %shard_map.76 = (bf16[576,128]{1,0:T(8,128)(2,1)}, f32[3,8,384]{2,1,0:T(8,128)S(1)}, bf16[3,2016,384]{2,1,0:T(8,128)(2,1)S(1)}, bf16[1584,128]{1,0:T(8,128)(2,1)S(1)}, bf16[1584,128]{1,0:T(8,128)(2,1)S(1)}) custom-call(s32[3]{0:T(128)S(1)} %fusion.7.start, bf16[1728,128]{1,0:T(8,128)(2,1)S(1)} %bitcast.36, bf16[3168,128]{1,0:T(8,128)(2,1)S(1)} %bitcast.43, ...), custom_call_target="tpu_custom_call" | custom-call | flops 5000000000 | bytes 14000000 | tf_op jit(solution)/shard_map/pallas_call | solution.py:199
  57.0 4.1 %collective-permute-start.6 = (bf16[1584,128]{1,0:T(8,128)(2,1)S(1)}, bf16[1584,128]{1,0:T(8,128)(2,1)S(1)}, u32[]{:S(2)}, u32[]{:S(2)}) collective-permute-start(bf16[1584,128]{1,0:T(8,128)(2,1)S(1)} %get-tuple-element.26), channel_id=1, source_target_pairs={{32,0},{64,32},{96,64},{128,96},{160,128},{192,160},{224,192},{256... | collective-permute-start | bytes 1216520 | tf_op jit(solution)/shard_map/ppermute | solution.py:261
  61.1 2.4 %collective-permute-start.7 = (bf16[1584,128]{1,0:T(8,128)(2,1)S(1)}, bf16[1584,128]{1,0:T(8,128)(2,1)S(1)}, u32[]{:S(2)}, u32[]{:S(2)}) collective-permute-start(bf16[1584,128]{1,0:T(8,128)(2,1)S(1)} %get-tuple-element.27), channel_id=1, source_target_pairs={{0,32},{32,64},{64,96},{96,128},{128,160},{160,192},{192,224},{224... | collective-permute-start | bytes 1216520 | tf_op jit(solution)/shard_map/ppermute | solution.py:261
  63.5 3.2 %collective-permute-start.8 = (bf16[1584,128]{1,0:T(8,128)(2,1)S(1)}, bf16[1584,128]{1,0:T(8,128)(2,1)S(1)}, u32[]{:S(2)}, u32[]{:S(2)}) collective-permute-start(bf16[1584,128]{1,0:T(8,128)(2,1)S(1)} %get-tuple-element.28), channel_id=1, source_target_pairs={{32,0},{64,32},{96,64},{128,96},{160,128},{192,160},{224,192},{256... | collective-permute-start | bytes 1216520 | tf_op jit(solution)/shard_map/ppermute | solution.py:261
  66.7 3.3 %collective-permute-start.9 = (bf16[1584,128]{1,0:T(8,128)(2,1)S(1)}, bf16[1584,128]{1,0:T(8,128)(2,1)S(1)}, u32[]{:S(2)}, u32[]{:S(2)}) collective-permute-start(bf16[1584,128]{1,0:T(8,128)(2,1)S(1)} %get-tuple-element.29), channel_id=1, source_target_pairs={{0,32},{32,64},{64,96},{96,128},{128,160},{160,192},{192,224},{224... | collective-permute-start | bytes 1216520 | tf_op jit(solution)/shard_map/ppermute | solution.py:261
  70.0 6.7 %shard_map.77 = (bf16[576,128]{1,0:T(8,128)(2,1)}, f32[2,1728,128]{2,1,0:T(8,128)S(1)}) custom-call(s32[3]{0:T(128)S(1)} %fusion.7.start, bf16[1728,128]{1,0:T(8,128)(2,1)S(1)} %bitcast.39, bf16[3168,128]{1,0:T(8,128)(2,1)S(1)} %bitcast.42, bf16[1728,128]{1,0:T(8,128)(2,1)S(1)} %bitcast.37, bf16[3,384,256]{2,1,0:T(8,128)(2,1)S(1)} %pad_maximum_fusion.2.q_ref, ...), custom_call_target="tpu_custom_call" | custom-call | flops 5000000000 | bytes 14000000 | tf_op jit(solution)/shard_map/pallas_call | solution.py:212
  76.8 5.2 %collective-permute-done.9 = bf16[1584,128]{1,0:T(8,128)(2,1)S(1)} collective-permute-done((bf16[1584,128]{1,0:T(8,128)(2,1)S(1)}, bf16[1584,128]{1,0:T(8,128)(2,1)S(1)}, u32[]{:S(2)}, u32[]{:S(2)}) %collective-permute-start.9) | collective-permute-done | bytes 405536 | tf_op jit(solution)/shard_map/ppermute | solution.py:261
  82.4 1.9 %collective-permute-start.10 = (bf16[2,24,24,128]{3,2,1,0:T(8,128)(2,1)S(1)}, bf16[2,24,24,128]{3,2,1,0:T(8,128)(2,1)S(1)}, u32[]{:S(2)}, u32[]{:S(2)}) collective-permute-start(bf16[2,24,24,128]{3,2,1,0:T(8,128)(2,1)S(1)} %get-tuple-element.34), channel_id=1, source_target_pairs={{0,1},{2,3},{4,5},{6,7},{8,9},{10,11},{12,13},{14,15},{16,17},{18,... | collective-permute-start | bytes 884744 | tf_op jit(solution)/shard_map/ppermute | solution.py:267
  84.4 9.8 %collective-permute-start.11 = (bf16[2,24,24,128]{3,2,1,0:T(8,128)(2,1)S(1)}, bf16[2,24,24,128]{3,2,1,0:T(8,128)(2,1)S(1)}, u32[]{:S(2)}, u32[]{:S(2)}) collective-permute-start(bf16[2,24,24,128]{3,2,1,0:T(8,128)(2,1)S(1)} %get-tuple-element.35), channel_id=1, source_target_pairs={{1,2},{3,4},{5,6},{7,8},{9,10},{11,12},{13,14},{15,16},{17,18},{19... | collective-permute-start | bytes 884744 | tf_op jit(solution)/shard_map/ppermute | solution.py:267
  94.2 3.0 %collective-permute-done.10 = bf16[2,24,24,128]{3,2,1,0:T(8,128)(2,1)S(1)} collective-permute-done((bf16[2,24,24,128]{3,2,1,0:T(8,128)(2,1)S(1)}, bf16[2,24,24,128]{3,2,1,0:T(8,128)(2,1)S(1)}, u32[]{:S(2)}, u32[]{:S(2)}) %collective-permute-start.10) | collective-permute-done | bytes 294944 | tf_op jit(solution)/shard_map/ppermute | solution.py:267
  97.2 3.7 %collective-permute-done.11 = bf16[2,24,24,128]{3,2,1,0:T(8,128)(2,1)S(1)} collective-permute-done((bf16[2,24,24,128]{3,2,1,0:T(8,128)(2,1)S(1)}, bf16[2,24,24,128]{3,2,1,0:T(8,128)(2,1)S(1)}, u32[]{:S(2)}, u32[]{:S(2)}) %collective-permute-start.11) | collective-permute-done | bytes 294944 | tf_op jit(solution)/shard_map/ppermute | solution.py:267
  (51 shorter events, 2.9 us)
Async XLA Ops:
  1.6 21.3 %collective-permute-start.1 = (bf16[2,24,24,128]{3,2,1,0:T(8,128)(2,1)S(1)}, bf16[2,24,24,128]{3,2,1,0:T(8,128)(2,1)S(1)}, u32[]{:S(2)}, u32[]{:S(2)}) collective-permute-start(bf16[2,24,24,128]{3,2,1,0:T(8,128)(2,1)S(1)} %pad_maximum_fusion.5), channel_id=1, source_target_pairs={{0,1},{2,3},{4,5},{6,7},{8,9},{10,11},{12,13},{14,15},{16,17},{18,... | collective-permute-start | bytes 884744 | tf_op jit(solution)/shard_map/ppermute | solution.py:267
  5.7 19.0 %collective-permute-start = (bf16[2,24,24,128]{3,2,1,0:T(8,128)(2,1)S(1)}, bf16[2,24,24,128]{3,2,1,0:T(8,128)(2,1)S(1)}, u32[]{:S(2)}, u32[]{:S(2)}) collective-permute-start(bf16[2,24,24,128]{3,2,1,0:T(8,128)(2,1)S(1)} %pad_maximum_fusion.5), channel_id=1, source_target_pairs={{1,2},{3,4},{5,6},{7,8},{9,10},{11,12},{13,14},{15,16},{17,18},{19... | collective-permute-start | bytes 884744 | tf_op jit(solution)/shard_map/ppermute | solution.py:267
  18.5 6.2 %copy-start = (bf16[24,24,128]{2,1,0:T(8,128)(2,1)S(1)}, bf16[24,24,128]{2,1,0:T(8,128)(2,1)}, u32[]{:S(2)}) copy-start(bf16[24,24,128]{2,1,0:T(8,128)(2,1)} %param.6) | copy-start | bytes 442372
  18.5 6.2 %copy-start.1 = (bf16[24,24,128]{2,1,0:T(8,128)(2,1)S(1)}, bf16[24,24,128]{2,1,0:T(8,128)(2,1)}, u32[]{:S(2)}) copy-start(bf16[24,24,128]{2,1,0:T(8,128)(2,1)} %param.5) | copy-start | bytes 442372
  24.7 5.9 %copy-start.2 = (bf16[24,24,128]{2,1,0:T(8,128)(2,1)S(1)}, bf16[24,24,128]{2,1,0:T(8,128)(2,1)}, u32[]{:S(2)}) copy-start(bf16[24,24,128]{2,1,0:T(8,128)(2,1)} %param.7) | copy-start | bytes 442372
  24.9 11.5 %collective-permute-start.4 = (bf16[22,72,128]{2,1,0:T(8,128)(2,1)S(1)}, bf16[22,72,128]{2,1,0:T(8,128)(2,1)S(1)}, u32[]{:S(2)}, u32[]{:S(2)}) collective-permute-start(bf16[22,72,128]{2,1,0:T(8,128)(2,1)S(1)} %get-tuple-element.40), channel_id=1, source_target_pairs={{0,32},{32,64},{64,96},{96,128},{128,160},{160,192},{192,224},{224... | collective-permute-start | bytes 1216520 | tf_op jit(solution)/shard_map/ppermute | solution.py:261
  26.9 12.6 %collective-permute-start.5 = (bf16[22,72,128]{2,1,0:T(8,128)(2,1)S(1)}, bf16[22,72,128]{2,1,0:T(8,128)(2,1)S(1)}, u32[]{:S(2)}, u32[]{:S(2)}) collective-permute-start(bf16[22,72,128]{2,1,0:T(8,128)(2,1)S(1)} %get-tuple-element.41), channel_id=1, source_target_pairs={{32,0},{64,32},{96,64},{128,96},{160,128},{192,160},{224,192},{256... | collective-permute-start | bytes 1216520 | tf_op jit(solution)/shard_map/ppermute | solution.py:261
  30.8 18.6 %collective-permute-start.2 = (bf16[22,72,128]{2,1,0:T(8,128)(2,1)S(1)}, bf16[22,72,128]{2,1,0:T(8,128)(2,1)S(1)}, u32[]{:S(2)}, u32[]{:S(2)}) collective-permute-start(bf16[22,72,128]{2,1,0:T(8,128)(2,1)S(1)} %get-tuple-element.42), channel_id=1, source_target_pairs={{0,32},{32,64},{64,96},{96,128},{128,160},{160,192},{192,224},{224... | collective-permute-start | bytes 1216520 | tf_op jit(solution)/shard_map/ppermute | solution.py:261
  32.8 16.7 %collective-permute-start.3 = (bf16[22,72,128]{2,1,0:T(8,128)(2,1)S(1)}, bf16[22,72,128]{2,1,0:T(8,128)(2,1)S(1)}, u32[]{:S(2)}, u32[]{:S(2)}) collective-permute-start(bf16[22,72,128]{2,1,0:T(8,128)(2,1)S(1)} %get-tuple-element.43), channel_id=1, source_target_pairs={{32,0},{64,32},{96,64},{128,96},{160,128},{192,160},{224,192},{256... | collective-permute-start | bytes 1216520 | tf_op jit(solution)/shard_map/ppermute | solution.py:261
  57.0 19.7 %collective-permute-start.6 = (bf16[1584,128]{1,0:T(8,128)(2,1)S(1)}, bf16[1584,128]{1,0:T(8,128)(2,1)S(1)}, u32[]{:S(2)}, u32[]{:S(2)}) collective-permute-start(bf16[1584,128]{1,0:T(8,128)(2,1)S(1)} %get-tuple-element.26), channel_id=1, source_target_pairs={{32,0},{64,32},{96,64},{128,96},{160,128},{192,160},{224,192},{256... | collective-permute-start | bytes 1216520 | tf_op jit(solution)/shard_map/ppermute | solution.py:261
  61.1 15.6 %collective-permute-start.7 = (bf16[1584,128]{1,0:T(8,128)(2,1)S(1)}, bf16[1584,128]{1,0:T(8,128)(2,1)S(1)}, u32[]{:S(2)}, u32[]{:S(2)}) collective-permute-start(bf16[1584,128]{1,0:T(8,128)(2,1)S(1)} %get-tuple-element.27), channel_id=1, source_target_pairs={{0,32},{32,64},{64,96},{96,128},{128,160},{160,192},{192,224},{224... | collective-permute-start | bytes 1216520 | tf_op jit(solution)/shard_map/ppermute | solution.py:261
  63.5 13.3 %collective-permute-start.8 = (bf16[1584,128]{1,0:T(8,128)(2,1)S(1)}, bf16[1584,128]{1,0:T(8,128)(2,1)S(1)}, u32[]{:S(2)}, u32[]{:S(2)}) collective-permute-start(bf16[1584,128]{1,0:T(8,128)(2,1)S(1)} %get-tuple-element.28), channel_id=1, source_target_pairs={{32,0},{64,32},{96,64},{128,96},{160,128},{192,160},{224,192},{256... | collective-permute-start | bytes 1216520 | tf_op jit(solution)/shard_map/ppermute | solution.py:261
  66.7 15.3 %collective-permute-start.9 = (bf16[1584,128]{1,0:T(8,128)(2,1)S(1)}, bf16[1584,128]{1,0:T(8,128)(2,1)S(1)}, u32[]{:S(2)}, u32[]{:S(2)}) collective-permute-start(bf16[1584,128]{1,0:T(8,128)(2,1)S(1)} %get-tuple-element.29), channel_id=1, source_target_pairs={{0,32},{32,64},{64,96},{96,128},{128,160},{160,192},{192,224},{224... | collective-permute-start | bytes 1216520 | tf_op jit(solution)/shard_map/ppermute | solution.py:261
  82.4 14.7 %collective-permute-start.10 = (bf16[2,24,24,128]{3,2,1,0:T(8,128)(2,1)S(1)}, bf16[2,24,24,128]{3,2,1,0:T(8,128)(2,1)S(1)}, u32[]{:S(2)}, u32[]{:S(2)}) collective-permute-start(bf16[2,24,24,128]{3,2,1,0:T(8,128)(2,1)S(1)} %get-tuple-element.34), channel_id=1, source_target_pairs={{0,1},{2,3},{4,5},{6,7},{8,9},{10,11},{12,13},{14,15},{16,17},{18,... | collective-permute-start | bytes 884744 | tf_op jit(solution)/shard_map/ppermute | solution.py:267
  84.4 16.5 %collective-permute-start.11 = (bf16[2,24,24,128]{3,2,1,0:T(8,128)(2,1)S(1)}, bf16[2,24,24,128]{3,2,1,0:T(8,128)(2,1)S(1)}, u32[]{:S(2)}, u32[]{:S(2)}) collective-permute-start(bf16[2,24,24,128]{3,2,1,0:T(8,128)(2,1)S(1)} %get-tuple-element.35), channel_id=1, source_target_pairs={{1,2},{3,4},{5,6},{7,8},{9,10},{11,12},{13,14},{15,16},{17,18},{19... | collective-permute-start | bytes 884744 | tf_op jit(solution)/shard_map/ppermute | solution.py:267
